TPU v7x, 32 devices: a whole 2x2x4 slice. The times are simulated.
32 devices in a mesh: cfg: 2 (over x), space: 16 (over z, y, core).
Axes of the slice: x: 2, y: 2, z: 4, core: 2. Of those that a mesh axis runs over, the one named last changes fastest.
Arguments:
- vectors: float32 [4, 2, 3, 2048, 256], P('cfg', None, None, 'space'), parts along dimension 0, may hold values from -1.75 to 1.75
- links: float32 [4, 3, 2, 3, 3, 2048], P('cfg', None, None, None, None, 'space'), parts along dimension 0, may hold values from -2.5 to 2.5
- directions: int32 [3], replicated, may hold values from 0 to 2
- slice_group: int32 [2], replicated, may hold values from 0 to 1, as said below
- peram: float32 [4, 1024, 1024], P('cfg', None, 'space'), parts along dimension 0, may hold values from -0.3125 to 0.3125
- block_group: int32 [16], P('space'), may hold values from 0 to 1
Outputs:
- elementals: float32 [4, 3, 2, 256, 256], P('cfg', None, None, 'space'), parts along dimension 0
- blocks: float32 [4, 1024, 64], P('cfg', 'space'), parts along dimension 0
There are 2 independent parts, one for each index of `cfg`. A program takes and returns all parts, laid end to end along the dimension named above; an argument that names none is the same for every part. Nothing has to cross between parts.
Inputs may be any that keep to these rules, and one draw needn't show every extreme that they name: `slice_group`: every group holds at least one timeslice.
All inputs are finite; a program needn't handle non-finite values.
Results may differ from a plain program's by a relative error of at most 0.0001.
Values sent between devices are 32-bit elements; how exact they have to be, the bound alone decides.
No kernel may reach another device: no remote copies, remote signals or barrier semaphores. Data moves between devices by JAX's collectives and lax.ppermute only.
A program may use at most 64 MiB of HBM per device.

v0:
```python
import functools

import jax
import jax.numpy as jnp
import numpy as np
from jax import lax
from jax.experimental import pallas as pl
from jax.experimental.pallas import tpu as pltpu
from jax.sharding import PartitionSpec as P

LZ = 16
VMEM = pl.BlockSpec(memory_space=pltpu.VMEM)
SMEM = pl.BlockSpec(memory_space=pltpu.SMEM)
NT_DIMS = (((1,), (1,)), ((), ()))
NN_DIMS = (((1,), (0,)), ((), ()))


def split(value):
    high = value.astype(jnp.bfloat16)
    low = (value - high.astype(jnp.float32)).astype(jnp.bfloat16)
    return high, low


def dot3(left, right, dims):
    dot = functools.partial(
        lax.dot_general, dimension_numbers=dims, preferred_element_type=jnp.float32
    )
    return dot(left[0], right[0]) + dot(left[0], right[1]) + dot(left[1], right[0])


def store_left(v_ref, left_ref):
    sites, width = v_ref.shape[2], v_ref.shape[3]
    for part in range(2):
        for colour in range(3):
            high, low = split(v_ref[part, colour].T)
            at = (part * 3 + colour) * sites
            other = ((1 - part) * 3 + colour) * sites
            for level, value in enumerate((high, low)):
                left_ref[level, :width, at : at + sites] = value
                left_ref[level, width:, other : other + sites] = value if part else -value


def add(total, term):
    return term if total is None else total + term


def store_right(right_ref, row, sites, sources):
    width = right_ref.shape[2]
    coefs = []
    for coef, base, _ in sources:
        wide = [jnp.broadcast_to(coef[:, base + j : base + j + 1], (LZ, 128)) for j in range(18)]
        coefs.append(wide)
    for lanes in range(0, width, 128):
        cut = slice(lanes, lanes + 128)
        fields = []
        for _, _, field in sources:
            real, imag = field(cut)
            fields.append(([r + i for r, i in zip(real, imag)], [r - i for r, i in zip(real, imag)]))
        for a in range(3):
            alpha = beta = None
            for wide, (plus, minus) in zip(coefs, fields):
                for b in range(3):
                    real, imag = wide[a * 6 + b * 2], wide[a * 6 + b * 2 + 1]
                    alpha = add(add(alpha, real * plus[b]), imag * minus[b])
                    beta = add(add(beta, imag * plus[b]), -(real * minus[b]))
            for part, value in enumerate((alpha, beta)):
                high, low = split(value)
                at = (part * 3 + a) * sites + row * LZ
                right_ref[0, at : at + LZ, cut] = high
                right_ref[1, at : at + LZ, cut] = low


def row_of(v_ref, row, turn=False):
    def load(cut):
        at = slice(row * LZ, (row + 1) * LZ)
        parts = [[v_ref[p, c, at, cut] for c in range(3)] for p in range(2)]
        if turn:
            parts = [[pltpu.roll(x, LZ - 1, 0) for x in part] for part in parts]
        return parts

    return load


def adjoint_rows(rows):
    out = []
    for a in range(3):
        for b in range(3):
            at = b * 6 + a * 2
            out += [-rows[at : at + 1], rows[at + 1 : at + 2]]
    return jnp.concatenate(out, axis=0)


def of_time(ref, odd):
    count = ref.shape[0] // 2
    return 0.5 * jnp.where(odd == 0, ref[:count], ref[count:])


def contract(left_ref, right_ref):
    left = (left_ref[0], left_ref[1])
    right = (right_ref[0], right_ref[1])
    both = dot3(left, right, NN_DIMS)
    width = right_ref.shape[2]
    return both[:width] - both[width:].T


def plane_yz(v_ref, halo_ref, coef, left_ref, right_ref):
    sites = v_ref.shape[2]
    rows = sites // LZ
    for row in range(rows):
        here = coef[row * LZ : (row + 1) * LZ]
        ahead = row_of(v_ref, row + 1) if row + 1 < rows else row_of(halo_ref, 0)
        store_right(right_ref.at[0], row, sites, [(here, 18, ahead)])
        store_right(right_ref.at[1], row, sites, [(here, 36, row_of(v_ref, row, turn=True))])
    return [contract(left_ref, right_ref.at[i]) for i in range(2)]


def own_kernel(place_ref, v_ref, halo_ref, link_ref, out_ref, left_ref, right_ref, coef_ref):
    odd = (place_ref[0] // 2) % 2
    coef_ref[:54, :] = of_time(link_ref, odd)
    store_left(v_ref, left_ref)
    coef = coef_ref[...].T
    for i, value in enumerate(plane_yz(v_ref, halo_ref, coef, left_ref, right_ref)):
        out_ref[i] = value


def main_kernel(place_ref, va_ref, vb_ref, vc_ref, halo_ref, link_a, link_b, link_c, own_ref,
                keep_ref, send_ref, left_ref, right_ref, coef_ref, total_ref):
    sites, width = vb_ref.shape[2], vb_ref.shape[3]
    odd = (place_ref[0] // 2) % 2
    coef_ref[:54, :] = of_time(link_b, odd)
    there = coef_ref[:18, :]
    before = adjoint_rows(of_time(link_a, odd)[:18])
    after = adjoint_rows(of_time(link_c, odd)[:18])
    coef_ref[56:74, :] = jnp.where(odd == 0, before, there)
    coef_ref[80:98, :] = jnp.where(odd == 0, there, after)
    coef = coef_ref[...].T
    store_left(vb_ref, left_ref)
    for i, value in enumerate(plane_yz(vb_ref, halo_ref, coef, left_ref, right_ref)):
        total_ref[(i + 1) * width : (i + 2) * width, :] = value + own_ref[i]
    for row in range(sites // LZ):
        here = coef[row * LZ : (row + 1) * LZ]
        sources = [(here, 56, row_of(va_ref, row)), (here, 80, row_of(vc_ref, row))]
        store_right(right_ref.at[2], row, sites, sources)
    total_ref[:width, :] = contract(left_ref, right_ref.at[2])
    core = place_ref[0] % 2
    half = 3 * width // 2
    keep_ref[...] = total_ref[pl.ds(pl.multiple_of(core * half, 8), half), :]
    send_ref[...] = total_ref[pl.ds(pl.multiple_of((1 - core) * half, 8), half), :]


def spread_kernel(place_ref, keep_ref, got_ref, *refs):
    outs, total_ref = refs[:-1], refs[-1]
    total_ref[...] = keep_ref[...] + got_ref[...]
    count = len(outs)
    size = outs[0].shape[0]
    pair = place_ref[0] // 4
    for d in range(count):
        at = lax.rem(pair + d, count) * size
        outs[d][...] = total_ref[pl.ds(pl.multiple_of(at, 8), size), :]


def sum_kernel(*refs):
    total = refs[0][...]
    for ref in refs[1:-1]:
        total = total + ref[...]
    refs[-1][...] = total


def table_kernel(p_ref, b_high, b_low, q_high, q_low):
    width = p_ref.shape[2] // 4
    cols = p_ref.shape[1]

    def spin(part, a):
        return p_ref[part, :, a * width : (a + 1) * width]

    m = [0.5 * (spin(0, a) - spin(1, a)) for a in (2, 3)]
    s = [0.5 * (spin(0, a) + spin(1, a)) for a in (2, 3)]
    pieces = {"m0": split(m[0]), "m1": split(m[1]), "s0": split(s[0]), "s1": split(s[1])}
    table = (
        ("+m1", "+s1", "+m0", "+s0"),
        ("+s1", "-m1", "-s0", "+m0"),
        ("+m0", "+s0", "-m1", "-s1"),
        ("-s1", "+m1", "-s0", "+m0"),
        ("+m1", "+s1", "-m0", "-s0"),
        ("-s0", "+m0", "+s1", "-m1"),
    )
    for k, names in enumerate(table):
        for j, name in enumerate(names):
            high, low = pieces[name[1:]]
            if name[0] == "-":
                high, low = -high, -low
            where = (slice(j * cols, (j + 1) * cols), slice(k * width, (k + 1) * width))
            b_high[where] = high
            b_low[where] = low
    for a in range(2):
        for part in range(2):
            high, low = split(spin(part, a))
            at = (a * 2 + part) * width
            q_high[:, at : at + width] = high
            q_low[:, at : at + width] = low


def take(ref, at, rows):
    if rows % 8 == 0:
        return ref[pl.ds(pl.multiple_of(at, 8), rows), :]
    inner = lax.rem(at, 8)
    tile = ref[pl.ds(pl.multiple_of(at - inner, 8), 8), :]
    return pltpu.roll(tile, lax.rem(8 - inner, 8), 0)[:rows]


def final_kernel(place_ref, direct_ref, slice_ref, block_ref, b_high, b_low, q_high, q_low,
                 *refs):
    count = (len(refs) - 4) // 4
    pieces = refs[: 4 * count]
    elem_ref, out_ref, all_ref, turn_ref = refs[4 * count :]
    size, width = pieces[0].shape
    place = place_ref[0]
    core = place % 2
    odd = (place // 2) % 2
    pair = place // 4
    half = 3 * width // 2
    for side in range(2):
        for other in range(2):
            for d in range(count):
                time = (odd + other) % 2
                base = (time * 2 + (core + side) % 2) * half
                at = base + lax.rem(pair - d + count, count) * size
                piece = pieces[(side * 2 + other) * count + d]
                all_ref[pl.ds(pl.multiple_of(at, 8), size), :] = piece[...]
    rows = elem_ref.shape[3]
    first = place * rows
    lane = pl.multiple_of((first // 128) * 128, 128)
    for i in range(6):
        block = all_ref[i * width : (i + 1) * width, pl.ds(lane, 128)]
        turn_ref[i * 128 : (i + 1) * 128, :] = block.T
    inner = lax.rem(first, 128)
    for g in range(2):
        time = jnp.where(slice_ref[0] == g, 0, 1)
        for k in range(3):
            which = time * 3 + direct_ref[k]
            row = take(all_ref, which * width + first, rows)
            col = take(turn_ref, which * 128 + inner, rows)
            elem_ref[g, k, 0] = 0.5 * (row - col)
            elem_ref[g, k, 1] = 0.5 * (row + col)
    time = jnp.where(slice_ref[0] == block_ref[0], 0, 1)
    turned = None
    for k in range(3):
        at = pl.multiple_of((time * 3 + direct_ref[k]) * width, 8)
        parts = split(all_ref[pl.ds(at, width), :])
        one = slice(k * width, (k + 1) * width)
        two = slice((3 + k) * width, (4 + k) * width)
        term = dot3((b_high[:, one], b_low[:, one]), parts, NT_DIMS) + dot3(
            (b_high[:, two], b_low[:, two]), parts, NN_DIMS
        )
        turned = term if turned is None else turned + term
    cols = q_high.shape[0]
    y = [turned[j * cols : (j + 1) * cols] for j in range(4)]
    same = split(jnp.concatenate([y[0], y[1], y[2], y[3]], axis=1))
    cross = split(jnp.concatenate([y[1], -y[0], y[3], -y[2]], axis=1))
    q = (q_high[...], q_low[...])
    out_ref[0] = dot3(q, cross, NT_DIMS) - dot3(cross, q, NT_DIMS)
    out_ref[1] = -(dot3(q, same, NT_DIMS) + dot3(same, q, NT_DIMS))


def shape(*dims, dtype=jnp.float32):
    return jax.ShapeDtypeStruct(dims, dtype)


def size_of(x):
    return x.size * jnp.dtype(x.dtype).itemsize


def call(kernel, out, operands, scalars=0, scratch=(), flops=0):
    outs = jax.tree.leaves(out)
    moved = sum(size_of(x) for x in list(operands) + outs)
    held = sum(int(np.prod(x.shape)) * jnp.dtype(x.dtype).itemsize for x in scratch)
    limit = moved + held + (4 << 20)
    return pl.pallas_call(
        kernel,
        out_shape=out,
        in_specs=[SMEM] * scalars + [VMEM] * (len(operands) - scalars),
        out_specs=jax.tree.map(lambda _: VMEM, out),
        scratch_shapes=list(scratch),
        cost_estimate=pl.CostEstimate(flops=flops, bytes_accessed=moved, transcendentals=0),
        compiler_params=pltpu.CompilerParams(vmem_limit_bytes=limit),
    )(*operands)


def program(vectors, links, directions, slice_group, peram, block_group):
    total = lax.axis_size("space")
    place = lax.axis_index("space")
    places = jnp.full((1,), place, jnp.int32)
    sites, width = vectors.shape[3], vectors.shape[4]
    pairs = total // 4
    odd = (place // 2) % 2

    def send(value, where):
        route = []
        for i in range(total):
            pair, o, core = where(i // 4, (i // 2) % 2, i % 2)
            route.append((i, ((pair % pairs) * 2 + o) * 2 + core))
        return lax.ppermute(value, "space", route)

    partner = lambda pair, o, core: (pair, 1 - o, core)
    across = lambda pair, o, core: (pair, 1 - o, 1 - core)
    twin = lambda pair, o, core: (pair, o, 1 - core)
    along = lambda pair, o, core: (pair + (1 if o else -1), o, core)

    def shift(d):
        return lambda pair, o, core: (pair + d, o, core)

    flat = links.transpose(0, 1, 3, 4, 2, 5).reshape(links.shape[0] * 54, sites)
    link_b = send(flat, partner)
    link_c = send(flat, along)
    theirs = lax.dynamic_index_in_dim(vectors, 1 - odd, 0, keepdims=False)
    mine = lax.dynamic_index_in_dim(vectors, odd, 0, keepdims=False)
    vec_b = send(theirs, partner)
    vec_c = send(mine, along)
    halo_a = send(mine[:, :, :LZ], twin)
    halo_b = send(theirs[:, :, :LZ], across)

    left = pltpu.VMEM((2, 2 * width, 6 * sites), jnp.bfloat16)
    right = lambda n: pltpu.VMEM((n, 2, 6 * sites, width), jnp.bfloat16)
    coef = pltpu.VMEM((128, sites), jnp.float32)
    work = 6 * 6 * sites * 2 * width * width
    own = call(own_kernel, shape(2, width, width), (places, mine, halo_a, flat), scalars=1,
               scratch=(left, right(2), coef), flops=2 * work)
    cols = peram.shape[2]
    turned = jnp.swapaxes(peram, 1, 2)
    bf16 = jnp.bfloat16
    tables = call(
        table_kernel,
        (shape(4 * cols, 6 * width, dtype=bf16),) * 2
        + (shape(cols, 4 * width, dtype=bf16),) * 2,
        (turned,))
    half = 3 * width // 2
    keep, give = call(
        main_kernel, (shape(half, width),) * 2,
        (places, mine, vec_b, vec_c, halo_b, flat, link_b, link_c, own), scalars=1,
        scratch=(left, right(3), coef, pltpu.VMEM((3 * width, width), jnp.float32)),
        flops=3 * work)
    got = send(give, twin)
    size = half // pairs
    spread = call(spread_kernel, (shape(size, width),) * pairs, (places, keep, got), scalars=1,
                  scratch=(pltpu.VMEM((half, width), jnp.float32),))
    parts = [spread[0]] + [send(spread[d], shift(d)) for d in range(1, pairs)]
    shard = call(sum_kernel, shape(size, width), parts)
    here = [shard] + [send(shard, shift(d)) for d in range(1, pairs)]
    there = [send(x, partner) for x in here]
    pieces = here + there
    pieces = pieces + [send(x, twin) for x in pieces]

    return call(
        final_kernel,
        (shape(2, 3, 2, width // total, width), shape(2, cols, cols)),
        (places, directions, slice_group, block_group, *tables, *pieces), scalars=4,
        scratch=(pltpu.VMEM((6 * width, width), jnp.float32),
                 pltpu.VMEM((6 * 128, width), jnp.float32)),
        flops=36 * cols * width * width)


def solution(mesh):
    return jax.shard_map(
        program,
        mesh=mesh,
        in_specs=(
            P("cfg", None, None, "space", None),
            P("cfg", None, None, None, None, "space"),
            P(),
            P(),
            P("cfg", None, "space"),
            P("space"),
        ),
        out_specs=(P("cfg", None, None, "space", None), P("cfg", "space", None)),
        check_vma=False,
    )
```

profile of v0, /device:TPU:0, one launch (start us, length us, event | category | flops | bytes accessed | tf_op | source)
XLA Modules:
  0.0 67.5 jit_solution(18251834947503652648)
XLA Ops:
  0.7 1.6 %dynamic-slice_bitcast_fusion = (f32[2,3,128,256]{3,2,1,0:T(8,128)S(1)}, f32[2,3,128,256]{3,2,1,0:T(8,128)S(1)}) fusion(f32[2,2,3,128,256]{4,3,2,1,0:T(8,128)} %param.6, s32[]{:T(128)S(6)} %select_n.21, s32[]{:T(128)S(6)} %select_n.20), kind=kLoop, calls=%fused_computation | loop fusion | bytes 3145736 | tf_op jit(solution)/shard_map/jit(dynamic_index_in_dim)/squeeze | solution.py:315
  2.2 3.1 %collective-permute-start = (f32[2,3,128,256]{3,2,1,0:T(8,128)S(1)}, f32[2,3,128,256]{3,2,1,0:T(8,128)S(1)}, u32[]{:S(2)}, u32[]{:S(2)}) collective-permute-start(f32[2,3,128,256]{3,2,1,0:T(8,128)S(1)} %get-tuple-element.22), channel_id=1, source_target_pairs={{0,2},{1,3},{2,0},{3,1},{4,6},{5,7},{6,4},{7,5},{8,10},{9,11},{10,... | collective-permute-start | bytes 2359304 | tf_op jit(solution)/shard_map/ppermute | solution.py:302
  5.3 3.6 %collective-permute-start.1 = (f32[2,3,128,256]{3,2,1,0:T(8,128)S(1)}, f32[2,3,128,256]{3,2,1,0:T(8,128)S(1)}, u32[]{:S(2)}, u32[]{:S(2)}) collective-permute-start(f32[2,3,128,256]{3,2,1,0:T(8,128)S(1)} %get-tuple-element.23.v_ref.va_ref), channel_id=1, source_target_pairs={{0,12},{1,13},{2,6},{3,7},{4,0},{5,1},{6,10},{7,11},{8,4},{9,5},{1... | collective-permute-start | bytes 2359304 | tf_op jit(solution)/shard_map/ppermute | solution.py:302
  9.6 0.6 collective-permute-done.5.halo_ref
  10.3 0.8 %collective-permute-start.2 = (f32[2,3,16,256]{3,2,1,0:T(8,128)S(1)}, f32[2,3,16,256]{3,2,1,0:T(8,128)S(1)}, u32[]{:S(2)}, u32[]{:S(2)}) collective-permute-start(f32[2,3,16,256]{3,2,1,0:T(8,128)S(1)} %slice.8), channel_id=1, source_target_pairs={{0,3},{1,2},{2,1},{3,0},{4,7},{5,6},{6,5},{7,4},{8,11},{9,10},{10,... | collective-permute-start | bytes 294920 | tf_op jit(solution)/shard_map/ppermute | solution.py:302
  11.0 3.1 %shard_map.78.own_ref = f32[2,256,256]{2,1,0:T(8,128)S(1)} custom-call(s32[1]{0:T(128)} %bitcast.place_ref, f32[2,3,128,256]{3,2,1,0:T(8,128)S(1)} %get-tuple-element.23.v_ref.va_ref, f32[2,3,16,256]{3,2,1,0:T(8,128)S(1)} %collective-permute-done.5.halo_ref, f32[108,128]{1,0:T(8,128)S(1)} %reshape.7.link_ref.link_a), custom_call_target="tpu_custom_call" | custom-call | flops 1207959552 | bytes 1464324 | tf_op jit(solution)/shard_map/pallas_call | solution.py:278
  14.2 10.8 %collective-permute-done.3.link_b = f32[108,128]{1,0:T(8,128)S(1)} collective-permute-done((f32[108,128]{1,0:T(8,128)S(1)}, f32[108,128]{1,0:T(8,128)S(1)}, u32[]{:S(2)}, u32[]{:S(2)}) %collective-permute-start.3) | collective-permute-done | bytes 55328 | tf_op jit(solution)/shard_map/ppermute | solution.py:302
  24.9 1.7 %collective-permute-done.4.link_c = f32[108,128]{1,0:T(8,128)S(1)} collective-permute-done((f32[108,128]{1,0:T(8,128)S(1)}, f32[108,128]{1,0:T(8,128)S(1)}, u32[]{:S(2)}, u32[]{:S(2)}) %collective-permute-start.4) | collective-permute-done | bytes 55328 | tf_op jit(solution)/shard_map/ppermute | solution.py:302
  26.7 4.4 %shard_map.79 = (f32[384,256]{1,0:T(8,128)S(1)}, f32[384,256]{1,0:T(8,128)S(1)}) custom-call(s32[1]{0:T(128)} %bitcast.place_ref, f32[2,3,128,256]{3,2,1,0:T(8,128)S(1)} %get-tuple-element.23.v_ref.va_ref, f32[2,3,128,256]{3,2,1,0:T(8,128)S(1)} %collective-permute-done.vb_ref, f32[2,3,128,256]{3,2,1,0:T(8,128)S(1)} %collective-permute-done.1.vc_ref, ...), custom_call_target="tpu_custom_call" | custom-call | flops 1811939328 | bytes 3934212 | tf_op jit(solution)/shard_map/pallas_call | solution.py:278
  31.2 1.7 %collective-permute-done.6.got_ref = f32[384,256]{1,0:T(8,128)S(1)} collective-permute-done((f32[384,256]{1,0:T(8,128)S(1)}, f32[384,256]{1,0:T(8,128)S(1)}, u32[]{:S(2)}, u32[]{:S(2)}) %collective-permute-start.6) | collective-permute-done | bytes 393248 | tf_op jit(solution)/shard_map/ppermute | solution.py:302
  33.0 0.8 %collective-permute-start.7 = (f32[96,256]{1,0:T(8,128)S(1)}, f32[96,256]{1,0:T(8,128)S(1)}, u32[]{:S(2)}, u32[]{:S(2)}) collective-permute-start(f32[96,256]{1,0:T(8,128)S(1)} %get-tuple-element.19), channel_id=1, source_target_pairs={{0,4},{1,5},{2,6},{3,7},{4,8},{5,9},{6,10},{7,11},{8,12},{9,13},{1... | collective-permute-start | bytes 294920 | tf_op jit(solution)/shard_map/ppermute | solution.py:302
  33.8 4.1 %collective-permute-start.8 = (f32[96,256]{1,0:T(8,128)S(1)}, f32[96,256]{1,0:T(8,128)S(1)}, u32[]{:S(2)}, u32[]{:S(2)}) collective-permute-start(f32[96,256]{1,0:T(8,128)S(1)} %get-tuple-element.20), channel_id=1, source_target_pairs={{0,8},{1,9},{2,10},{3,11},{4,12},{5,13},{6,14},{7,15},{8,0},{9,1},... | collective-permute-start | bytes 294920 | tf_op jit(solution)/shard_map/ppermute | solution.py:302
  37.9 3.2 %collective-permute-done.7.refs_1_ = f32[96,256]{1,0:T(8,128)S(1)} collective-permute-done((f32[96,256]{1,0:T(8,128)S(1)}, f32[96,256]{1,0:T(8,128)S(1)}, u32[]{:S(2)}, u32[]{:S(2)}) %collective-permute-start.7) | collective-permute-done | bytes 98336 | tf_op jit(solution)/shard_map/ppermute | solution.py:302
  41.1 3.6 %collective-permute-done.8.refs_2_ = f32[96,256]{1,0:T(8,128)S(1)} collective-permute-done((f32[96,256]{1,0:T(8,128)S(1)}, f32[96,256]{1,0:T(8,128)S(1)}, u32[]{:S(2)}, u32[]{:S(2)}) %collective-permute-start.8) | collective-permute-done | bytes 98336 | tf_op jit(solution)/shard_map/ppermute | solution.py:302
  44.8 2.6 %collective-permute-start.10 = (f32[96,256]{1,0:T(8,128)S(1)}, f32[96,256]{1,0:T(8,128)S(1)}, u32[]{:S(2)}, u32[]{:S(2)}) collective-permute-start(f32[96,256]{1,0:T(8,128)S(1)} %shard_map.81.refs_0_), channel_id=1, source_target_pairs={{0,4},{1,5},{2,6},{3,7},{4,8},{5,9},{6,10},{7,11},{8,12},{9,13},{1... | collective-permute-start | bytes 294920 | tf_op jit(solution)/shard_map/ppermute | solution.py:302
  47.4 0.7 collective-permute-start.11
  48.1 1.8 %collective-permute-start.12 = (f32[96,256]{1,0:T(8,128)S(1)}, f32[96,256]{1,0:T(8,128)S(1)}, u32[]{:S(2)}, u32[]{:S(2)}) collective-permute-start(f32[96,256]{1,0:T(8,128)S(1)} %shard_map.81.refs_0_), channel_id=1, source_target_pairs={{0,12},{1,13},{2,14},{3,15},{4,0},{5,1},{6,2},{7,3},{8,4},{9,5},{1... | collective-permute-start | bytes 294920 | tf_op jit(solution)/shard_map/ppermute | solution.py:302
  49.8 0.5 collective-permute-start.13
  50.4 1.8 %collective-permute-done.10.refs_1_ = f32[96,256]{1,0:T(8,128)S(1)} collective-permute-done((f32[96,256]{1,0:T(8,128)S(1)}, f32[96,256]{1,0:T(8,128)S(1)}, u32[]{:S(2)}, u32[]{:S(2)}) %collective-permute-start.10) | collective-permute-done | bytes 98336 | tf_op jit(solution)/shard_map/ppermute | solution.py:302
  52.7 2.9 %collective-permute-done.11.refs_2_ = f32[96,256]{1,0:T(8,128)S(1)} collective-permute-done((f32[96,256]{1,0:T(8,128)S(1)}, f32[96,256]{1,0:T(8,128)S(1)}, u32[]{:S(2)}, u32[]{:S(2)}) %collective-permute-start.11) | collective-permute-done | bytes 98336 | tf_op jit(solution)/shard_map/ppermute | solution.py:302
  56.1 1.5 %collective-permute-start.16 = (f32[96,256]{1,0:T(8,128)S(1)}, f32[96,256]{1,0:T(8,128)S(1)}, u32[]{:S(2)}, u32[]{:S(2)}) collective-permute-start(f32[96,256]{1,0:T(8,128)S(1)} %collective-permute-done.12.refs_3_), channel_id=1, source_target_pairs={{0,2},{1,3},{2,0},{3,1},{4,6},{5,7},{6,4},{7,5},{8,10},{9,11},{10,... | collective-permute-start | bytes 294920 | tf_op jit(solution)/shard_map/ppermute | solution.py:302
  58.2 3.0 %collective-permute-done.15.refs_6_ = f32[96,256]{1,0:T(8,128)S(1)} collective-permute-done((f32[96,256]{1,0:T(8,128)S(1)}, f32[96,256]{1,0:T(8,128)S(1)}, u32[]{:S(2)}, u32[]{:S(2)}) %collective-permute-start.15) | collective-permute-done | bytes 98336 | tf_op jit(solution)/shard_map/ppermute | solution.py:302
  61.2 1.1 %collective-permute-done.16.refs_7_ = f32[96,256]{1,0:T(8,128)S(1)} collective-permute-done((f32[96,256]{1,0:T(8,128)S(1)}, f32[96,256]{1,0:T(8,128)S(1)}, u32[]{:S(2)}, u32[]{:S(2)}) %collective-permute-start.16) | collective-permute-done | bytes 98336 | tf_op jit(solution)/shard_map/ppermute | solution.py:302
  64.1 3.4 %shard_map.82 = (f32[2,3,2,16,256]{4,3,2,1,0:T(8,128)}, f32[2,64,64]{2,1,0:T(8,128)}) custom-call(s32[1]{0:T(128)} %bitcast.place_ref, s32[3]{0:T(128)S(1)} %copy-done.1, s32[2]{0:T(128)S(1)} %copy-done.2, s32[1]{0:T(128)S(6)} %copy.8.block_ref, bf16[256,1536]{1,0:T(8,128)(2,1)S(1)} %get-tuple-element.12.b_high, ...), custom_call_target="tpu_custom_call" | custom-call | flops 150994944 | bytes 3637276 | tf_op jit(solution)/shard_map/pallas_call | solution.py:278
  (44 shorter events, 3.7 us)
Async XLA Ops:
  2.2 24.4 %collective-permute-start = (f32[2,3,128,256]{3,2,1,0:T(8,128)S(1)}, f32[2,3,128,256]{3,2,1,0:T(8,128)S(1)}, u32[]{:S(2)}, u32[]{:S(2)}) collective-permute-start(f32[2,3,128,256]{3,2,1,0:T(8,128)S(1)} %get-tuple-element.22), channel_id=1, source_target_pairs={{0,2},{1,3},{2,0},{3,1},{4,6},{5,7},{6,4},{7,5},{8,10},{9,11},{10,... | collective-permute-start | bytes 2359304 | tf_op jit(solution)/shard_map/ppermute | solution.py:302
  5.3 21.4 %collective-permute-start.1 = (f32[2,3,128,256]{3,2,1,0:T(8,128)S(1)}, f32[2,3,128,256]{3,2,1,0:T(8,128)S(1)}, u32[]{:S(2)}, u32[]{:S(2)}) collective-permute-start(f32[2,3,128,256]{3,2,1,0:T(8,128)S(1)} %get-tuple-element.23.v_ref.va_ref), channel_id=1, source_target_pairs={{0,12},{1,13},{2,6},{3,7},{4,0},{5,1},{6,10},{7,11},{8,4},{9,5},{1... | collective-permute-start | bytes 2359304 | tf_op jit(solution)/shard_map/ppermute | solution.py:302
  8.9 1.4 %collective-permute-start.5 = (f32[2,3,16,256]{3,2,1,0:T(8,128)S(1)}, f32[2,3,16,256]{3,2,1,0:T(8,128)S(1)}, u32[]{:S(2)}, u32[]{:S(2)}) collective-permute-start(f32[2,3,16,256]{3,2,1,0:T(8,128)S(1)} %slice.9), channel_id=1, source_target_pairs={{0,1},{1,0},{2,3},{3,2},{4,5},{5,4},{6,7},{7,6},{8,9},{9,8},{10,11... | collective-permute-start | bytes 294920 | tf_op jit(solution)/shard_map/ppermute | solution.py:302
  9.0 15.9 %collective-permute-start.3 = (f32[108,128]{1,0:T(8,128)S(1)}, f32[108,128]{1,0:T(8,128)S(1)}, u32[]{:S(2)}, u32[]{:S(2)}) collective-permute-start(f32[108,128]{1,0:T(8,128)S(1)} %reshape.7.link_ref.link_a), channel_id=1, source_target_pairs={{0,2},{1,3},{2,0},{3,1},{4,6},{5,7},{6,4},{7,5},{8,10},{9,11},{10,... | collective-permute-start | bytes 165896 | tf_op jit(solution)/shard_map/ppermute | solution.py:302
  9.1 17.5 %collective-permute-start.4 = (f32[108,128]{1,0:T(8,128)S(1)}, f32[108,128]{1,0:T(8,128)S(1)}, u32[]{:S(2)}, u32[]{:S(2)}) collective-permute-start(f32[108,128]{1,0:T(8,128)S(1)} %reshape.7.link_ref.link_a), channel_id=1, source_target_pairs={{0,12},{1,13},{2,6},{3,7},{4,0},{5,1},{6,10},{7,11},{8,4},{9,5},{1... | collective-permute-start | bytes 165896 | tf_op jit(solution)/shard_map/ppermute | solution.py:302
  10.3 16.4 %collective-permute-start.2 = (f32[2,3,16,256]{3,2,1,0:T(8,128)S(1)}, f32[2,3,16,256]{3,2,1,0:T(8,128)S(1)}, u32[]{:S(2)}, u32[]{:S(2)}) collective-permute-start(f32[2,3,16,256]{3,2,1,0:T(8,128)S(1)} %slice.8), channel_id=1, source_target_pairs={{0,3},{1,2},{2,1},{3,0},{4,7},{5,6},{6,5},{7,4},{8,11},{9,10},{10,... | collective-permute-start | bytes 294920 | tf_op jit(solution)/shard_map/ppermute | solution.py:302
  31.1 1.8 %collective-permute-start.6 = (f32[384,256]{1,0:T(8,128)S(1)}, f32[384,256]{1,0:T(8,128)S(1)}, u32[]{:S(2)}, u32[]{:S(2)}) collective-permute-start(f32[384,256]{1,0:T(8,128)S(1)} %get-tuple-element.17), channel_id=1, source_target_pairs={{0,1},{1,0},{2,3},{3,2},{4,5},{5,4},{6,7},{7,6},{8,9},{9,8},{10,11... | collective-permute-start | bytes 1179656 | tf_op jit(solution)/shard_map/ppermute | solution.py:302
  33.0 8.1 %collective-permute-start.7 = (f32[96,256]{1,0:T(8,128)S(1)}, f32[96,256]{1,0:T(8,128)S(1)}, u32[]{:S(2)}, u32[]{:S(2)}) collective-permute-start(f32[96,256]{1,0:T(8,128)S(1)} %get-tuple-element.19), channel_id=1, source_target_pairs={{0,4},{1,5},{2,6},{3,7},{4,8},{5,9},{6,10},{7,11},{8,12},{9,13},{1... | collective-permute-start | bytes 294920 | tf_op jit(solution)/shard_map/ppermute | solution.py:302
  33.8 10.9 %collective-permute-start.8 = (f32[96,256]{1,0:T(8,128)S(1)}, f32[96,256]{1,0:T(8,128)S(1)}, u32[]{:S(2)}, u32[]{:S(2)}) collective-permute-start(f32[96,256]{1,0:T(8,128)S(1)} %get-tuple-element.20), channel_id=1, source_target_pairs={{0,8},{1,9},{2,10},{3,11},{4,12},{5,13},{6,14},{7,15},{8,0},{9,1},... | collective-permute-start | bytes 294920 | tf_op jit(solution)/shard_map/ppermute | solution.py:302
  37.9 6.8 %collective-permute-start.9 = (f32[96,256]{1,0:T(8,128)S(1)}, f32[96,256]{1,0:T(8,128)S(1)}, u32[]{:S(2)}, u32[]{:S(2)}) collective-permute-start(f32[96,256]{1,0:T(8,128)S(1)} %get-tuple-element.21), channel_id=1, source_target_pairs={{0,12},{1,13},{2,14},{3,15},{4,0},{5,1},{6,2},{7,3},{8,4},{9,5},{1... | collective-permute-start | bytes 294920 | tf_op jit(solution)/shard_map/ppermute | solution.py:302
  44.8 7.4 %collective-permute-start.10 = (f32[96,256]{1,0:T(8,128)S(1)}, f32[96,256]{1,0:T(8,128)S(1)}, u32[]{:S(2)}, u32[]{:S(2)}) collective-permute-start(f32[96,256]{1,0:T(8,128)S(1)} %shard_map.81.refs_0_), channel_id=1, source_target_pairs={{0,4},{1,5},{2,6},{3,7},{4,8},{5,9},{6,10},{7,11},{8,12},{9,13},{1... | collective-permute-start | bytes 294920 | tf_op jit(solution)/shard_map/ppermute | solution.py:302
  47.4 8.2 %collective-permute-start.11 = (f32[96,256]{1,0:T(8,128)S(1)}, f32[96,256]{1,0:T(8,128)S(1)}, u32[]{:S(2)}, u32[]{:S(2)}) collective-permute-start(f32[96,256]{1,0:T(8,128)S(1)} %shard_map.81.refs_0_), channel_id=1, source_target_pairs={{0,8},{1,9},{2,10},{3,11},{4,12},{5,13},{6,14},{7,15},{8,0},{9,1},... | collective-permute-start | bytes 294920 | tf_op jit(solution)/shard_map/ppermute | solution.py:302
  48.1 8.0 %collective-permute-start.12 = (f32[96,256]{1,0:T(8,128)S(1)}, f32[96,256]{1,0:T(8,128)S(1)}, u32[]{:S(2)}, u32[]{:S(2)}) collective-permute-start(f32[96,256]{1,0:T(8,128)S(1)} %shard_map.81.refs_0_), channel_id=1, source_target_pairs={{0,12},{1,13},{2,14},{3,15},{4,0},{5,1},{6,2},{7,3},{8,4},{9,5},{1... | collective-permute-start | bytes 294920 | tf_op jit(solution)/shard_map/ppermute | solution.py:302
  49.8 7.8 %collective-permute-start.13 = (f32[96,256]{1,0:T(8,128)S(1)}, f32[96,256]{1,0:T(8,128)S(1)}, u32[]{:S(2)}, u32[]{:S(2)}) collective-permute-start(f32[96,256]{1,0:T(8,128)S(1)} %shard_map.81.refs_0_), channel_id=1, source_target_pairs={{0,2},{1,3},{2,0},{3,1},{4,6},{5,7},{6,4},{7,5},{8,10},{9,11},{10,... | collective-permute-start | bytes 294920 | tf_op jit(solution)/shard_map/ppermute | solution.py:302
  50.4 7.3 %collective-permute-start.17 = (f32[96,256]{1,0:T(8,128)S(1)}, f32[96,256]{1,0:T(8,128)S(1)}, u32[]{:S(2)}, u32[]{:S(2)}) collective-permute-start(f32[96,256]{1,0:T(8,128)S(1)} %shard_map.81.refs_0_), channel_id=1, source_target_pairs={{0,1},{1,0},{2,3},{3,2},{4,5},{5,4},{6,7},{7,6},{8,9},{9,8},{10,11... | collective-permute-start | bytes 294920 | tf_op jit(solution)/shard_map/ppermute | solution.py:302
  52.2 5.9 %collective-permute-start.14 = (f32[96,256]{1,0:T(8,128)S(1)}, f32[96,256]{1,0:T(8,128)S(1)}, u32[]{:S(2)}, u32[]{:S(2)}) collective-permute-start(f32[96,256]{1,0:T(8,128)S(1)} %collective-permute-done.10.refs_1_), channel_id=1, source_target_pairs={{0,2},{1,3},{2,0},{3,1},{4,6},{5,7},{6,4},{7,5},{8,10},{9,11},{10,... | collective-permute-start | bytes 294920 | tf_op jit(solution)/shard_map/ppermute | solution.py:302
  55.6 5.7 %collective-permute-start.15 = (f32[96,256]{1,0:T(8,128)S(1)}, f32[96,256]{1,0:T(8,128)S(1)}, u32[]{:S(2)}, u32[]{:S(2)}) collective-permute-start(f32[96,256]{1,0:T(8,128)S(1)} %collective-permute-done.11.refs_2_), channel_id=1, source_target_pairs={{0,2},{1,3},{2,0},{3,1},{4,6},{5,7},{6,4},{7,5},{8,10},{9,11},{10,... | collective-permute-start | bytes 294920 | tf_op jit(solution)/shard_map/ppermute | solution.py:302
  56.1 6.2 %collective-permute-start.16 = (f32[96,256]{1,0:T(8,128)S(1)}, f32[96,256]{1,0:T(8,128)S(1)}, u32[]{:S(2)}, u32[]{:S(2)}) collective-permute-start(f32[96,256]{1,0:T(8,128)S(1)} %collective-permute-done.12.refs_3_), channel_id=1, source_target_pairs={{0,2},{1,3},{2,0},{3,1},{4,6},{5,7},{6,4},{7,5},{8,10},{9,11},{10,... | collective-permute-start | bytes 294920 | tf_op jit(solution)/shard_map/ppermute | solution.py:302
  57.6 4.7 %collective-permute-start.18 = (f32[96,256]{1,0:T(8,128)S(1)}, f32[96,256]{1,0:T(8,128)S(1)}, u32[]{:S(2)}, u32[]{:S(2)}) collective-permute-start(f32[96,256]{1,0:T(8,128)S(1)} %collective-permute-done.10.refs_1_), channel_id=1, source_target_pairs={{0,1},{1,0},{2,3},{3,2},{4,5},{5,4},{6,7},{7,6},{8,9},{9,8},{10,11... | collective-permute-start | bytes 294920 | tf_op jit(solution)/shard_map/ppermute | solution.py:302
  57.6 5.2 %collective-permute-start.19 = (f32[96,256]{1,0:T(8,128)S(1)}, f32[96,256]{1,0:T(8,128)S(1)}, u32[]{:S(2)}, u32[]{:S(2)}) collective-permute-start(f32[96,256]{1,0:T(8,128)S(1)} %collective-permute-done.11.refs_2_), channel_id=1, source_target_pairs={{0,1},{1,0},{2,3},{3,2},{4,5},{5,4},{6,7},{7,6},{8,9},{9,8},{10,11... | collective-permute-start | bytes 294920 | tf_op jit(solution)/shard_map/ppermute | solution.py:302
  58.1 5.6 %collective-permute-start.20 = (f32[96,256]{1,0:T(8,128)S(1)}, f32[96,256]{1,0:T(8,128)S(1)}, u32[]{:S(2)}, u32[]{:S(2)}) collective-permute-start(f32[96,256]{1,0:T(8,128)S(1)} %collective-permute-done.12.refs_3_), channel_id=1, source_target_pairs={{0,1},{1,0},{2,3},{3,2},{4,5},{5,4},{6,7},{7,6},{8,9},{9,8},{10,11... | collective-permute-start | bytes 294920 | tf_op jit(solution)/shard_map/ppermute | solution.py:302
  61.2 2.5 %collective-permute-start.21 = (f32[96,256]{1,0:T(8,128)S(1)}, f32[96,256]{1,0:T(8,128)S(1)}, u32[]{:S(2)}, u32[]{:S(2)}) collective-permute-start(f32[96,256]{1,0:T(8,128)S(1)} %collective-permute-done.13.refs_4_), channel_id=1, source_target_pairs={{0,1},{1,0},{2,3},{3,2},{4,5},{5,4},{6,7},{7,6},{8,9},{9,8},{10,11... | collective-permute-start | bytes 294920 | tf_op jit(solution)/shard_map/ppermute | solution.py:302
  62.3 1.4 %collective-permute-start.22 = (f32[96,256]{1,0:T(8,128)S(1)}, f32[96,256]{1,0:T(8,128)S(1)}, u32[]{:S(2)}, u32[]{:S(2)}) collective-permute-start(f32[96,256]{1,0:T(8,128)S(1)} %collective-permute-done.14.refs_5_), channel_id=1, source_target_pairs={{0,1},{1,0},{2,3},{3,2},{4,5},{5,4},{6,7},{7,6},{8,9},{9,8},{10,11... | collective-permute-start | bytes 294920 | tf_op jit(solution)/shard_map/ppermute | solution.py:302
  62.3 1.5 %collective-permute-start.23 = (f32[96,256]{1,0:T(8,128)S(1)}, f32[96,256]{1,0:T(8,128)S(1)}, u32[]{:S(2)}, u32[]{:S(2)}) collective-permute-start(f32[96,256]{1,0:T(8,128)S(1)} %collective-permute-done.15.refs_6_), channel_id=1, source_target_pairs={{0,1},{1,0},{2,3},{3,2},{4,5},{5,4},{6,7},{7,6},{8,9},{9,8},{10,11... | collective-permute-start | bytes 294920 | tf_op jit(solution)/shard_map/ppermute | solution.py:302
  (5 other events, 107.4 us)
where the time goes:
time: 67.7 us; the launch traced here: 67.5 us
  waiting for transfers between devices  30.9 us (46%)
  starting transfers between devices  22.3 us (33%)
  Pallas kernels  11.2 us (17%)
  local copies, waits for them, and re-layouts  1.63 us (2%)
  between operations  1.47 us (2%)
    ppermute x25, waiting for transfers between devices, send(): return lax.ppermute(value, 'space', route)  30.9 us
    ppermute x25, starting transfers between devices, send(): return lax.ppermute(value, 'space', route)  22.3 us
    pallas_call x6, Pallas kernels, call(): pl.pallas_call(kernel, out_shape=out, in_specs=[SMEM] * scalars + [VMEM]...  11.2 us
    squeeze x1, local copies, waits for them, and re-layouts, program(): theirs = lax.dynamic_index_in_dim(vectors, 1 - odd, 0, keepdims=False)  1.55 us
  transfers between devices with their start and end apart: 25, of which 11 were waited for; matrix products, arithmetic and copies ran while one was open for 0% of the time, Pallas kernels for 5%

commit v1 on v0

--- a/solution.py
+++ b/solution.py
@@ -155,7 +155,7 @@
     size = outs[0].shape[0]
     pair = place_ref[0] // 4
     for d in range(count):
-        at = lax.rem(pair + d, count) * size
+        at = (pair ^ d) * size
         outs[d][...] = total_ref[pl.ds(pl.multiple_of(at, 8), size), :]
 
 
@@ -224,7 +224,7 @@
             for d in range(count):
                 time = (odd + other) % 2
                 base = (time * 2 + (core + side) % 2) * half
-                at = base + lax.rem(pair - d + count, count) * size
+                at = base + (pair ^ d) * size
                 piece = pieces[(side * 2 + other) * count + d]
                 all_ref[pl.ds(pl.multiple_of(at, 8), size), :] = piece[...]
     rows = elem_ref.shape[3]
@@ -306,16 +306,21 @@
     twin = lambda pair, o, core: (pair, o, 1 - core)
     along = lambda pair, o, core: (pair + (1 if o else -1), o, core)
 
-    def shift(d):
-        return lambda pair, o, core: (pair + d, o, core)
+    def hop(d):
+        return lambda pair, o, core: (pair ^ d, o, core)
+
+    hops = sorted(range(1, pairs), key=lambda d: (d & 1, -d))
+    if pairs == 4:
+        hops = [2, 1, 3]
 
     flat = links.transpose(0, 1, 3, 4, 2, 5).reshape(links.shape[0] * 54, sites)
+    theirs = lax.dynamic_index_in_dim(vectors, 1 - odd, 0, keepdims=False)
+    vectors, theirs = lax.optimization_barrier((vectors, theirs))
+    vec_b = send(theirs, partner)
+    mine = lax.dynamic_index_in_dim(vectors, odd, 0, keepdims=False)
+    vec_c = send(mine, along)
     link_b = send(flat, partner)
     link_c = send(flat, along)
-    theirs = lax.dynamic_index_in_dim(vectors, 1 - odd, 0, keepdims=False)
-    mine = lax.dynamic_index_in_dim(vectors, odd, 0, keepdims=False)
-    vec_b = send(theirs, partner)
-    vec_c = send(mine, along)
     halo_a = send(mine[:, :, :LZ], twin)
     halo_b = send(theirs[:, :, :LZ], across)
 
@@ -343,11 +348,17 @@
     size = half // pairs
     spread = call(spread_kernel, (shape(size, width),) * pairs, (places, keep, got), scalars=1,
                   scratch=(pltpu.VMEM((half, width), jnp.float32),))
-    parts = [spread[0]] + [send(spread[d], shift(d)) for d in range(1, pairs)]
+    parts = [spread[0]]
+    for d in hops:
+        parts.append(send(spread[d], hop(d)))
     shard = call(sum_kernel, shape(size, width), parts)
-    here = [shard] + [send(shard, shift(d)) for d in range(1, pairs)]
-    there = [send(x, partner) for x in here]
-    pieces = here + there
+    here = {0: shard}
+    for d in hops:
+        here[d] = send(shard, hop(d))
+    there = {}
+    for d in [0] + hops:
+        there[d] = send(here[d], partner)
+    pieces = [here[d] for d in range(pairs)] + [there[d] for d in range(pairs)]
     pieces = pieces + [send(x, twin) for x in pieces]
 
     return call(

time: 67.7 us -> 70.8 us (1.046)
  local copies, waits for them, and re-layouts: 1.63 us -> 3.36 us
  starting transfers between devices: 22.3 us -> 23.6 us
  Pallas kernels: 11.2 us -> 12.3 us
  waiting for transfers between devices: 30.9 us -> 29.9 us
    unnamed x8 -> x10, local copies, waits for them, and re-layouts: 0.02 us -> 1.39 us
    ppermute x25, starting transfers between devices: 22.3 us -> 23.6 us  [send(): return lax.ppermute(value, 'space', route)]
    pallas_call x6, Pallas kernels: 11.2 us -> 12.3 us  [call(): pl.pallas_call(kernel, out_shape=out, in_specs=[SMEM] * scalars + [VMEM]...]
    ppermute x25, waiting for transfers between devices: 30.9 us -> 29.9 us  [send(): return lax.ppermute(value, 'space', route)]
    slice x1, local copies, waits for them, and re-layouts: 0.01 us -> 0.9 us  [program(): halo_b = send(theirs[:, :, :LZ], across)]
  transfers between devices with their start and end apart: 25 -> 25, of which waited for: 11 -> 9; matrix products, arithmetic and copies ran while one was open for 0% -> 1% of each run, Pallas kernels for 5% -> 5%
where the time goes in v1:
time: 70.8 us; the launch traced here: 70.6 us
  waiting for transfers between devices  29.9 us (42%)
  starting transfers between devices  23.6 us (33%)
  Pallas kernels  12.3 us (17%)
  local copies, waits for them, and re-layouts  3.36 us (5%)
  between operations  1.47 us (2%)
    ppermute x25, waiting for transfers between devices, send(): return lax.ppermute(value, 'space', route)  29.9 us
    ppermute x25, starting transfers between devices, send(): return lax.ppermute(value, 'space', route)  23.6 us
    pallas_call x6, Pallas kernels, call(): pl.pallas_call(kernel, out_shape=out, in_specs=[SMEM] * scalars + [VMEM]...  12.3 us
  transfers between devices with their start and end apart: 25, of which 9 were waited for; matrix products, arithmetic and copies ran while one was open for 1% of the time, Pallas kernels for 5%

profile of v1, /device:TPU:0, one launch (start us, length us, event | category | flops | bytes accessed | tf_op | source)
XLA Modules:
  0.0 70.6 jit_solution(159749526345640572)
XLA Ops:
  0.7 1.4 %copy-done = f32[2,2,3,128,256]{4,3,2,1,0:T(8,128)S(1)} copy-done((f32[2,2,3,128,256]{4,3,2,1,0:T(8,128)S(1)}, f32[2,2,3,128,256]{4,3,2,1,0:T(8,128)}, u32[]{:S(2)}) %copy-start) | copy-done | bytes 1572888
  2.0 0.9 %dynamic-slice_bitcast_fusion.1 = f32[2,3,128,256]{3,2,1,0:T(8,128)} fusion(f32[2,2,3,128,256]{4,3,2,1,0:T(8,128)S(1)} %copy-done, s32[]{:T(128)S(6)} %select_n.20), kind=kLoop, calls=%fused_computation.1 | loop fusion | bytes 1572868 | tf_op jit(solution)/shard_map/jit(dynamic_index_in_dim)/squeeze | solution.py:317
  3.1 5.1 %collective-permute-start.1 = (f32[2,3,128,256]{3,2,1,0:T(8,128)S(1)}, f32[2,3,128,256]{3,2,1,0:T(8,128)S(1)}, u32[]{:S(2)}, u32[]{:S(2)}) collective-permute-start(f32[2,3,128,256]{3,2,1,0:T(8,128)S(1)} %dynamic-slice_bitcast_fusion.v_ref.va_ref), channel_id=1, source_target_pairs={{0,12},{1,13},{2,6},{3,7},{4,0},{5,1},{6,10},{7,11},{8,4},{9,5},{1... | collective-permute-start | bytes 2359304 | tf_op jit(solution)/shard_map/ppermute | solution.py:302
  8.4 2.1 %collective-permute-start.3 = (f32[108,128]{1,0:T(8,128)S(1)}, f32[108,128]{1,0:T(8,128)S(1)}, u32[]{:S(2)}, u32[]{:S(2)}) collective-permute-start(f32[108,128]{1,0:T(8,128)S(1)} %reshape.7.link_ref.link_a), channel_id=1, source_target_pairs={{0,2},{1,3},{2,0},{3,1},{4,6},{5,7},{6,4},{7,5},{8,10},{9,11},{10,... | collective-permute-start | bytes 165896 | tf_op jit(solution)/shard_map/ppermute | solution.py:302
  10.9 0.9 %slice.6 = f32[2,3,16,256]{3,2,1,0:T(8,128)S(1)} slice(f32[2,3,128,256]{3,2,1,0:T(8,128)} %dynamic-slice_bitcast_fusion.1), slice={[0:2], [0:3], [0:16], [0:256]} | slice | bytes 196608 | tf_op jit(solution)/shard_map/slice | solution.py:325
  12.0 3.1 %shard_map.78.own_ref = f32[2,256,256]{2,1,0:T(8,128)S(1)} custom-call(s32[1]{0:T(128)} %bitcast.place_ref, f32[2,3,128,256]{3,2,1,0:T(8,128)S(1)} %dynamic-slice_bitcast_fusion.v_ref.va_ref, f32[2,3,16,256]{3,2,1,0:T(8,128)S(1)} %collective-permute-done.5.halo_ref, f32[108,128]{1,0:T(8,128)S(1)} %reshape.7.link_ref.link_a), custom_call_target="tpu_custom_call" | custom-call | flops 1207959552 | bytes 1464324 | tf_op jit(solution)/shard_map/pallas_call | solution.py:278
  15.1 14.6 %collective-permute-done.3.link_b = f32[108,128]{1,0:T(8,128)S(1)} collective-permute-done((f32[108,128]{1,0:T(8,128)S(1)}, f32[108,128]{1,0:T(8,128)S(1)}, u32[]{:S(2)}, u32[]{:S(2)}) %collective-permute-start.3) | collective-permute-done | bytes 55328 | tf_op jit(solution)/shard_map/ppermute | solution.py:302
  29.7 5.5 %shard_map.79 = (f32[384,256]{1,0:T(8,128)S(1)}, f32[384,256]{1,0:T(8,128)S(1)}) custom-call(s32[1]{0:T(128)} %bitcast.place_ref, f32[2,3,128,256]{3,2,1,0:T(8,128)S(1)} %dynamic-slice_bitcast_fusion.v_ref.va_ref, f32[2,3,128,256]{3,2,1,0:T(8,128)} %collective-permute-done.vb_ref, f32[2,3,128,256]{3,2,1,0:T(8,128)S(1)} %collective-permute-done.1.vc_ref, ...), custom_call_target="tpu_custom_call" | custom-call | flops 1811939328 | bytes 3934212 | tf_op jit(solution)/shard_map/pallas_call | solution.py:278
  35.3 0.9 %collective-permute-start.6 = (f32[384,256]{1,0:T(8,128)S(1)}, f32[384,256]{1,0:T(8,128)S(1)}, u32[]{:S(2)}, u32[]{:S(2)}) collective-permute-start(f32[384,256]{1,0:T(8,128)S(1)} %get-tuple-element.21), channel_id=1, source_target_pairs={{0,1},{1,0},{2,3},{3,2},{4,5},{5,4},{6,7},{7,6},{8,9},{9,8},{10,11... | collective-permute-start | bytes 1179656 | tf_op jit(solution)/shard_map/ppermute | solution.py:302
  36.2 1.3 %collective-permute-done.6.got_ref = f32[384,256]{1,0:T(8,128)S(1)} collective-permute-done((f32[384,256]{1,0:T(8,128)S(1)}, f32[384,256]{1,0:T(8,128)S(1)}, u32[]{:S(2)}, u32[]{:S(2)}) %collective-permute-start.6) | collective-permute-done | bytes 393248 | tf_op jit(solution)/shard_map/ppermute | solution.py:302
  38.0 0.7 collective-permute-start.8
  38.7 3.4 %collective-permute-start.9 = (f32[96,256]{1,0:T(8,128)S(1)}, f32[96,256]{1,0:T(8,128)S(1)}, u32[]{:S(2)}, u32[]{:S(2)}) collective-permute-start(f32[96,256]{1,0:T(8,128)S(1)} %get-tuple-element.25), channel_id=1, source_target_pairs={{0,12},{1,13},{2,14},{3,15},{4,8},{5,9},{6,10},{7,11},{8,4},{9,5},... | collective-permute-start | bytes 294920 | tf_op jit(solution)/shard_map/ppermute | solution.py:302
  42.1 3.2 %collective-permute-done.7.refs_1_ = f32[96,256]{1,0:T(8,128)S(1)} collective-permute-done((f32[96,256]{1,0:T(8,128)S(1)}, f32[96,256]{1,0:T(8,128)S(1)}, u32[]{:S(2)}, u32[]{:S(2)}) %collective-permute-start.7) | collective-permute-done | bytes 98336 | tf_op jit(solution)/shard_map/ppermute | solution.py:302
  45.8 1.2 %collective-permute-done.9.refs_3_ = f32[96,256]{1,0:T(8,128)S(1)} collective-permute-done((f32[96,256]{1,0:T(8,128)S(1)}, f32[96,256]{1,0:T(8,128)S(1)}, u32[]{:S(2)}, u32[]{:S(2)}) %collective-permute-start.9) | collective-permute-done | bytes 98336 | tf_op jit(solution)/shard_map/ppermute | solution.py:302
  47.1 2.4 %collective-permute-start.10 = (f32[96,256]{1,0:T(8,128)S(1)}, f32[96,256]{1,0:T(8,128)S(1)}, u32[]{:S(2)}, u32[]{:S(2)}) collective-permute-start(f32[96,256]{1,0:T(8,128)S(1)} %shard_map.81.refs_0_), channel_id=1, source_target_pairs={{0,4},{1,5},{2,6},{3,7},{4,0},{5,1},{6,2},{7,3},{8,12},{9,13},{10,... | collective-permute-start | bytes 294920 | tf_op jit(solution)/shard_map/ppermute | solution.py:302
  49.9 2.0 %collective-permute-start.12 = (f32[96,256]{1,0:T(8,128)S(1)}, f32[96,256]{1,0:T(8,128)S(1)}, u32[]{:S(2)}, u32[]{:S(2)}) collective-permute-start(f32[96,256]{1,0:T(8,128)S(1)} %shard_map.81.refs_0_), channel_id=1, source_target_pairs={{0,12},{1,13},{2,14},{3,15},{4,8},{5,9},{6,10},{7,11},{8,4},{9,5},... | collective-permute-start | bytes 294920 | tf_op jit(solution)/shard_map/ppermute | solution.py:302
  51.9 1.5 %collective-permute-start.13 = (f32[96,256]{1,0:T(8,128)S(1)}, f32[96,256]{1,0:T(8,128)S(1)}, u32[]{:S(2)}, u32[]{:S(2)}) collective-permute-start(f32[96,256]{1,0:T(8,128)S(1)} %shard_map.81.refs_0_), channel_id=1, source_target_pairs={{0,2},{1,3},{2,0},{3,1},{4,6},{5,7},{6,4},{7,5},{8,10},{9,11},{10,... | collective-permute-start | bytes 294920 | tf_op jit(solution)/shard_map/ppermute | solution.py:302
  53.4 0.7 %collective-permute-start.14 = (f32[96,256]{1,0:T(8,128)S(1)}, f32[96,256]{1,0:T(8,128)S(1)}, u32[]{:S(2)}, u32[]{:S(2)}) collective-permute-start(f32[96,256]{1,0:T(8,128)S(1)} %collective-permute-done.10.refs_1_), channel_id=1, source_target_pairs={{0,2},{1,3},{2,0},{3,1},{4,6},{5,7},{6,4},{7,5},{8,10},{9,11},{10,... | collective-permute-start | bytes 294920 | tf_op jit(solution)/shard_map/ppermute | solution.py:302
  54.1 5.3 %collective-permute-done.11.refs_2_ = f32[96,256]{1,0:T(8,128)S(1)} collective-permute-done((f32[96,256]{1,0:T(8,128)S(1)}, f32[96,256]{1,0:T(8,128)S(1)}, u32[]{:S(2)}, u32[]{:S(2)}) %collective-permute-start.11) | collective-permute-done | bytes 98336 | tf_op jit(solution)/shard_map/ppermute | solution.py:302
  59.5 1.3 %collective-permute-start.15 = (f32[96,256]{1,0:T(8,128)S(1)}, f32[96,256]{1,0:T(8,128)S(1)}, u32[]{:S(2)}, u32[]{:S(2)}) collective-permute-start(f32[96,256]{1,0:T(8,128)S(1)} %collective-permute-done.11.refs_2_), channel_id=1, source_target_pairs={{0,2},{1,3},{2,0},{3,1},{4,6},{5,7},{6,4},{7,5},{8,10},{9,11},{10,... | collective-permute-start | bytes 294920 | tf_op jit(solution)/shard_map/ppermute | solution.py:302
  60.8 0.8 %collective-permute-start.16 = (f32[96,256]{1,0:T(8,128)S(1)}, f32[96,256]{1,0:T(8,128)S(1)}, u32[]{:S(2)}, u32[]{:S(2)}) collective-permute-start(f32[96,256]{1,0:T(8,128)S(1)} %collective-permute-done.12.refs_3_), channel_id=1, source_target_pairs={{0,2},{1,3},{2,0},{3,1},{4,6},{5,7},{6,4},{7,5},{8,10},{9,11},{10,... | collective-permute-start | bytes 294920 | tf_op jit(solution)/shard_map/ppermute | solution.py:302
  62.1 2.1 %collective-permute-done.15.refs_6_ = f32[96,256]{1,0:T(8,128)S(1)} collective-permute-done((f32[96,256]{1,0:T(8,128)S(1)}, f32[96,256]{1,0:T(8,128)S(1)}, u32[]{:S(2)}, u32[]{:S(2)}) %collective-permute-start.15) | collective-permute-done | bytes 98336 | tf_op jit(solution)/shard_map/ppermute | solution.py:302
  64.2 1.2 %collective-permute-done.16.refs_7_ = f32[96,256]{1,0:T(8,128)S(1)} collective-permute-done((f32[96,256]{1,0:T(8,128)S(1)}, f32[96,256]{1,0:T(8,128)S(1)}, u32[]{:S(2)}, u32[]{:S(2)}) %collective-permute-start.16) | collective-permute-done | bytes 98336 | tf_op jit(solution)/shard_map/ppermute | solution.py:302
  67.2 3.4 %shard_map.82 = (f32[2,3,2,16,256]{4,3,2,1,0:T(8,128)}, f32[2,64,64]{2,1,0:T(8,128)}) custom-call(s32[1]{0:T(128)} %bitcast.place_ref, s32[3]{0:T(128)S(1)} %copy-done.2, s32[2]{0:T(128)S(1)} %copy-done.3, s32[1]{0:T(128)S(6)} %copy.8.block_ref, bf16[256,1536]{1,0:T(8,128)(2,1)S(1)} %get-tuple-element.14.b_high, ...), custom_call_target="tpu_custom_call" | custom-call | flops 150994944 | bytes 3637276 | tf_op jit(solution)/shard_map/pallas_call | solution.py:278
  (47 shorter events, 4.2 us)
Async XLA Ops:
  3.1 26.6 %collective-permute-start.1 = (f32[2,3,128,256]{3,2,1,0:T(8,128)S(1)}, f32[2,3,128,256]{3,2,1,0:T(8,128)S(1)}, u32[]{:S(2)}, u32[]{:S(2)}) collective-permute-start(f32[2,3,128,256]{3,2,1,0:T(8,128)S(1)} %dynamic-slice_bitcast_fusion.v_ref.va_ref), channel_id=1, source_target_pairs={{0,12},{1,13},{2,6},{3,7},{4,0},{5,1},{6,10},{7,11},{8,4},{9,5},{1... | collective-permute-start | bytes 2359304 | tf_op jit(solution)/shard_map/ppermute | solution.py:302
  8.2 21.5 %collective-permute-start = (f32[2,3,128,256]{3,2,1,0:T(8,128)}, f32[2,3,128,256]{3,2,1,0:T(8,128)}, u32[]{:S(2)}, u32[]{:S(2)}) collective-permute-start(f32[2,3,128,256]{3,2,1,0:T(8,128)} %dynamic-slice_bitcast_fusion.1), channel_id=1, source_target_pairs={{0,2},{1,3},{2,0},{3,1},{4,6},{5,7},{6,4},{7,5},{8,10},{9,11},{10,... | collective-permute-start | bytes 2359304 | tf_op jit(solution)/shard_map/ppermute | solution.py:302
  8.2 3.6 %collective-permute-start.5 = (f32[2,3,16,256]{3,2,1,0:T(8,128)S(1)}, f32[2,3,16,256]{3,2,1,0:T(8,128)S(1)}, u32[]{:S(2)}, u32[]{:S(2)}) collective-permute-start(f32[2,3,16,256]{3,2,1,0:T(8,128)S(1)} %slice.8), channel_id=1, source_target_pairs={{0,1},{1,0},{2,3},{3,2},{4,5},{5,4},{6,7},{7,6},{8,9},{9,8},{10,11... | collective-permute-start | bytes 294920 | tf_op jit(solution)/shard_map/ppermute | solution.py:302
  8.4 21.3 %collective-permute-start.3 = (f32[108,128]{1,0:T(8,128)S(1)}, f32[108,128]{1,0:T(8,128)S(1)}, u32[]{:S(2)}, u32[]{:S(2)}) collective-permute-start(f32[108,128]{1,0:T(8,128)S(1)} %reshape.7.link_ref.link_a), channel_id=1, source_target_pairs={{0,2},{1,3},{2,0},{3,1},{4,6},{5,7},{6,4},{7,5},{8,10},{9,11},{10,... | collective-permute-start | bytes 165896 | tf_op jit(solution)/shard_map/ppermute | solution.py:302
  10.4 19.3 %collective-permute-start.4 = (f32[108,128]{1,0:T(8,128)S(1)}, f32[108,128]{1,0:T(8,128)S(1)}, u32[]{:S(2)}, u32[]{:S(2)}) collective-permute-start(f32[108,128]{1,0:T(8,128)S(1)} %reshape.7.link_ref.link_a), channel_id=1, source_target_pairs={{0,12},{1,13},{2,6},{3,7},{4,0},{5,1},{6,10},{7,11},{8,4},{9,5},{1... | collective-permute-start | bytes 165896 | tf_op jit(solution)/shard_map/ppermute | solution.py:302
  11.8 17.9 %collective-permute-start.2 = (f32[2,3,16,256]{3,2,1,0:T(8,128)S(1)}, f32[2,3,16,256]{3,2,1,0:T(8,128)S(1)}, u32[]{:S(2)}, u32[]{:S(2)}) collective-permute-start(f32[2,3,16,256]{3,2,1,0:T(8,128)S(1)} %slice.6), channel_id=1, source_target_pairs={{0,3},{1,2},{2,1},{3,0},{4,7},{5,6},{6,5},{7,4},{8,11},{9,10},{10,... | collective-permute-start | bytes 294920 | tf_op jit(solution)/shard_map/ppermute | solution.py:302
  35.3 2.3 %collective-permute-start.6 = (f32[384,256]{1,0:T(8,128)S(1)}, f32[384,256]{1,0:T(8,128)S(1)}, u32[]{:S(2)}, u32[]{:S(2)}) collective-permute-start(f32[384,256]{1,0:T(8,128)S(1)} %get-tuple-element.21), channel_id=1, source_target_pairs={{0,1},{1,0},{2,3},{3,2},{4,5},{5,4},{6,7},{7,6},{8,9},{9,8},{10,11... | collective-permute-start | bytes 1179656 | tf_op jit(solution)/shard_map/ppermute | solution.py:302
  37.6 7.7 %collective-permute-start.7 = (f32[96,256]{1,0:T(8,128)S(1)}, f32[96,256]{1,0:T(8,128)S(1)}, u32[]{:S(2)}, u32[]{:S(2)}) collective-permute-start(f32[96,256]{1,0:T(8,128)S(1)} %get-tuple-element.23), channel_id=1, source_target_pairs={{0,8},{1,9},{2,10},{3,11},{4,12},{5,13},{6,14},{7,15},{8,0},{9,1},... | collective-permute-start | bytes 294920 | tf_op jit(solution)/shard_map/ppermute | solution.py:302
  38.0 7.8 %collective-permute-start.8 = (f32[96,256]{1,0:T(8,128)S(1)}, f32[96,256]{1,0:T(8,128)S(1)}, u32[]{:S(2)}, u32[]{:S(2)}) collective-permute-start(f32[96,256]{1,0:T(8,128)S(1)} %get-tuple-element.24), channel_id=1, source_target_pairs={{0,4},{1,5},{2,6},{3,7},{4,0},{5,1},{6,2},{7,3},{8,12},{9,13},{10,... | collective-permute-start | bytes 294920 | tf_op jit(solution)/shard_map/ppermute | solution.py:302
  38.7 8.3 %collective-permute-start.9 = (f32[96,256]{1,0:T(8,128)S(1)}, f32[96,256]{1,0:T(8,128)S(1)}, u32[]{:S(2)}, u32[]{:S(2)}) collective-permute-start(f32[96,256]{1,0:T(8,128)S(1)} %get-tuple-element.25), channel_id=1, source_target_pairs={{0,12},{1,13},{2,14},{3,15},{4,8},{5,9},{6,10},{7,11},{8,4},{9,5},... | collective-permute-start | bytes 294920 | tf_op jit(solution)/shard_map/ppermute | solution.py:302
  47.1 6.3 %collective-permute-start.10 = (f32[96,256]{1,0:T(8,128)S(1)}, f32[96,256]{1,0:T(8,128)S(1)}, u32[]{:S(2)}, u32[]{:S(2)}) collective-permute-start(f32[96,256]{1,0:T(8,128)S(1)} %shard_map.81.refs_0_), channel_id=1, source_target_pairs={{0,4},{1,5},{2,6},{3,7},{4,0},{5,1},{6,2},{7,3},{8,12},{9,13},{10,... | collective-permute-start | bytes 294920 | tf_op jit(solution)/shard_map/ppermute | solution.py:302
  49.5 10.0 %collective-permute-start.11 = (f32[96,256]{1,0:T(8,128)S(1)}, f32[96,256]{1,0:T(8,128)S(1)}, u32[]{:S(2)}, u32[]{:S(2)}) collective-permute-start(f32[96,256]{1,0:T(8,128)S(1)} %shard_map.81.refs_0_), channel_id=1, source_target_pairs={{0,8},{1,9},{2,10},{3,11},{4,12},{5,13},{6,14},{7,15},{8,0},{9,1},... | collective-permute-start | bytes 294920 | tf_op jit(solution)/shard_map/ppermute | solution.py:302
  49.9 10.8 %collective-permute-start.12 = (f32[96,256]{1,0:T(8,128)S(1)}, f32[96,256]{1,0:T(8,128)S(1)}, u32[]{:S(2)}, u32[]{:S(2)}) collective-permute-start(f32[96,256]{1,0:T(8,128)S(1)} %shard_map.81.refs_0_), channel_id=1, source_target_pairs={{0,12},{1,13},{2,14},{3,15},{4,8},{5,9},{6,10},{7,11},{8,4},{9,5},... | collective-permute-start | bytes 294920 | tf_op jit(solution)/shard_map/ppermute | solution.py:302
  51.9 9.6 %collective-permute-start.13 = (f32[96,256]{1,0:T(8,128)S(1)}, f32[96,256]{1,0:T(8,128)S(1)}, u32[]{:S(2)}, u32[]{:S(2)}) collective-permute-start(f32[96,256]{1,0:T(8,128)S(1)} %shard_map.81.refs_0_), channel_id=1, source_target_pairs={{0,2},{1,3},{2,0},{3,1},{4,6},{5,7},{6,4},{7,5},{8,10},{9,11},{10,... | collective-permute-start | bytes 294920 | tf_op jit(solution)/shard_map/ppermute | solution.py:302
  53.4 8.1 %collective-permute-start.17 = (f32[96,256]{1,0:T(8,128)S(1)}, f32[96,256]{1,0:T(8,128)S(1)}, u32[]{:S(2)}, u32[]{:S(2)}) collective-permute-start(f32[96,256]{1,0:T(8,128)S(1)} %shard_map.81.refs_0_), channel_id=1, source_target_pairs={{0,1},{1,0},{2,3},{3,2},{4,5},{5,4},{6,7},{7,6},{8,9},{9,8},{10,11... | collective-permute-start | bytes 294920 | tf_op jit(solution)/shard_map/ppermute | solution.py:302
  53.4 8.6 %collective-permute-start.14 = (f32[96,256]{1,0:T(8,128)S(1)}, f32[96,256]{1,0:T(8,128)S(1)}, u32[]{:S(2)}, u32[]{:S(2)}) collective-permute-start(f32[96,256]{1,0:T(8,128)S(1)} %collective-permute-done.10.refs_1_), channel_id=1, source_target_pairs={{0,2},{1,3},{2,0},{3,1},{4,6},{5,7},{6,4},{7,5},{8,10},{9,11},{10,... | collective-permute-start | bytes 294920 | tf_op jit(solution)/shard_map/ppermute | solution.py:302
  59.5 4.7 %collective-permute-start.15 = (f32[96,256]{1,0:T(8,128)S(1)}, f32[96,256]{1,0:T(8,128)S(1)}, u32[]{:S(2)}, u32[]{:S(2)}) collective-permute-start(f32[96,256]{1,0:T(8,128)S(1)} %collective-permute-done.11.refs_2_), channel_id=1, source_target_pairs={{0,2},{1,3},{2,0},{3,1},{4,6},{5,7},{6,4},{7,5},{8,10},{9,11},{10,... | collective-permute-start | bytes 294920 | tf_op jit(solution)/shard_map/ppermute | solution.py:302
  60.8 4.6 %collective-permute-start.16 = (f32[96,256]{1,0:T(8,128)S(1)}, f32[96,256]{1,0:T(8,128)S(1)}, u32[]{:S(2)}, u32[]{:S(2)}) collective-permute-start(f32[96,256]{1,0:T(8,128)S(1)} %collective-permute-done.12.refs_3_), channel_id=1, source_target_pairs={{0,2},{1,3},{2,0},{3,1},{4,6},{5,7},{6,4},{7,5},{8,10},{9,11},{10,... | collective-permute-start | bytes 294920 | tf_op jit(solution)/shard_map/ppermute | solution.py:302
  61.5 3.9 %collective-permute-start.18 = (f32[96,256]{1,0:T(8,128)S(1)}, f32[96,256]{1,0:T(8,128)S(1)}, u32[]{:S(2)}, u32[]{:S(2)}) collective-permute-start(f32[96,256]{1,0:T(8,128)S(1)} %collective-permute-done.10.refs_1_), channel_id=1, source_target_pairs={{0,1},{1,0},{2,3},{3,2},{4,5},{5,4},{6,7},{7,6},{8,9},{9,8},{10,11... | collective-permute-start | bytes 294920 | tf_op jit(solution)/shard_map/ppermute | solution.py:302
  61.5 4.4 %collective-permute-start.19 = (f32[96,256]{1,0:T(8,128)S(1)}, f32[96,256]{1,0:T(8,128)S(1)}, u32[]{:S(2)}, u32[]{:S(2)}) collective-permute-start(f32[96,256]{1,0:T(8,128)S(1)} %collective-permute-done.11.refs_2_), channel_id=1, source_target_pairs={{0,1},{1,0},{2,3},{3,2},{4,5},{5,4},{6,7},{7,6},{8,9},{9,8},{10,11... | collective-permute-start | bytes 294920 | tf_op jit(solution)/shard_map/ppermute | solution.py:302
  62.0 4.7 %collective-permute-start.20 = (f32[96,256]{1,0:T(8,128)S(1)}, f32[96,256]{1,0:T(8,128)S(1)}, u32[]{:S(2)}, u32[]{:S(2)}) collective-permute-start(f32[96,256]{1,0:T(8,128)S(1)} %collective-permute-done.12.refs_3_), channel_id=1, source_target_pairs={{0,1},{1,0},{2,3},{3,2},{4,5},{5,4},{6,7},{7,6},{8,9},{9,8},{10,11... | collective-permute-start | bytes 294920 | tf_op jit(solution)/shard_map/ppermute | solution.py:302
  64.2 2.6 %collective-permute-start.21 = (f32[96,256]{1,0:T(8,128)S(1)}, f32[96,256]{1,0:T(8,128)S(1)}, u32[]{:S(2)}, u32[]{:S(2)}) collective-permute-start(f32[96,256]{1,0:T(8,128)S(1)} %collective-permute-done.13.refs_4_), channel_id=1, source_target_pairs={{0,1},{1,0},{2,3},{3,2},{4,5},{5,4},{6,7},{7,6},{8,9},{9,8},{10,11... | collective-permute-start | bytes 294920 | tf_op jit(solution)/shard_map/ppermute | solution.py:302
  65.4 1.4 %collective-permute-start.22 = (f32[96,256]{1,0:T(8,128)S(1)}, f32[96,256]{1,0:T(8,128)S(1)}, u32[]{:S(2)}, u32[]{:S(2)}) collective-permute-start(f32[96,256]{1,0:T(8,128)S(1)} %collective-permute-done.14.refs_5_), channel_id=1, source_target_pairs={{0,1},{1,0},{2,3},{3,2},{4,5},{5,4},{6,7},{7,6},{8,9},{9,8},{10,11... | collective-permute-start | bytes 294920 | tf_op jit(solution)/shard_map/ppermute | solution.py:302
  65.4 1.5 %collective-permute-start.23 = (f32[96,256]{1,0:T(8,128)S(1)}, f32[96,256]{1,0:T(8,128)S(1)}, u32[]{:S(2)}, u32[]{:S(2)}) collective-permute-start(f32[96,256]{1,0:T(8,128)S(1)} %collective-permute-done.15.refs_6_), channel_id=1, source_target_pairs={{0,1},{1,0},{2,3},{3,2},{4,5},{5,4},{6,7},{7,6},{8,9},{9,8},{10,11... | collective-permute-start | bytes 294920 | tf_op jit(solution)/shard_map/ppermute | solution.py:302
  (6 other events, 103.6 us)

commit v2 on v0

--- a/solution.py
+++ b/solution.py
@@ -28,16 +28,14 @@
     return dot(left[0], right[0]) + dot(left[0], right[1]) + dot(left[1], right[0])
 
 
-def store_left(v_ref, left_ref):
-    sites, width = v_ref.shape[2], v_ref.shape[3]
-    for part in range(2):
-        for colour in range(3):
-            high, low = split(v_ref[part, colour].T)
-            at = (part * 3 + colour) * sites
-            other = ((1 - part) * 3 + colour) * sites
-            for level, value in enumerate((high, low)):
-                left_ref[level, :width, at : at + sites] = value
-                left_ref[level, width:, other : other + sites] = value if part else -value
+def store_left(load, left_ref):
+    for colour in range(3):
+        real, imag = load(0, colour), load(1, colour)
+        count, width = 2 * real.shape[0], real.shape[1]
+        at = slice(colour * count, (colour + 1) * count)
+        for i, pair in enumerate(((real, imag), (imag, -real))):
+            for level, value in enumerate(split(jnp.concatenate(pair, axis=0).T)):
+                left_ref[level, i * width : (i + 1) * width, at] = value
 
 
 def add(total, term):
@@ -47,13 +45,16 @@
 def store_right(right_ref, row, sites, sources):
     width = right_ref.shape[2]
     coefs = []
-    for coef, base, _ in sources:
+    for coef, base, _, turned in sources:
         wide = [jnp.broadcast_to(coef[:, base + j : base + j + 1], (LZ, 128)) for j in range(18)]
+        if turned:
+            order = [(b * 6 + a * 2, a, b) for a in range(3) for b in range(3)]
+            wide = [w for at, _, _ in order for w in (-wide[at], wide[at + 1])]
         coefs.append(wide)
     for lanes in range(0, width, 128):
         cut = slice(lanes, lanes + 128)
         fields = []
-        for _, _, field in sources:
+        for _, _, field, _ in sources:
             real, imag = field(cut)
             fields.append(([r + i for r, i in zip(real, imag)], [r - i for r, i in zip(real, imag)]))
         for a in range(3):
@@ -64,8 +65,10 @@
                     alpha = add(add(alpha, real * plus[b]), imag * minus[b])
                     beta = add(add(beta, imag * plus[b]), -(real * minus[b]))
             for part, value in enumerate((alpha, beta)):
+                at = (a * 2 + part) * sites + row * LZ
+                if value is None:
+                    value = jnp.zeros((LZ, 128), jnp.float32)
                 high, low = split(value)
-                at = (part * 3 + a) * sites + row * LZ
                 right_ref[0, at : at + LZ, cut] = high
                 right_ref[1, at : at + LZ, cut] = low
 
@@ -103,29 +106,44 @@
     return both[:width] - both[width:].T
 
 
-def plane_yz(v_ref, halo_ref, coef, left_ref, right_ref):
-    sites = v_ref.shape[2]
-    rows = sites // LZ
-    for row in range(rows):
-        here = coef[row * LZ : (row + 1) * LZ]
-        ahead = row_of(v_ref, row + 1) if row + 1 < rows else row_of(halo_ref, 0)
-        store_right(right_ref.at[0], row, sites, [(here, 18, ahead)])
-        store_right(right_ref.at[1], row, sites, [(here, 36, row_of(v_ref, row, turn=True))])
-    return [contract(left_ref, right_ref.at[i]) for i in range(2)]
-
-
-def own_kernel(place_ref, v_ref, halo_ref, link_ref, out_ref, left_ref, right_ref, coef_ref):
+def own_kernel(place_ref, v0_ref, v1_ref, halo_ref, link_ref, out_ref, left_ref, right_ref,
+               coef_ref):
     odd = (place_ref[0] // 2) % 2
     coef_ref[:54, :] = of_time(link_ref, odd)
-    store_left(v_ref, left_ref)
+    store_left(lambda p, c: jnp.concatenate([v0_ref[p, c], v1_ref[p, c]], axis=0), left_ref)
     coef = coef_ref[...].T
-    for i, value in enumerate(plane_yz(v_ref, halo_ref, coef, left_ref, right_ref)):
-        out_ref[i] = value
-
-
-def main_kernel(place_ref, va_ref, vb_ref, vc_ref, halo_ref, link_a, link_b, link_c, own_ref,
-                keep_ref, send_ref, left_ref, right_ref, coef_ref, total_ref):
-    sites, width = vb_ref.shape[2], vb_ref.shape[3]
+    half = v0_ref.shape[2] // LZ
+
+    def at(row, turn=False):
+        if row == 2 * half:
+            return row_of(halo_ref, 0)
+        return row_of((v0_ref, v1_ref)[row // half], row % half, turn)
+
+    for row in range(2 * half):
+        here = coef[row * LZ : (row + 1) * LZ]
+        sites = 2 * half * LZ
+        store_right(right_ref.at[0], row, sites, [(here, 18, at(row + 1), False)])
+        store_right(right_ref.at[1], row, sites, [(here, 36, at(row, True), False)])
+    for i in range(2):
+        out_ref[i] = contract(left_ref, right_ref.at[i])
+
+
+def chunk(va_ref, vb_ref, vc_ref, coef, start, ahead, left_ref, right_ref):
+    sites = vb_ref.shape[2]
+    store_left(lambda p, c: vb_ref[p, c], left_ref)
+    for row in range(sites // LZ):
+        here = coef[start + row * LZ : start + (row + 1) * LZ]
+        along = [(here, 56, row_of(va_ref, row), False), (here, 80, row_of(vc_ref, row), False)]
+        store_right(right_ref.at[0], row, sites, along)
+        store_right(right_ref.at[1], row, sites, ahead(row, here))
+        store_right(right_ref.at[2], row, sites, [(here, 36, row_of(vb_ref, row, True), False)])
+    return [contract(left_ref, right_ref.at[i]) for i in range(3)]
+
+
+def first_kernel(place_ref, va_ref, vb_ref, vc_ref, link_a, link_b, link_c, own_ref,
+                 out_ref, turned_ref, left_ref, right_ref, coef_ref):
+    width = vb_ref.shape[3]
+    rows = vb_ref.shape[2] // LZ
     odd = (place_ref[0] // 2) % 2
     coef_ref[:54, :] = of_time(link_b, odd)
     there = coef_ref[:18, :]
@@ -133,15 +151,34 @@
     after = adjoint_rows(of_time(link_c, odd)[:18])
     coef_ref[56:74, :] = jnp.where(odd == 0, before, there)
     coef_ref[80:98, :] = jnp.where(odd == 0, there, after)
-    coef = coef_ref[...].T
-    store_left(vb_ref, left_ref)
-    for i, value in enumerate(plane_yz(vb_ref, halo_ref, coef, left_ref, right_ref)):
-        total_ref[(i + 1) * width : (i + 2) * width, :] = value + own_ref[i]
-    for row in range(sites // LZ):
-        here = coef[row * LZ : (row + 1) * LZ]
-        sources = [(here, 56, row_of(va_ref, row)), (here, 80, row_of(vc_ref, row))]
-        store_right(right_ref.at[2], row, sites, sources)
-    total_ref[:width, :] = contract(left_ref, right_ref.at[2])
+    turned_ref[...] = coef_ref[...].T
+    coef = turned_ref[...]
+
+    def ahead(row, here):
+        return [(here, 18, row_of(vb_ref, row + 1), False)] if row + 1 < rows else []
+
+    sums = chunk(va_ref, vb_ref, vc_ref, coef, 0, ahead, left_ref, right_ref)
+    for i, value in enumerate(sums):
+        out_ref[i * width : (i + 1) * width, :] = value + own_ref[i - 1] if i else value
+
+
+def last_kernel(place_ref, va_ref, vb_ref, vc_ref, before_ref, halo_ref, turned_ref, first_ref,
+                keep_ref, send_ref, left_ref, right_ref, total_ref):
+    sites, width = vb_ref.shape[2], vb_ref.shape[3]
+    rows = sites // LZ
+    coef = turned_ref[...]
+
+    def ahead(row, here):
+        field = row_of(vb_ref, row + 1) if row + 1 < rows else row_of(halo_ref, 0)
+        out = [(here, 18, field, False)]
+        if row == 0:
+            out.append((coef[sites - LZ : sites], 18, row_of(before_ref, rows - 1), True))
+        return out
+
+    sums = chunk(va_ref, vb_ref, vc_ref, coef, sites, ahead, left_ref, right_ref)
+    for i, value in enumerate(sums):
+        at = slice(i * width, (i + 1) * width)
+        total_ref[at, :] = value + first_ref[at, :]
     core = place_ref[0] % 2
     half = 3 * width // 2
     keep_ref[...] = total_ref[pl.ds(pl.multiple_of(core * half, 8), half), :]
@@ -302,7 +339,6 @@
         return lax.ppermute(value, "space", route)
 
     partner = lambda pair, o, core: (pair, 1 - o, core)
-    across = lambda pair, o, core: (pair, 1 - o, 1 - core)
     twin = lambda pair, o, core: (pair, o, 1 - core)
     along = lambda pair, o, core: (pair + (1 if o else -1), o, core)
 
@@ -310,21 +346,33 @@
         return lambda pair, o, core: (pair + d, o, core)
 
     flat = links.transpose(0, 1, 3, 4, 2, 5).reshape(links.shape[0] * 54, sites)
+    part = sites // 2
+
+    def cut(time, i):
+        block = (1,) + vectors.shape[1:3] + (part, width)
+        return lax.dynamic_slice(vectors, (time, 0, 0, i * part, 0), block)[0]
+
+    mine = [cut(odd, i) for i in range(2)]
+    theirs = [cut(1 - odd, i) for i in range(2)]
+    vec_b, vec_c = [], []
+    for i in range(2):
+        vec_b.append(send(theirs[i], partner))
+        vec_c.append(send(mine[i], along))
     link_b = send(flat, partner)
     link_c = send(flat, along)
-    theirs = lax.dynamic_index_in_dim(vectors, 1 - odd, 0, keepdims=False)
-    mine = lax.dynamic_index_in_dim(vectors, odd, 0, keepdims=False)
-    vec_b = send(theirs, partner)
-    vec_c = send(mine, along)
-    halo_a = send(mine[:, :, :LZ], twin)
-    halo_b = send(theirs[:, :, :LZ], across)
-
-    left = pltpu.VMEM((2, 2 * width, 6 * sites), jnp.bfloat16)
-    right = lambda n: pltpu.VMEM((n, 2, 6 * sites, width), jnp.bfloat16)
+    halo_a = send(mine[0][:, :, :LZ], twin)
+    halo_b = send(vec_b[0][:, :, :LZ], twin)
+
+    def left(n):
+        return pltpu.VMEM((2, 2 * width, 6 * n), jnp.bfloat16)
+
+    def right(count, n):
+        return pltpu.VMEM((count, 2, 6 * n, width), jnp.bfloat16)
+
     coef = pltpu.VMEM((128, sites), jnp.float32)
     work = 6 * 6 * sites * 2 * width * width
-    own = call(own_kernel, shape(2, width, width), (places, mine, halo_a, flat), scalars=1,
-               scratch=(left, right(2), coef), flops=2 * work)
+    own = call(own_kernel, shape(2, width, width), (places, *mine, halo_a, flat), scalars=1,
+               scratch=(left(sites), right(2, sites), coef), flops=2 * work)
     cols = peram.shape[2]
     turned = jnp.swapaxes(peram, 1, 2)
     bf16 = jnp.bfloat16
@@ -334,11 +382,15 @@
         + (shape(cols, 4 * width, dtype=bf16),) * 2,
         (turned,))
     half = 3 * width // 2
+    first, turned = call(
+        first_kernel, (shape(3 * width, width), shape(sites, 128)),
+        (places, mine[0], vec_b[0], vec_c[0], flat, link_b, link_c, own), scalars=1,
+        scratch=(left(part), right(3, part), coef), flops=2 * work)
     keep, give = call(
-        main_kernel, (shape(half, width),) * 2,
-        (places, mine, vec_b, vec_c, halo_b, flat, link_b, link_c, own), scalars=1,
-        scratch=(left, right(3), coef, pltpu.VMEM((3 * width, width), jnp.float32)),
-        flops=3 * work)
+        last_kernel, (shape(half, width),) * 2,
+        (places, mine[1], vec_b[1], vec_c[1], vec_b[0], halo_b, turned, first), scalars=1,
+        scratch=(left(part), right(3, part), pltpu.VMEM((3 * width, width), jnp.float32)),
+        flops=2 * work)
     got = send(give, twin)
     size = half // pairs
     spread = call(spread_kernel, (shape(size, width),) * pairs, (places, keep, got), scalars=1,

time: 67.7 us -> 67.9 us (level)
  waiting for transfers between devices: 30.9 us -> 26.5 us
  starting transfers between devices: 22.3 us -> 26.4 us
    ppermute x25 -> x27, waiting for transfers between devices: 30.9 us -> 26.5 us  [send(): return lax.ppermute(value, 'space', route)]
    ppermute x25 -> x27, starting transfers between devices: 22.3 us -> 26.4 us  [send(): return lax.ppermute(value, 'space', route)]
    pallas_call x6 -> x7, Pallas kernels: 11.2 us -> 11.7 us  [call(): pl.pallas_call(kernel, out_shape=out, in_specs=[SMEM] * scalars + [VMEM]...]
  transfers between devices with their start and end apart: 25 -> 27, of which waited for: 11 -> 13; matrix products, arithmetic and copies ran while one was open for 0% -> 0% of each run, Pallas kernels for 5% -> 8%
where the time goes in v2:
time: 67.9 us; the launch traced here: 67.7 us
  waiting for transfers between devices  26.5 us (39%)
  starting transfers between devices  26.4 us (39%)
  Pallas kernels  11.7 us (17%)
  local copies, waits for them, and re-layouts  1.59 us (2%)
  between operations  1.5 us (2%)
    ppermute x27, waiting for transfers between devices, send(): return lax.ppermute(value, 'space', route)  26.5 us
    ppermute x27, starting transfers between devices, send(): return lax.ppermute(value, 'space', route)  26.4 us
    pallas_call x7, Pallas kernels, call(): pl.pallas_call(kernel, out_shape=out, in_specs=[SMEM] * scalars + [VMEM]...  11.7 us
    squeeze x1, local copies, waits for them, and re-layouts, cut(): return lax.dynamic_slice(vectors, (time, 0, 0, i * part, 0), block)[0]  1.51 us
  transfers between devices with their start and end apart: 27, of which 13 were waited for; matrix products, arithmetic and copies ran while one was open for 0% of the time, Pallas kernels for 8%

profile of v2, /device:TPU:0, one launch (start us, length us, event | category | flops | bytes accessed | tf_op | source)
XLA Modules:
  0.0 67.7 jit_solution(12391059053202102536)
XLA Ops:
  0.7 1.5 %dynamic-slice_bitcast_fusion = (f32[2,3,64,256]{3,2,1,0:T(8,128)S(1)}, f32[2,3,64,256]{3,2,1,0:T(8,128)S(1)}, f32[2,3,64,256]{3,2,1,0:T(8,128)S(1)}, f32[2,3,64,256]{3,2,1,0:T(8,128)S(1)}) fusion(f32[2,2,3,128,256]{4,3,2,1,0:T(8,128)} %param.6, s32[]{:T(128)S(6)} %select_n.21, s32[]{:T(128)S(6)} %select_n.22), kind=kLoop, calls=%fused_computation | loop fusion | bytes 3145736 | tf_op jit(solution)/shard_map/squeeze | solution.py:353
  2.2 3.1 %collective-permute-start.2 = (f32[2,3,64,256]{3,2,1,0:T(8,128)S(1)}, f32[2,3,64,256]{3,2,1,0:T(8,128)S(1)}, u32[]{:S(2)}, u32[]{:S(2)}) collective-permute-start(f32[2,3,64,256]{3,2,1,0:T(8,128)S(1)} %get-tuple-element.29), channel_id=1, source_target_pairs={{0,2},{1,3},{2,0},{3,1},{4,6},{5,7},{6,4},{7,5},{8,10},{9,11},{10,... | collective-permute-start | bytes 1179656 | tf_op jit(solution)/shard_map/ppermute | solution.py:339
  5.3 3.6 %collective-permute-start.4 = (f32[2,3,64,256]{3,2,1,0:T(8,128)S(1)}, f32[2,3,64,256]{3,2,1,0:T(8,128)S(1)}, u32[]{:S(2)}, u32[]{:S(2)}) collective-permute-start(f32[2,3,64,256]{3,2,1,0:T(8,128)S(1)} %get-tuple-element.26.v0_ref.va_ref), channel_id=1, source_target_pairs={{0,12},{1,13},{2,6},{3,7},{4,0},{5,1},{6,10},{7,11},{8,4},{9,5},{1... | collective-permute-start | bytes 1179656 | tf_op jit(solution)/shard_map/ppermute | solution.py:339
  9.5 1.2 %collective-permute-done.7.halo_ref = f32[2,3,16,256]{3,2,1,0:T(8,128)S(1)} collective-permute-done((f32[2,3,16,256]{3,2,1,0:T(8,128)S(1)}, f32[2,3,16,256]{3,2,1,0:T(8,128)S(1)}, u32[]{:S(2)}, u32[]{:S(2)}) %collective-permute-start.7) | collective-permute-done | bytes 98336 | tf_op jit(solution)/shard_map/ppermute | solution.py:339
  10.7 1.5 %collective-permute-start.5 = (f32[108,128]{1,0:T(8,128)S(1)}, f32[108,128]{1,0:T(8,128)S(1)}, u32[]{:S(2)}, u32[]{:S(2)}) collective-permute-start(f32[108,128]{1,0:T(8,128)S(1)} %reshape.7.link_ref.link_a), channel_id=1, source_target_pairs={{0,2},{1,3},{2,0},{3,1},{4,6},{5,7},{6,4},{7,5},{8,10},{9,11},{10,... | collective-permute-start | bytes 165896 | tf_op jit(solution)/shard_map/ppermute | solution.py:339
  12.3 3.0 %collective-permute-done.2.vb_ref.before_ref = f32[2,3,64,256]{3,2,1,0:T(8,128)S(1)} collective-permute-done((f32[2,3,64,256]{3,2,1,0:T(8,128)S(1)}, f32[2,3,64,256]{3,2,1,0:T(8,128)S(1)}, u32[]{:S(2)}, u32[]{:S(2)}) %collective-permute-start.2) | collective-permute-done | bytes 393248 | tf_op jit(solution)/shard_map/ppermute | solution.py:339
  15.2 4.1 %collective-permute-start.6 = (f32[108,128]{1,0:T(8,128)S(1)}, f32[108,128]{1,0:T(8,128)S(1)}, u32[]{:S(2)}, u32[]{:S(2)}) collective-permute-start(f32[108,128]{1,0:T(8,128)S(1)} %reshape.7.link_ref.link_a), channel_id=1, source_target_pairs={{0,12},{1,13},{2,6},{3,7},{4,0},{5,1},{6,10},{7,11},{8,4},{9,5},{1... | collective-permute-start | bytes 165896 | tf_op jit(solution)/shard_map/ppermute | solution.py:339
  19.3 2.9 %shard_map.78.own_ref = f32[2,256,256]{2,1,0:T(8,128)S(1)} custom-call(s32[1]{0:T(128)} %bitcast.place_ref, f32[2,3,64,256]{3,2,1,0:T(8,128)S(1)} %get-tuple-element.26.v0_ref.va_ref, f32[2,3,64,256]{3,2,1,0:T(8,128)S(1)} %get-tuple-element.28.v1_ref.va_ref, f32[2,3,16,256]{3,2,1,0:T(8,128)S(1)} %collective-permute-done.7.halo_ref, ...), custom_call_target="tpu_custom_call" | custom-call | flops 1207959552 | bytes 1464324 | tf_op jit(solution)/shard_map/pallas_call | solution.py:315
  22.3 1.8 %collective-permute-done.5.link_b = f32[108,128]{1,0:T(8,128)S(1)} collective-permute-done((f32[108,128]{1,0:T(8,128)S(1)}, f32[108,128]{1,0:T(8,128)S(1)}, u32[]{:S(2)}, u32[]{:S(2)}) %collective-permute-start.5) | collective-permute-done | bytes 55328 | tf_op jit(solution)/shard_map/ppermute | solution.py:339
  24.0 2.6 %collective-permute-done.6.link_c = f32[108,128]{1,0:T(8,128)S(1)} collective-permute-done((f32[108,128]{1,0:T(8,128)S(1)}, f32[108,128]{1,0:T(8,128)S(1)}, u32[]{:S(2)}, u32[]{:S(2)}) %collective-permute-start.6) | collective-permute-done | bytes 55328 | tf_op jit(solution)/shard_map/ppermute | solution.py:339
  26.6 2.5 %shard_map.79 = (f32[768,256]{1,0:T(8,128)S(1)}, f32[128,128]{1,0:T(8,128)S(1)}) custom-call(s32[1]{0:T(128)} %bitcast.place_ref, f32[2,3,64,256]{3,2,1,0:T(8,128)S(1)} %get-tuple-element.26.v0_ref.va_ref, f32[2,3,64,256]{3,2,1,0:T(8,128)S(1)} %collective-permute-done.2.vb_ref.before_ref, f32[2,3,64,256]{3,2,1,0:T(8,128)S(1)} %collective-permute-done.4.vc_ref, ...), custom_call_target="tpu_custom_call" | custom-call | flops 1207959552 | bytes 2721796 | tf_op jit(solution)/shard_map/pallas_call | solution.py:315
  29.2 2.6 %shard_map.80 = (f32[384,256]{1,0:T(8,128)S(1)}, f32[384,256]{1,0:T(8,128)S(1)}) custom-call(s32[1]{0:T(128)} %bitcast.place_ref, f32[2,3,64,256]{3,2,1,0:T(8,128)S(1)} %get-tuple-element.28.v1_ref.va_ref, f32[2,3,64,256]{3,2,1,0:T(8,128)S(1)} %collective-permute-done.vb_ref, f32[2,3,64,256]{3,2,1,0:T(8,128)S(1)} %collective-permute-done.1.vc_ref, ...), custom_call_target="tpu_custom_call" | custom-call | flops 1207959552 | bytes 3309572 | tf_op jit(solution)/shard_map/pallas_call | solution.py:315
  31.9 1.7 %collective-permute-done.8.got_ref = f32[384,256]{1,0:T(8,128)S(1)} collective-permute-done((f32[384,256]{1,0:T(8,128)S(1)}, f32[384,256]{1,0:T(8,128)S(1)}, u32[]{:S(2)}, u32[]{:S(2)}) %collective-permute-start.8) | collective-permute-done | bytes 393248 | tf_op jit(solution)/shard_map/ppermute | solution.py:339
  33.7 1.5 %collective-permute-start.10 = (f32[96,256]{1,0:T(8,128)S(1)}, f32[96,256]{1,0:T(8,128)S(1)}, u32[]{:S(2)}, u32[]{:S(2)}) collective-permute-start(f32[96,256]{1,0:T(8,128)S(1)} %get-tuple-element.24), channel_id=1, source_target_pairs={{0,8},{1,9},{2,10},{3,11},{4,12},{5,13},{6,14},{7,15},{8,0},{9,1},... | collective-permute-start | bytes 294920 | tf_op jit(solution)/shard_map/ppermute | solution.py:339
  35.2 2.9 %collective-permute-start.11 = (f32[96,256]{1,0:T(8,128)S(1)}, f32[96,256]{1,0:T(8,128)S(1)}, u32[]{:S(2)}, u32[]{:S(2)}) collective-permute-start(f32[96,256]{1,0:T(8,128)S(1)} %get-tuple-element.25), channel_id=1, source_target_pairs={{0,12},{1,13},{2,14},{3,15},{4,0},{5,1},{6,2},{7,3},{8,4},{9,5},{1... | collective-permute-start | bytes 294920 | tf_op jit(solution)/shard_map/ppermute | solution.py:339
  38.6 3.4 %collective-permute-done.10.refs_2_ = f32[96,256]{1,0:T(8,128)S(1)} collective-permute-done((f32[96,256]{1,0:T(8,128)S(1)}, f32[96,256]{1,0:T(8,128)S(1)}, u32[]{:S(2)}, u32[]{:S(2)}) %collective-permute-start.10) | collective-permute-done | bytes 98336 | tf_op jit(solution)/shard_map/ppermute | solution.py:339
  42.0 3.5 %collective-permute-done.9.refs_1_ = f32[96,256]{1,0:T(8,128)S(1)} collective-permute-done((f32[96,256]{1,0:T(8,128)S(1)}, f32[96,256]{1,0:T(8,128)S(1)}, u32[]{:S(2)}, u32[]{:S(2)}) %collective-permute-start.9) | collective-permute-done | bytes 98336 | tf_op jit(solution)/shard_map/ppermute | solution.py:339
  46.5 2.4 %collective-permute-start.13 = (f32[96,256]{1,0:T(8,128)S(1)}, f32[96,256]{1,0:T(8,128)S(1)}, u32[]{:S(2)}, u32[]{:S(2)}) collective-permute-start(f32[96,256]{1,0:T(8,128)S(1)} %shard_map.82.refs_0_), channel_id=1, source_target_pairs={{0,8},{1,9},{2,10},{3,11},{4,12},{5,13},{6,14},{7,15},{8,0},{9,1},... | collective-permute-start | bytes 294920 | tf_op jit(solution)/shard_map/ppermute | solution.py:339
  48.8 1.5 %collective-permute-start.14 = (f32[96,256]{1,0:T(8,128)S(1)}, f32[96,256]{1,0:T(8,128)S(1)}, u32[]{:S(2)}, u32[]{:S(2)}) collective-permute-start(f32[96,256]{1,0:T(8,128)S(1)} %shard_map.82.refs_0_), channel_id=1, source_target_pairs={{0,12},{1,13},{2,14},{3,15},{4,0},{5,1},{6,2},{7,3},{8,4},{9,5},{1... | collective-permute-start | bytes 294920 | tf_op jit(solution)/shard_map/ppermute | solution.py:339
  51.0 2.1 %collective-permute-done.12.refs_1_ = f32[96,256]{1,0:T(8,128)S(1)} collective-permute-done((f32[96,256]{1,0:T(8,128)S(1)}, f32[96,256]{1,0:T(8,128)S(1)}, u32[]{:S(2)}, u32[]{:S(2)}) %collective-permute-start.12) | collective-permute-done | bytes 98336 | tf_op jit(solution)/shard_map/ppermute | solution.py:339
  53.1 2.7 %collective-permute-done.13.refs_2_ = f32[96,256]{1,0:T(8,128)S(1)} collective-permute-done((f32[96,256]{1,0:T(8,128)S(1)}, f32[96,256]{1,0:T(8,128)S(1)}, u32[]{:S(2)}, u32[]{:S(2)}) %collective-permute-start.13) | collective-permute-done | bytes 98336 | tf_op jit(solution)/shard_map/ppermute | solution.py:339
  56.0 1.9 %collective-permute-start.18 = (f32[96,256]{1,0:T(8,128)S(1)}, f32[96,256]{1,0:T(8,128)S(1)}, u32[]{:S(2)}, u32[]{:S(2)}) collective-permute-start(f32[96,256]{1,0:T(8,128)S(1)} %collective-permute-done.14.refs_3_), channel_id=1, source_target_pairs={{0,2},{1,3},{2,0},{3,1},{4,6},{5,7},{6,4},{7,5},{8,10},{9,11},{10,... | collective-permute-start | bytes 294920 | tf_op jit(solution)/shard_map/ppermute | solution.py:339
  58.5 2.9 %collective-permute-done.17.refs_6_ = f32[96,256]{1,0:T(8,128)S(1)} collective-permute-done((f32[96,256]{1,0:T(8,128)S(1)}, f32[96,256]{1,0:T(8,128)S(1)}, u32[]{:S(2)}, u32[]{:S(2)}) %collective-permute-start.17) | collective-permute-done | bytes 98336 | tf_op jit(solution)/shard_map/ppermute | solution.py:339
  64.3 3.4 %shard_map.83 = (f32[2,3,2,16,256]{4,3,2,1,0:T(8,128)}, f32[2,64,64]{2,1,0:T(8,128)}) custom-call(s32[1]{0:T(128)} %bitcast.place_ref, s32[3]{0:T(128)S(1)} %copy-done.1, s32[2]{0:T(128)S(1)} %copy-done.2, s32[1]{0:T(128)S(6)} %copy.8.block_ref, bf16[256,1536]{1,0:T(8,128)(2,1)S(1)} %get-tuple-element.14.b_high, ...), custom_call_target="tpu_custom_call" | custom-call | flops 150994944 | bytes 3637276 | tf_op jit(solution)/shard_map/pallas_call | solution.py:315
  (49 shorter events, 5.8 us)
Async XLA Ops:
  2.2 13.0 %collective-permute-start.2 = (f32[2,3,64,256]{3,2,1,0:T(8,128)S(1)}, f32[2,3,64,256]{3,2,1,0:T(8,128)S(1)}, u32[]{:S(2)}, u32[]{:S(2)}) collective-permute-start(f32[2,3,64,256]{3,2,1,0:T(8,128)S(1)} %get-tuple-element.29), channel_id=1, source_target_pairs={{0,2},{1,3},{2,0},{3,1},{4,6},{5,7},{6,4},{7,5},{8,10},{9,11},{10,... | collective-permute-start | bytes 1179656 | tf_op jit(solution)/shard_map/ppermute | solution.py:339
  5.3 21.4 %collective-permute-start.4 = (f32[2,3,64,256]{3,2,1,0:T(8,128)S(1)}, f32[2,3,64,256]{3,2,1,0:T(8,128)S(1)}, u32[]{:S(2)}, u32[]{:S(2)}) collective-permute-start(f32[2,3,64,256]{3,2,1,0:T(8,128)S(1)} %get-tuple-element.26.v0_ref.va_ref), channel_id=1, source_target_pairs={{0,12},{1,13},{2,6},{3,7},{4,0},{5,1},{6,10},{7,11},{8,4},{9,5},{1... | collective-permute-start | bytes 1179656 | tf_op jit(solution)/shard_map/ppermute | solution.py:339
  8.9 20.3 %collective-permute-start = (f32[2,3,64,256]{3,2,1,0:T(8,128)S(1)}, f32[2,3,64,256]{3,2,1,0:T(8,128)S(1)}, u32[]{:S(2)}, u32[]{:S(2)}) collective-permute-start(f32[2,3,64,256]{3,2,1,0:T(8,128)S(1)} %get-tuple-element.27), channel_id=1, source_target_pairs={{0,2},{1,3},{2,0},{3,1},{4,6},{5,7},{6,4},{7,5},{8,10},{9,11},{10,... | collective-permute-start | bytes 1179656 | tf_op jit(solution)/shard_map/ppermute | solution.py:339
  8.9 20.3 %collective-permute-start.1 = (f32[2,3,64,256]{3,2,1,0:T(8,128)S(1)}, f32[2,3,64,256]{3,2,1,0:T(8,128)S(1)}, u32[]{:S(2)}, u32[]{:S(2)}) collective-permute-start(f32[2,3,64,256]{3,2,1,0:T(8,128)S(1)} %get-tuple-element.28.v1_ref.va_ref), channel_id=1, source_target_pairs={{0,12},{1,13},{2,6},{3,7},{4,0},{5,1},{6,10},{7,11},{8,4},{9,5},{1... | collective-permute-start | bytes 1179656 | tf_op jit(solution)/shard_map/ppermute | solution.py:339
  10.7 13.3 %collective-permute-start.5 = (f32[108,128]{1,0:T(8,128)S(1)}, f32[108,128]{1,0:T(8,128)S(1)}, u32[]{:S(2)}, u32[]{:S(2)}) collective-permute-start(f32[108,128]{1,0:T(8,128)S(1)} %reshape.7.link_ref.link_a), channel_id=1, source_target_pairs={{0,2},{1,3},{2,0},{3,1},{4,6},{5,7},{6,4},{7,5},{8,10},{9,11},{10,... | collective-permute-start | bytes 165896 | tf_op jit(solution)/shard_map/ppermute | solution.py:339
  15.2 11.4 %collective-permute-start.6 = (f32[108,128]{1,0:T(8,128)S(1)}, f32[108,128]{1,0:T(8,128)S(1)}, u32[]{:S(2)}, u32[]{:S(2)}) collective-permute-start(f32[108,128]{1,0:T(8,128)S(1)} %reshape.7.link_ref.link_a), channel_id=1, source_target_pairs={{0,12},{1,13},{2,6},{3,7},{4,0},{5,1},{6,10},{7,11},{8,4},{9,5},{1... | collective-permute-start | bytes 165896 | tf_op jit(solution)/shard_map/ppermute | solution.py:339
  24.0 5.1 %collective-permute-start.3 = (f32[2,3,16,256]{3,2,1,0:T(8,128)S(1)}, f32[2,3,16,256]{3,2,1,0:T(8,128)S(1)}, u32[]{:S(2)}, u32[]{:S(2)}) collective-permute-start(f32[2,3,16,256]{3,2,1,0:T(8,128)S(1)} %slice.8), channel_id=1, source_target_pairs={{0,1},{1,0},{2,3},{3,2},{4,5},{5,4},{6,7},{7,6},{8,9},{9,8},{10,11... | collective-permute-start | bytes 294920 | tf_op jit(solution)/shard_map/ppermute | solution.py:339
  31.8 1.8 %collective-permute-start.8 = (f32[384,256]{1,0:T(8,128)S(1)}, f32[384,256]{1,0:T(8,128)S(1)}, u32[]{:S(2)}, u32[]{:S(2)}) collective-permute-start(f32[384,256]{1,0:T(8,128)S(1)} %get-tuple-element.21), channel_id=1, source_target_pairs={{0,1},{1,0},{2,3},{3,2},{4,5},{5,4},{6,7},{7,6},{8,9},{9,8},{10,11... | collective-permute-start | bytes 1179656 | tf_op jit(solution)/shard_map/ppermute | solution.py:339
  33.7 8.3 %collective-permute-start.10 = (f32[96,256]{1,0:T(8,128)S(1)}, f32[96,256]{1,0:T(8,128)S(1)}, u32[]{:S(2)}, u32[]{:S(2)}) collective-permute-start(f32[96,256]{1,0:T(8,128)S(1)} %get-tuple-element.24), channel_id=1, source_target_pairs={{0,8},{1,9},{2,10},{3,11},{4,12},{5,13},{6,14},{7,15},{8,0},{9,1},... | collective-permute-start | bytes 294920 | tf_op jit(solution)/shard_map/ppermute | solution.py:339
  35.2 6.7 %collective-permute-start.11 = (f32[96,256]{1,0:T(8,128)S(1)}, f32[96,256]{1,0:T(8,128)S(1)}, u32[]{:S(2)}, u32[]{:S(2)}) collective-permute-start(f32[96,256]{1,0:T(8,128)S(1)} %get-tuple-element.25), channel_id=1, source_target_pairs={{0,12},{1,13},{2,14},{3,15},{4,0},{5,1},{6,2},{7,3},{8,4},{9,5},{1... | collective-permute-start | bytes 294920 | tf_op jit(solution)/shard_map/ppermute | solution.py:339
  38.1 7.4 %collective-permute-start.9 = (f32[96,256]{1,0:T(8,128)S(1)}, f32[96,256]{1,0:T(8,128)S(1)}, u32[]{:S(2)}, u32[]{:S(2)}) collective-permute-start(f32[96,256]{1,0:T(8,128)S(1)} %get-tuple-element.23), channel_id=1, source_target_pairs={{0,4},{1,5},{2,6},{3,7},{4,8},{5,9},{6,10},{7,11},{8,12},{9,13},{1... | collective-permute-start | bytes 294920 | tf_op jit(solution)/shard_map/ppermute | solution.py:339
  45.5 7.6 %collective-permute-start.12 = (f32[96,256]{1,0:T(8,128)S(1)}, f32[96,256]{1,0:T(8,128)S(1)}, u32[]{:S(2)}, u32[]{:S(2)}) collective-permute-start(f32[96,256]{1,0:T(8,128)S(1)} %shard_map.82.refs_0_), channel_id=1, source_target_pairs={{0,4},{1,5},{2,6},{3,7},{4,8},{5,9},{6,10},{7,11},{8,12},{9,13},{1... | collective-permute-start | bytes 294920 | tf_op jit(solution)/shard_map/ppermute | solution.py:339
  46.5 9.4 %collective-permute-start.13 = (f32[96,256]{1,0:T(8,128)S(1)}, f32[96,256]{1,0:T(8,128)S(1)}, u32[]{:S(2)}, u32[]{:S(2)}) collective-permute-start(f32[96,256]{1,0:T(8,128)S(1)} %shard_map.82.refs_0_), channel_id=1, source_target_pairs={{0,8},{1,9},{2,10},{3,11},{4,12},{5,13},{6,14},{7,15},{8,0},{9,1},... | collective-permute-start | bytes 294920 | tf_op jit(solution)/shard_map/ppermute | solution.py:339
  48.8 7.2 %collective-permute-start.14 = (f32[96,256]{1,0:T(8,128)S(1)}, f32[96,256]{1,0:T(8,128)S(1)}, u32[]{:S(2)}, u32[]{:S(2)}) collective-permute-start(f32[96,256]{1,0:T(8,128)S(1)} %shard_map.82.refs_0_), channel_id=1, source_target_pairs={{0,12},{1,13},{2,14},{3,15},{4,0},{5,1},{6,2},{7,3},{8,4},{9,5},{1... | collective-permute-start | bytes 294920 | tf_op jit(solution)/shard_map/ppermute | solution.py:339
  50.3 7.6 %collective-permute-start.15 = (f32[96,256]{1,0:T(8,128)S(1)}, f32[96,256]{1,0:T(8,128)S(1)}, u32[]{:S(2)}, u32[]{:S(2)}) collective-permute-start(f32[96,256]{1,0:T(8,128)S(1)} %shard_map.82.refs_0_), channel_id=1, source_target_pairs={{0,2},{1,3},{2,0},{3,1},{4,6},{5,7},{6,4},{7,5},{8,10},{9,11},{10,... | collective-permute-start | bytes 294920 | tf_op jit(solution)/shard_map/ppermute | solution.py:339
  51.0 6.9 %collective-permute-start.19 = (f32[96,256]{1,0:T(8,128)S(1)}, f32[96,256]{1,0:T(8,128)S(1)}, u32[]{:S(2)}, u32[]{:S(2)}) collective-permute-start(f32[96,256]{1,0:T(8,128)S(1)} %shard_map.82.refs_0_), channel_id=1, source_target_pairs={{0,1},{1,0},{2,3},{3,2},{4,5},{5,4},{6,7},{7,6},{8,9},{9,8},{10,11... | collective-permute-start | bytes 294920 | tf_op jit(solution)/shard_map/ppermute | solution.py:339
  53.1 5.3 %collective-permute-start.16 = (f32[96,256]{1,0:T(8,128)S(1)}, f32[96,256]{1,0:T(8,128)S(1)}, u32[]{:S(2)}, u32[]{:S(2)}) collective-permute-start(f32[96,256]{1,0:T(8,128)S(1)} %collective-permute-done.12.refs_1_), channel_id=1, source_target_pairs={{0,2},{1,3},{2,0},{3,1},{4,6},{5,7},{6,4},{7,5},{8,10},{9,11},{10,... | collective-permute-start | bytes 294920 | tf_op jit(solution)/shard_map/ppermute | solution.py:339
  55.9 5.6 %collective-permute-start.17 = (f32[96,256]{1,0:T(8,128)S(1)}, f32[96,256]{1,0:T(8,128)S(1)}, u32[]{:S(2)}, u32[]{:S(2)}) collective-permute-start(f32[96,256]{1,0:T(8,128)S(1)} %collective-permute-done.13.refs_2_), channel_id=1, source_target_pairs={{0,2},{1,3},{2,0},{3,1},{4,6},{5,7},{6,4},{7,5},{8,10},{9,11},{10,... | collective-permute-start | bytes 294920 | tf_op jit(solution)/shard_map/ppermute | solution.py:339
  56.0 6.5 %collective-permute-start.18 = (f32[96,256]{1,0:T(8,128)S(1)}, f32[96,256]{1,0:T(8,128)S(1)}, u32[]{:S(2)}, u32[]{:S(2)}) collective-permute-start(f32[96,256]{1,0:T(8,128)S(1)} %collective-permute-done.14.refs_3_), channel_id=1, source_target_pairs={{0,2},{1,3},{2,0},{3,1},{4,6},{5,7},{6,4},{7,5},{8,10},{9,11},{10,... | collective-permute-start | bytes 294920 | tf_op jit(solution)/shard_map/ppermute | solution.py:339
  57.9 4.6 %collective-permute-start.20 = (f32[96,256]{1,0:T(8,128)S(1)}, f32[96,256]{1,0:T(8,128)S(1)}, u32[]{:S(2)}, u32[]{:S(2)}) collective-permute-start(f32[96,256]{1,0:T(8,128)S(1)} %collective-permute-done.12.refs_1_), channel_id=1, source_target_pairs={{0,1},{1,0},{2,3},{3,2},{4,5},{5,4},{6,7},{7,6},{8,9},{9,8},{10,11... | collective-permute-start | bytes 294920 | tf_op jit(solution)/shard_map/ppermute | solution.py:339
  57.9 5.1 %collective-permute-start.21 = (f32[96,256]{1,0:T(8,128)S(1)}, f32[96,256]{1,0:T(8,128)S(1)}, u32[]{:S(2)}, u32[]{:S(2)}) collective-permute-start(f32[96,256]{1,0:T(8,128)S(1)} %collective-permute-done.13.refs_2_), channel_id=1, source_target_pairs={{0,1},{1,0},{2,3},{3,2},{4,5},{5,4},{6,7},{7,6},{8,9},{9,8},{10,11... | collective-permute-start | bytes 294920 | tf_op jit(solution)/shard_map/ppermute | solution.py:339
  58.4 5.5 %collective-permute-start.22 = (f32[96,256]{1,0:T(8,128)S(1)}, f32[96,256]{1,0:T(8,128)S(1)}, u32[]{:S(2)}, u32[]{:S(2)}) collective-permute-start(f32[96,256]{1,0:T(8,128)S(1)} %collective-permute-done.14.refs_3_), channel_id=1, source_target_pairs={{0,1},{1,0},{2,3},{3,2},{4,5},{5,4},{6,7},{7,6},{8,9},{9,8},{10,11... | collective-permute-start | bytes 294920 | tf_op jit(solution)/shard_map/ppermute | solution.py:339
  61.4 2.5 %collective-permute-start.23 = (f32[96,256]{1,0:T(8,128)S(1)}, f32[96,256]{1,0:T(8,128)S(1)}, u32[]{:S(2)}, u32[]{:S(2)}) collective-permute-start(f32[96,256]{1,0:T(8,128)S(1)} %collective-permute-done.15.refs_4_), channel_id=1, source_target_pairs={{0,1},{1,0},{2,3},{3,2},{4,5},{5,4},{6,7},{7,6},{8,9},{9,8},{10,11... | collective-permute-start | bytes 294920 | tf_op jit(solution)/shard_map/ppermute | solution.py:339
  62.5 1.5 %collective-permute-start.25 = (f32[96,256]{1,0:T(8,128)S(1)}, f32[96,256]{1,0:T(8,128)S(1)}, u32[]{:S(2)}, u32[]{:S(2)}) collective-permute-start(f32[96,256]{1,0:T(8,128)S(1)} %collective-permute-done.17.refs_6_), channel_id=1, source_target_pairs={{0,1},{1,0},{2,3},{3,2},{4,5},{5,4},{6,7},{7,6},{8,9},{9,8},{10,11... | collective-permute-start | bytes 294920 | tf_op jit(solution)/shard_map/ppermute | solution.py:339
  (7 other events, 109.2 us)

commit v3 on v2

--- a/solution.py
+++ b/solution.py
@@ -185,6 +185,12 @@
     send_ref[...] = total_ref[pl.ds(pl.multiple_of((1 - core) * half, 8), half), :]
 
 
+def part_row(pair, d, count, size):
+    if count == 4:
+        return (((pair % 2) ^ (d // 2)) * 2 + d % 2) * size
+    return lax.rem(pair + count - d, count) * size
+
+
 def spread_kernel(place_ref, keep_ref, got_ref, *refs):
     outs, total_ref = refs[:-1], refs[-1]
     total_ref[...] = keep_ref[...] + got_ref[...]
@@ -192,7 +198,7 @@
     size = outs[0].shape[0]
     pair = place_ref[0] // 4
     for d in range(count):
-        at = lax.rem(pair + d, count) * size
+        at = part_row(pair, d if count == 4 else -d, count, size)
         outs[d][...] = total_ref[pl.ds(pl.multiple_of(at, 8), size), :]
 
 
@@ -261,7 +267,7 @@
             for d in range(count):
                 time = (odd + other) % 2
                 base = (time * 2 + (core + side) % 2) * half
-                at = base + lax.rem(pair - d + count, count) * size
+                at = base + part_row(pair, d, count, size)
                 piece = pieces[(side * 2 + other) * count + d]
                 all_ref[pl.ds(pl.multiple_of(at, 8), size), :] = piece[...]
     rows = elem_ref.shape[3]
@@ -395,9 +401,23 @@
     size = half // pairs
     spread = call(spread_kernel, (shape(size, width),) * pairs, (places, keep, got), scalars=1,
                   scratch=(pltpu.VMEM((half, width), jnp.float32),))
-    parts = [spread[0]] + [send(spread[d], shift(d)) for d in range(1, pairs)]
-    shard = call(sum_kernel, shape(size, width), parts)
-    here = [shard] + [send(shard, shift(d)) for d in range(1, pairs)]
+
+    def plus(*values):
+        return call(sum_kernel, shape(size, width), values)
+
+    if pairs == 4:
+        near = lambda pair, o, core: (pair ^ 1, o, core)
+        far = lambda pair, o, core: (pair ^ 2, o, core)
+        got = [send(spread[2 + i], near) for i in range(2)]
+        sums = [plus(spread[i], got[i]) for i in range(2)]
+        got = [send(sums[i], far) for i in range(2)]
+        done = [plus(sums[i], got[i]) for i in range(2)]
+        rest = [send(done[i], near) for i in range(2)]
+        here = done + rest
+    else:
+        parts = [spread[0]] + [send(spread[d], shift(d)) for d in range(1, pairs)]
+        shard = plus(*parts)
+        here = [shard] + [send(shard, shift(d)) for d in range(1, pairs)]
     there = [send(x, partner) for x in here]
     pieces = here + there
     pieces = pieces + [send(x, twin) for x in pieces]

time: 67.9 us -> 67 us (0.987)
  waiting for transfers between devices: 26.5 us -> 24.7 us
    ppermute x27, waiting for transfers between devices: 26.5 us -> 24.7 us  [send(): return lax.ppermute(value, 'space', route)]
    pallas_call x7 -> x10, Pallas kernels: 11.7 us -> 11.7 us  [call(): pl.pallas_call(kernel, out_shape=out, in_specs=[SMEM] * scalars + [VMEM]...]
  transfers between devices with their start and end apart: 27 -> 27, of which waited for: 13 -> 15; matrix products, arithmetic and copies ran while one was open for 0% -> 0% of each run, Pallas kernels for 8% -> 9%
where the time goes in v3:
time: 67 us; the launch traced here: 66.2 us
  starting transfers between devices  26.6 us (40%)
  waiting for transfers between devices  24.7 us (37%)
  Pallas kernels  11.7 us (17%)
  local copies, waits for them, and re-layouts  1.59 us (2%)
  between operations  1.52 us (2%)
    ppermute x27, starting transfers between devices, send(): return lax.ppermute(value, 'space', route)  26.6 us
    ppermute x27, waiting for transfers between devices, send(): return lax.ppermute(value, 'space', route)  24.7 us
    pallas_call x10, Pallas kernels, call(): pl.pallas_call(kernel, out_shape=out, in_specs=[SMEM] * scalars + [VMEM]...  11.7 us
    squeeze x1, local copies, waits for them, and re-layouts, cut(): return lax.dynamic_slice(vectors, (time, 0, 0, i * part, 0), block)[0]  1.51 us
  transfers between devices with their start and end apart: 27, of which 15 were waited for; matrix products, arithmetic and copies ran while one was open for 0% of the time, Pallas kernels for 9%

profile of v3, /device:TPU:0, one launch (start us, length us, event | category | flops | bytes accessed | tf_op | source)
XLA Modules:
  0.0 66.2 jit_solution(8893344038998522835)
XLA Ops:
  0.7 1.5 %dynamic-slice_bitcast_fusion = (f32[2,3,64,256]{3,2,1,0:T(8,128)S(1)}, f32[2,3,64,256]{3,2,1,0:T(8,128)S(1)}, f32[2,3,64,256]{3,2,1,0:T(8,128)S(1)}, f32[2,3,64,256]{3,2,1,0:T(8,128)S(1)}) fusion(f32[2,2,3,128,256]{4,3,2,1,0:T(8,128)} %param.6, s32[]{:T(128)S(6)} %select_n.21, s32[]{:T(128)S(6)} %select_n.22), kind=kLoop, calls=%fused_computation | loop fusion | bytes 3145736 | tf_op jit(solution)/shard_map/squeeze | solution.py:359
  2.2 3.1 %collective-permute-start.2 = (f32[2,3,64,256]{3,2,1,0:T(8,128)S(1)}, f32[2,3,64,256]{3,2,1,0:T(8,128)S(1)}, u32[]{:S(2)}, u32[]{:S(2)}) collective-permute-start(f32[2,3,64,256]{3,2,1,0:T(8,128)S(1)} %get-tuple-element.29), channel_id=1, source_target_pairs={{0,2},{1,3},{2,0},{3,1},{4,6},{5,7},{6,4},{7,5},{8,10},{9,11},{10,... | collective-permute-start | bytes 1179656 | tf_op jit(solution)/shard_map/ppermute | solution.py:345
  5.3 3.6 %collective-permute-start.4 = (f32[2,3,64,256]{3,2,1,0:T(8,128)S(1)}, f32[2,3,64,256]{3,2,1,0:T(8,128)S(1)}, u32[]{:S(2)}, u32[]{:S(2)}) collective-permute-start(f32[2,3,64,256]{3,2,1,0:T(8,128)S(1)} %get-tuple-element.26.v0_ref.va_ref), channel_id=1, source_target_pairs={{0,12},{1,13},{2,6},{3,7},{4,0},{5,1},{6,10},{7,11},{8,4},{9,5},{1... | collective-permute-start | bytes 1179656 | tf_op jit(solution)/shard_map/ppermute | solution.py:345
  9.5 1.2 %collective-permute-done.7.halo_ref = f32[2,3,16,256]{3,2,1,0:T(8,128)S(1)} collective-permute-done((f32[2,3,16,256]{3,2,1,0:T(8,128)S(1)}, f32[2,3,16,256]{3,2,1,0:T(8,128)S(1)}, u32[]{:S(2)}, u32[]{:S(2)}) %collective-permute-start.7) | collective-permute-done | bytes 98336 | tf_op jit(solution)/shard_map/ppermute | solution.py:345
  10.7 1.5 %collective-permute-start.5 = (f32[108,128]{1,0:T(8,128)S(1)}, f32[108,128]{1,0:T(8,128)S(1)}, u32[]{:S(2)}, u32[]{:S(2)}) collective-permute-start(f32[108,128]{1,0:T(8,128)S(1)} %reshape.7.link_ref.link_a), channel_id=1, source_target_pairs={{0,2},{1,3},{2,0},{3,1},{4,6},{5,7},{6,4},{7,5},{8,10},{9,11},{10,... | collective-permute-start | bytes 165896 | tf_op jit(solution)/shard_map/ppermute | solution.py:345
  12.3 3.0 %collective-permute-done.2.vb_ref.before_ref = f32[2,3,64,256]{3,2,1,0:T(8,128)S(1)} collective-permute-done((f32[2,3,64,256]{3,2,1,0:T(8,128)S(1)}, f32[2,3,64,256]{3,2,1,0:T(8,128)S(1)}, u32[]{:S(2)}, u32[]{:S(2)}) %collective-permute-start.2) | collective-permute-done | bytes 393248 | tf_op jit(solution)/shard_map/ppermute | solution.py:345
  15.2 4.1 %collective-permute-start.6 = (f32[108,128]{1,0:T(8,128)S(1)}, f32[108,128]{1,0:T(8,128)S(1)}, u32[]{:S(2)}, u32[]{:S(2)}) collective-permute-start(f32[108,128]{1,0:T(8,128)S(1)} %reshape.7.link_ref.link_a), channel_id=1, source_target_pairs={{0,12},{1,13},{2,6},{3,7},{4,0},{5,1},{6,10},{7,11},{8,4},{9,5},{1... | collective-permute-start | bytes 165896 | tf_op jit(solution)/shard_map/ppermute | solution.py:345
  19.3 2.9 %shard_map.78.own_ref = f32[2,256,256]{2,1,0:T(8,128)S(1)} custom-call(s32[1]{0:T(128)} %bitcast.place_ref, f32[2,3,64,256]{3,2,1,0:T(8,128)S(1)} %get-tuple-element.26.v0_ref.va_ref, f32[2,3,64,256]{3,2,1,0:T(8,128)S(1)} %get-tuple-element.28.v1_ref.va_ref, f32[2,3,16,256]{3,2,1,0:T(8,128)S(1)} %collective-permute-done.7.halo_ref, ...), custom_call_target="tpu_custom_call" | custom-call | flops 1207959552 | bytes 1464324 | tf_op jit(solution)/shard_map/pallas_call | solution.py:321
  22.3 1.8 %collective-permute-done.5.link_b = f32[108,128]{1,0:T(8,128)S(1)} collective-permute-done((f32[108,128]{1,0:T(8,128)S(1)}, f32[108,128]{1,0:T(8,128)S(1)}, u32[]{:S(2)}, u32[]{:S(2)}) %collective-permute-start.5) | collective-permute-done | bytes 55328 | tf_op jit(solution)/shard_map/ppermute | solution.py:345
  24.0 2.6 %collective-permute-done.6.link_c = f32[108,128]{1,0:T(8,128)S(1)} collective-permute-done((f32[108,128]{1,0:T(8,128)S(1)}, f32[108,128]{1,0:T(8,128)S(1)}, u32[]{:S(2)}, u32[]{:S(2)}) %collective-permute-start.6) | collective-permute-done | bytes 55328 | tf_op jit(solution)/shard_map/ppermute | solution.py:345
  26.6 2.5 %shard_map.79 = (f32[768,256]{1,0:T(8,128)S(1)}, f32[128,128]{1,0:T(8,128)S(1)}) custom-call(s32[1]{0:T(128)} %bitcast.place_ref, f32[2,3,64,256]{3,2,1,0:T(8,128)S(1)} %get-tuple-element.26.v0_ref.va_ref, f32[2,3,64,256]{3,2,1,0:T(8,128)S(1)} %collective-permute-done.2.vb_ref.before_ref, f32[2,3,64,256]{3,2,1,0:T(8,128)S(1)} %collective-permute-done.4.vc_ref, ...), custom_call_target="tpu_custom_call" | custom-call | flops 1207959552 | bytes 2721796 | tf_op jit(solution)/shard_map/pallas_call | solution.py:321
  29.2 2.6 %shard_map.80 = (f32[384,256]{1,0:T(8,128)S(1)}, f32[384,256]{1,0:T(8,128)S(1)}) custom-call(s32[1]{0:T(128)} %bitcast.place_ref, f32[2,3,64,256]{3,2,1,0:T(8,128)S(1)} %get-tuple-element.28.v1_ref.va_ref, f32[2,3,64,256]{3,2,1,0:T(8,128)S(1)} %collective-permute-done.vb_ref, f32[2,3,64,256]{3,2,1,0:T(8,128)S(1)} %collective-permute-done.1.vc_ref, ...), custom_call_target="tpu_custom_call" | custom-call | flops 1207959552 | bytes 3309572 | tf_op jit(solution)/shard_map/pallas_call | solution.py:321
  31.9 1.7 %collective-permute-done.8.got_ref = f32[384,256]{1,0:T(8,128)S(1)} collective-permute-done((f32[384,256]{1,0:T(8,128)S(1)}, f32[384,256]{1,0:T(8,128)S(1)}, u32[]{:S(2)}, u32[]{:S(2)}) %collective-permute-start.8) | collective-permute-done | bytes 393248 | tf_op jit(solution)/shard_map/ppermute | solution.py:345
  34.2 1.6 %collective-permute-start.9 = (f32[96,256]{1,0:T(8,128)S(1)}, f32[96,256]{1,0:T(8,128)S(1)}, u32[]{:S(2)}, u32[]{:S(2)}) collective-permute-start(f32[96,256]{1,0:T(8,128)S(1)} %get-tuple-element.23), channel_id=1, source_target_pairs={{0,4},{1,5},{2,6},{3,7},{4,0},{5,1},{6,2},{7,3},{8,12},{9,13},{10,... | collective-permute-start | bytes 294920 | tf_op jit(solution)/shard_map/ppermute | solution.py:345
  35.8 3.6 %collective-permute-done.11.refs_1_ = f32[96,256]{1,0:T(8,128)S(1)} collective-permute-done((f32[96,256]{1,0:T(8,128)S(1)}, f32[96,256]{1,0:T(8,128)S(1)}, u32[]{:S(2)}, u32[]{:S(2)}) %collective-permute-start.11) | collective-permute-done | bytes 98336 | tf_op jit(solution)/shard_map/ppermute | solution.py:345
  39.4 2.9 %collective-permute-start.12 = (f32[96,256]{1,0:T(8,128)S(1)}, f32[96,256]{1,0:T(8,128)S(1)}, u32[]{:S(2)}, u32[]{:S(2)}) collective-permute-start(f32[96,256]{1,0:T(8,128)S(1)} %shard_map.84.refs_0_), channel_id=1, source_target_pairs={{0,8},{1,9},{2,10},{3,11},{4,12},{5,13},{6,14},{7,15},{8,0},{9,1},... | collective-permute-start | bytes 294920 | tf_op jit(solution)/shard_map/ppermute | solution.py:345
  42.3 1.7 %collective-permute-start.10 = (f32[96,256]{1,0:T(8,128)S(1)}, f32[96,256]{1,0:T(8,128)S(1)}, u32[]{:S(2)}, u32[]{:S(2)}) collective-permute-start(f32[96,256]{1,0:T(8,128)S(1)} %shard_map.82.refs_0_), channel_id=1, source_target_pairs={{0,8},{1,9},{2,10},{3,11},{4,12},{5,13},{6,14},{7,15},{8,0},{9,1},... | collective-permute-start | bytes 294920 | tf_op jit(solution)/shard_map/ppermute | solution.py:345
  44.0 4.1 %collective-permute-done.12.refs_1_ = f32[96,256]{1,0:T(8,128)S(1)} collective-permute-done((f32[96,256]{1,0:T(8,128)S(1)}, f32[96,256]{1,0:T(8,128)S(1)}, u32[]{:S(2)}, u32[]{:S(2)}) %collective-permute-start.12) | collective-permute-done | bytes 98336 | tf_op jit(solution)/shard_map/ppermute | solution.py:345
  48.2 2.1 %collective-permute-start.14 = (f32[96,256]{1,0:T(8,128)S(1)}, f32[96,256]{1,0:T(8,128)S(1)}, u32[]{:S(2)}, u32[]{:S(2)}) collective-permute-start(f32[96,256]{1,0:T(8,128)S(1)} %shard_map.85.refs_1_), channel_id=1, source_target_pairs={{0,4},{1,5},{2,6},{3,7},{4,0},{5,1},{6,2},{7,3},{8,12},{9,13},{10,... | collective-permute-start | bytes 294920 | tf_op jit(solution)/shard_map/ppermute | solution.py:345
  50.6 1.6 %collective-permute-start.13 = (f32[96,256]{1,0:T(8,128)S(1)}, f32[96,256]{1,0:T(8,128)S(1)}, u32[]{:S(2)}, u32[]{:S(2)}) collective-permute-start(f32[96,256]{1,0:T(8,128)S(1)} %shard_map.83.refs_0_), channel_id=1, source_target_pairs={{0,4},{1,5},{2,6},{3,7},{4,0},{5,1},{6,2},{7,3},{8,12},{9,13},{10,... | collective-permute-start | bytes 294920 | tf_op jit(solution)/shard_map/ppermute | solution.py:345
  52.9 2.0 %collective-permute-done.16.refs_5_ = f32[96,256]{1,0:T(8,128)S(1)} collective-permute-done((f32[96,256]{1,0:T(8,128)S(1)}, f32[96,256]{1,0:T(8,128)S(1)}, u32[]{:S(2)}, u32[]{:S(2)}) %collective-permute-start.16) | collective-permute-done | bytes 98336 | tf_op jit(solution)/shard_map/ppermute | solution.py:345
  55.7 1.9 %collective-permute-start.17 = (f32[96,256]{1,0:T(8,128)S(1)}, f32[96,256]{1,0:T(8,128)S(1)}, u32[]{:S(2)}, u32[]{:S(2)}) collective-permute-start(f32[96,256]{1,0:T(8,128)S(1)} %collective-permute-done.13.refs_2_), channel_id=1, source_target_pairs={{0,2},{1,3},{2,0},{3,1},{4,6},{5,7},{6,4},{7,5},{8,10},{9,11},{10,... | collective-permute-start | bytes 294920 | tf_op jit(solution)/shard_map/ppermute | solution.py:345
  58.4 2.0 %collective-permute-done.18.refs_7_ = f32[96,256]{1,0:T(8,128)S(1)} collective-permute-done((f32[96,256]{1,0:T(8,128)S(1)}, f32[96,256]{1,0:T(8,128)S(1)}, u32[]{:S(2)}, u32[]{:S(2)}) %collective-permute-start.18) | collective-permute-done | bytes 98336 | tf_op jit(solution)/shard_map/ppermute | solution.py:345
  62.8 3.4 %shard_map.86 = (f32[2,3,2,16,256]{4,3,2,1,0:T(8,128)}, f32[2,64,64]{2,1,0:T(8,128)}) custom-call(s32[1]{0:T(128)} %bitcast.place_ref, s32[3]{0:T(128)S(1)} %copy-done.1, s32[2]{0:T(128)S(1)} %copy-done.2, s32[1]{0:T(128)S(6)} %copy.8.block_ref, bf16[256,1536]{1,0:T(8,128)(2,1)S(1)} %get-tuple-element.14.b_high, ...), custom_call_target="tpu_custom_call" | custom-call | flops 150994944 | bytes 3637276 | tf_op jit(solution)/shard_map/pallas_call | solution.py:321
  (52 shorter events, 5.6 us)
Async XLA Ops:
  2.2 13.0 %collective-permute-start.2 = (f32[2,3,64,256]{3,2,1,0:T(8,128)S(1)}, f32[2,3,64,256]{3,2,1,0:T(8,128)S(1)}, u32[]{:S(2)}, u32[]{:S(2)}) collective-permute-start(f32[2,3,64,256]{3,2,1,0:T(8,128)S(1)} %get-tuple-element.29), channel_id=1, source_target_pairs={{0,2},{1,3},{2,0},{3,1},{4,6},{5,7},{6,4},{7,5},{8,10},{9,11},{10,... | collective-permute-start | bytes 1179656 | tf_op jit(solution)/shard_map/ppermute | solution.py:345
  5.3 21.4 %collective-permute-start.4 = (f32[2,3,64,256]{3,2,1,0:T(8,128)S(1)}, f32[2,3,64,256]{3,2,1,0:T(8,128)S(1)}, u32[]{:S(2)}, u32[]{:S(2)}) collective-permute-start(f32[2,3,64,256]{3,2,1,0:T(8,128)S(1)} %get-tuple-element.26.v0_ref.va_ref), channel_id=1, source_target_pairs={{0,12},{1,13},{2,6},{3,7},{4,0},{5,1},{6,10},{7,11},{8,4},{9,5},{1... | collective-permute-start | bytes 1179656 | tf_op jit(solution)/shard_map/ppermute | solution.py:345
  8.9 20.3 %collective-permute-start = (f32[2,3,64,256]{3,2,1,0:T(8,128)S(1)}, f32[2,3,64,256]{3,2,1,0:T(8,128)S(1)}, u32[]{:S(2)}, u32[]{:S(2)}) collective-permute-start(f32[2,3,64,256]{3,2,1,0:T(8,128)S(1)} %get-tuple-element.27), channel_id=1, source_target_pairs={{0,2},{1,3},{2,0},{3,1},{4,6},{5,7},{6,4},{7,5},{8,10},{9,11},{10,... | collective-permute-start | bytes 1179656 | tf_op jit(solution)/shard_map/ppermute | solution.py:345
  8.9 20.3 %collective-permute-start.1 = (f32[2,3,64,256]{3,2,1,0:T(8,128)S(1)}, f32[2,3,64,256]{3,2,1,0:T(8,128)S(1)}, u32[]{:S(2)}, u32[]{:S(2)}) collective-permute-start(f32[2,3,64,256]{3,2,1,0:T(8,128)S(1)} %get-tuple-element.28.v1_ref.va_ref), channel_id=1, source_target_pairs={{0,12},{1,13},{2,6},{3,7},{4,0},{5,1},{6,10},{7,11},{8,4},{9,5},{1... | collective-permute-start | bytes 1179656 | tf_op jit(solution)/shard_map/ppermute | solution.py:345
  10.7 13.3 %collective-permute-start.5 = (f32[108,128]{1,0:T(8,128)S(1)}, f32[108,128]{1,0:T(8,128)S(1)}, u32[]{:S(2)}, u32[]{:S(2)}) collective-permute-start(f32[108,128]{1,0:T(8,128)S(1)} %reshape.7.link_ref.link_a), channel_id=1, source_target_pairs={{0,2},{1,3},{2,0},{3,1},{4,6},{5,7},{6,4},{7,5},{8,10},{9,11},{10,... | collective-permute-start | bytes 165896 | tf_op jit(solution)/shard_map/ppermute | solution.py:345
  15.2 11.4 %collective-permute-start.6 = (f32[108,128]{1,0:T(8,128)S(1)}, f32[108,128]{1,0:T(8,128)S(1)}, u32[]{:S(2)}, u32[]{:S(2)}) collective-permute-start(f32[108,128]{1,0:T(8,128)S(1)} %reshape.7.link_ref.link_a), channel_id=1, source_target_pairs={{0,12},{1,13},{2,6},{3,7},{4,0},{5,1},{6,10},{7,11},{8,4},{9,5},{1... | collective-permute-start | bytes 165896 | tf_op jit(solution)/shard_map/ppermute | solution.py:345
  24.0 5.1 %collective-permute-start.3 = (f32[2,3,16,256]{3,2,1,0:T(8,128)S(1)}, f32[2,3,16,256]{3,2,1,0:T(8,128)S(1)}, u32[]{:S(2)}, u32[]{:S(2)}) collective-permute-start(f32[2,3,16,256]{3,2,1,0:T(8,128)S(1)} %slice.8), channel_id=1, source_target_pairs={{0,1},{1,0},{2,3},{3,2},{4,5},{5,4},{6,7},{7,6},{8,9},{9,8},{10,11... | collective-permute-start | bytes 294920 | tf_op jit(solution)/shard_map/ppermute | solution.py:345
  33.7 5.7 %collective-permute-start.11 = (f32[96,256]{1,0:T(8,128)S(1)}, f32[96,256]{1,0:T(8,128)S(1)}, u32[]{:S(2)}, u32[]{:S(2)}) collective-permute-start(f32[96,256]{1,0:T(8,128)S(1)} %get-tuple-element.25), channel_id=1, source_target_pairs={{0,4},{1,5},{2,6},{3,7},{4,0},{5,1},{6,2},{7,3},{8,12},{9,13},{10,... | collective-permute-start | bytes 294920 | tf_op jit(solution)/shard_map/ppermute | solution.py:345
  34.2 8.1 %collective-permute-start.9 = (f32[96,256]{1,0:T(8,128)S(1)}, f32[96,256]{1,0:T(8,128)S(1)}, u32[]{:S(2)}, u32[]{:S(2)}) collective-permute-start(f32[96,256]{1,0:T(8,128)S(1)} %get-tuple-element.23), channel_id=1, source_target_pairs={{0,4},{1,5},{2,6},{3,7},{4,0},{5,1},{6,2},{7,3},{8,12},{9,13},{10,... | collective-permute-start | bytes 294920 | tf_op jit(solution)/shard_map/ppermute | solution.py:345
  39.4 8.7 %collective-permute-start.12 = (f32[96,256]{1,0:T(8,128)S(1)}, f32[96,256]{1,0:T(8,128)S(1)}, u32[]{:S(2)}, u32[]{:S(2)}) collective-permute-start(f32[96,256]{1,0:T(8,128)S(1)} %shard_map.84.refs_0_), channel_id=1, source_target_pairs={{0,8},{1,9},{2,10},{3,11},{4,12},{5,13},{6,14},{7,15},{8,0},{9,1},... | collective-permute-start | bytes 294920 | tf_op jit(solution)/shard_map/ppermute | solution.py:345
  42.3 8.3 %collective-permute-start.10 = (f32[96,256]{1,0:T(8,128)S(1)}, f32[96,256]{1,0:T(8,128)S(1)}, u32[]{:S(2)}, u32[]{:S(2)}) collective-permute-start(f32[96,256]{1,0:T(8,128)S(1)} %shard_map.82.refs_0_), channel_id=1, source_target_pairs={{0,8},{1,9},{2,10},{3,11},{4,12},{5,13},{6,14},{7,15},{8,0},{9,1},... | collective-permute-start | bytes 294920 | tf_op jit(solution)/shard_map/ppermute | solution.py:345
  48.2 4.7 %collective-permute-start.14 = (f32[96,256]{1,0:T(8,128)S(1)}, f32[96,256]{1,0:T(8,128)S(1)}, u32[]{:S(2)}, u32[]{:S(2)}) collective-permute-start(f32[96,256]{1,0:T(8,128)S(1)} %shard_map.85.refs_1_), channel_id=1, source_target_pairs={{0,4},{1,5},{2,6},{3,7},{4,0},{5,1},{6,2},{7,3},{8,12},{9,13},{10,... | collective-permute-start | bytes 294920 | tf_op jit(solution)/shard_map/ppermute | solution.py:345
  50.3 4.6 %collective-permute-start.16 = (f32[96,256]{1,0:T(8,128)S(1)}, f32[96,256]{1,0:T(8,128)S(1)}, u32[]{:S(2)}, u32[]{:S(2)}) collective-permute-start(f32[96,256]{1,0:T(8,128)S(1)} %shard_map.85.refs_1_), channel_id=1, source_target_pairs={{0,2},{1,3},{2,0},{3,1},{4,6},{5,7},{6,4},{7,5},{8,10},{9,11},{10,... | collective-permute-start | bytes 294920 | tf_op jit(solution)/shard_map/ppermute | solution.py:345
  50.3 4.6 %collective-permute-start.20 = (f32[96,256]{1,0:T(8,128)S(1)}, f32[96,256]{1,0:T(8,128)S(1)}, u32[]{:S(2)}, u32[]{:S(2)}) collective-permute-start(f32[96,256]{1,0:T(8,128)S(1)} %shard_map.85.refs_1_), channel_id=1, source_target_pairs={{0,1},{1,0},{2,3},{3,2},{4,5},{5,4},{6,7},{7,6},{8,9},{9,8},{10,11... | collective-permute-start | bytes 294920 | tf_op jit(solution)/shard_map/ppermute | solution.py:345
  50.6 5.1 %collective-permute-start.13 = (f32[96,256]{1,0:T(8,128)S(1)}, f32[96,256]{1,0:T(8,128)S(1)}, u32[]{:S(2)}, u32[]{:S(2)}) collective-permute-start(f32[96,256]{1,0:T(8,128)S(1)} %shard_map.83.refs_0_), channel_id=1, source_target_pairs={{0,4},{1,5},{2,6},{3,7},{4,0},{5,1},{6,2},{7,3},{8,12},{9,13},{10,... | collective-permute-start | bytes 294920 | tf_op jit(solution)/shard_map/ppermute | solution.py:345
  52.2 5.7 %collective-permute-start.15 = (f32[96,256]{1,0:T(8,128)S(1)}, f32[96,256]{1,0:T(8,128)S(1)}, u32[]{:S(2)}, u32[]{:S(2)}) collective-permute-start(f32[96,256]{1,0:T(8,128)S(1)} %shard_map.83.refs_0_), channel_id=1, source_target_pairs={{0,2},{1,3},{2,0},{3,1},{4,6},{5,7},{6,4},{7,5},{8,10},{9,11},{10,... | collective-permute-start | bytes 294920 | tf_op jit(solution)/shard_map/ppermute | solution.py:345
  52.9 5.0 %collective-permute-start.19 = (f32[96,256]{1,0:T(8,128)S(1)}, f32[96,256]{1,0:T(8,128)S(1)}, u32[]{:S(2)}, u32[]{:S(2)}) collective-permute-start(f32[96,256]{1,0:T(8,128)S(1)} %shard_map.83.refs_0_), channel_id=1, source_target_pairs={{0,1},{1,0},{2,3},{3,2},{4,5},{5,4},{6,7},{7,6},{8,9},{9,8},{10,11... | collective-permute-start | bytes 294920 | tf_op jit(solution)/shard_map/ppermute | solution.py:345
  54.9 5.5 %collective-permute-start.18 = (f32[96,256]{1,0:T(8,128)S(1)}, f32[96,256]{1,0:T(8,128)S(1)}, u32[]{:S(2)}, u32[]{:S(2)}) collective-permute-start(f32[96,256]{1,0:T(8,128)S(1)} %collective-permute-done.14.refs_3_), channel_id=1, source_target_pairs={{0,2},{1,3},{2,0},{3,1},{4,6},{5,7},{6,4},{7,5},{8,10},{9,11},{10,... | collective-permute-start | bytes 294920 | tf_op jit(solution)/shard_map/ppermute | solution.py:345
  54.9 5.5 %collective-permute-start.22 = (f32[96,256]{1,0:T(8,128)S(1)}, f32[96,256]{1,0:T(8,128)S(1)}, u32[]{:S(2)}, u32[]{:S(2)}) collective-permute-start(f32[96,256]{1,0:T(8,128)S(1)} %collective-permute-done.14.refs_3_), channel_id=1, source_target_pairs={{0,1},{1,0},{2,3},{3,2},{4,5},{5,4},{6,7},{7,6},{8,9},{9,8},{10,11... | collective-permute-start | bytes 294920 | tf_op jit(solution)/shard_map/ppermute | solution.py:345
  55.7 5.8 %collective-permute-start.17 = (f32[96,256]{1,0:T(8,128)S(1)}, f32[96,256]{1,0:T(8,128)S(1)}, u32[]{:S(2)}, u32[]{:S(2)}) collective-permute-start(f32[96,256]{1,0:T(8,128)S(1)} %collective-permute-done.13.refs_2_), channel_id=1, source_target_pairs={{0,2},{1,3},{2,0},{3,1},{4,6},{5,7},{6,4},{7,5},{8,10},{9,11},{10,... | collective-permute-start | bytes 294920 | tf_op jit(solution)/shard_map/ppermute | solution.py:345
  57.9 4.4 %collective-permute-start.21 = (f32[96,256]{1,0:T(8,128)S(1)}, f32[96,256]{1,0:T(8,128)S(1)}, u32[]{:S(2)}, u32[]{:S(2)}) collective-permute-start(f32[96,256]{1,0:T(8,128)S(1)} %collective-permute-done.13.refs_2_), channel_id=1, source_target_pairs={{0,1},{1,0},{2,3},{3,2},{4,5},{5,4},{6,7},{7,6},{8,9},{9,8},{10,11... | collective-permute-start | bytes 294920 | tf_op jit(solution)/shard_map/ppermute | solution.py:345
  57.9 4.4 %collective-permute-start.24 = (f32[96,256]{1,0:T(8,128)S(1)}, f32[96,256]{1,0:T(8,128)S(1)}, u32[]{:S(2)}, u32[]{:S(2)}) collective-permute-start(f32[96,256]{1,0:T(8,128)S(1)} %collective-permute-done.16.refs_5_), channel_id=1, source_target_pairs={{0,1},{1,0},{2,3},{3,2},{4,5},{5,4},{6,7},{7,6},{8,9},{9,8},{10,11... | collective-permute-start | bytes 294920 | tf_op jit(solution)/shard_map/ppermute | solution.py:345
  60.4 1.9 %collective-permute-start.23 = (f32[96,256]{1,0:T(8,128)S(1)}, f32[96,256]{1,0:T(8,128)S(1)}, u32[]{:S(2)}, u32[]{:S(2)}) collective-permute-start(f32[96,256]{1,0:T(8,128)S(1)} %collective-permute-done.15.refs_4_), channel_id=1, source_target_pairs={{0,1},{1,0},{2,3},{3,2},{4,5},{5,4},{6,7},{7,6},{8,9},{9,8},{10,11... | collective-permute-start | bytes 294920 | tf_op jit(solution)/shard_map/ppermute | solution.py:345
  60.4 1.9 %collective-permute-start.26 = (f32[96,256]{1,0:T(8,128)S(1)}, f32[96,256]{1,0:T(8,128)S(1)}, u32[]{:S(2)}, u32[]{:S(2)}) collective-permute-start(f32[96,256]{1,0:T(8,128)S(1)} %collective-permute-done.18.refs_7_), channel_id=1, source_target_pairs={{0,1},{1,0},{2,3},{3,2},{4,5},{5,4},{6,7},{7,6},{8,9},{9,8},{10,11... | collective-permute-start | bytes 294920 | tf_op jit(solution)/shard_map/ppermute | solution.py:345
  (7 other events, 104.9 us)

commit v4 on v2

--- a/solution.py
+++ b/solution.py
@@ -148,7 +148,7 @@
     coef_ref[:54, :] = of_time(link_b, odd)
     there = coef_ref[:18, :]
     before = adjoint_rows(of_time(link_a, odd)[:18])
-    after = adjoint_rows(of_time(link_c, odd)[:18])
+    after = adjoint_rows(of_time(link_c, odd))
     coef_ref[56:74, :] = jnp.where(odd == 0, before, there)
     coef_ref[80:98, :] = jnp.where(odd == 0, there, after)
     turned_ref[...] = coef_ref[...].T
@@ -359,7 +359,8 @@
         vec_b.append(send(theirs[i], partner))
         vec_c.append(send(mine[i], along))
     link_b = send(flat, partner)
-    link_c = send(flat, along)
+    rows = flat.reshape(links.shape[0], 54, sites)[:, :18]
+    link_c = send(rows.reshape(links.shape[0] * 18, sites), along)
     halo_a = send(mine[0][:, :, :LZ], twin)
     halo_b = send(vec_b[0][:, :, :LZ], twin)
 
@@ -395,6 +396,7 @@
     size = half // pairs
     spread = call(spread_kernel, (shape(size, width),) * pairs, (places, keep, got), scalars=1,
                   scratch=(pltpu.VMEM((half, width), jnp.float32),))
+
     parts = [spread[0]] + [send(spread[d], shift(d)) for d in range(1, pairs)]
     shard = call(sum_kernel, shape(size, width), parts)
     here = [shard] + [send(shard, shift(d)) for d in range(1, pairs)]

time: 67.9 us -> 67.3 us (level)
  waiting for transfers between devices: 26.5 us -> 25.2 us
    ppermute x27, waiting for transfers between devices: 26.5 us -> 25.2 us  [send(): return lax.ppermute(value, 'space', route)]
  transfers between devices with their start and end apart: 27 -> 27, of which waited for: 13 -> 11; matrix products, arithmetic and copies ran while one was open for 0% -> 0% of each run, Pallas kernels for 8% -> 8%
where the time goes in v4:
time: 67.3 us; the launch traced here: 67.1 us
  starting transfers between devices  27 us (40%)
  waiting for transfers between devices  25.2 us (37%)
  Pallas kernels  11.7 us (17%)
  local copies, waits for them, and re-layouts  1.63 us (2%)
  between operations  1.53 us (2%)
    ppermute x27, starting transfers between devices, send(): return lax.ppermute(value, 'space', route)  27 us
    ppermute x27, waiting for transfers between devices, send(): return lax.ppermute(value, 'space', route)  25.2 us
    pallas_call x7, Pallas kernels, call(): pl.pallas_call(kernel, out_shape=out, in_specs=[SMEM] * scalars + [VMEM]...  11.7 us
    squeeze x1, local copies, waits for them, and re-layouts, cut(): return lax.dynamic_slice(vectors, (time, 0, 0, i * part, 0), block)[0]  1.51 us
  transfers between devices with their start and end apart: 27, of which 11 were waited for; matrix products, arithmetic and copies ran while one was open for 0% of the time, Pallas kernels for 8%

profile of v4, /device:TPU:0, one launch (start us, length us, event | category | flops | bytes accessed | tf_op | source)
XLA Modules:
  0.0 67.1 jit_solution(12495101933841771891)
XLA Ops:
  0.7 1.5 %dynamic-slice_bitcast_fusion = (f32[2,3,64,256]{3,2,1,0:T(8,128)S(1)}, f32[2,3,64,256]{3,2,1,0:T(8,128)S(1)}, f32[2,3,64,256]{3,2,1,0:T(8,128)S(1)}, f32[2,3,64,256]{3,2,1,0:T(8,128)S(1)}) fusion(f32[2,2,3,128,256]{4,3,2,1,0:T(8,128)} %param.6, s32[]{:T(128)S(6)} %select_n.21, s32[]{:T(128)S(6)} %select_n.22), kind=kLoop, calls=%fused_computation | loop fusion | bytes 3145736 | tf_op jit(solution)/shard_map/squeeze | solution.py:353
  2.2 3.1 %collective-permute-start.2 = (f32[2,3,64,256]{3,2,1,0:T(8,128)S(1)}, f32[2,3,64,256]{3,2,1,0:T(8,128)S(1)}, u32[]{:S(2)}, u32[]{:S(2)}) collective-permute-start(f32[2,3,64,256]{3,2,1,0:T(8,128)S(1)} %get-tuple-element.29), channel_id=1, source_target_pairs={{0,2},{1,3},{2,0},{3,1},{4,6},{5,7},{6,4},{7,5},{8,10},{9,11},{10,... | collective-permute-start | bytes 1179656 | tf_op jit(solution)/shard_map/ppermute | solution.py:339
  5.3 3.6 %collective-permute-start.4 = (f32[2,3,64,256]{3,2,1,0:T(8,128)S(1)}, f32[2,3,64,256]{3,2,1,0:T(8,128)S(1)}, u32[]{:S(2)}, u32[]{:S(2)}) collective-permute-start(f32[2,3,64,256]{3,2,1,0:T(8,128)S(1)} %get-tuple-element.26.v0_ref.va_ref), channel_id=1, source_target_pairs={{0,12},{1,13},{2,6},{3,7},{4,0},{5,1},{6,10},{7,11},{8,4},{9,5},{1... | collective-permute-start | bytes 1179656 | tf_op jit(solution)/shard_map/ppermute | solution.py:339
  9.6 1.2 %collective-permute-done.7.halo_ref = f32[2,3,16,256]{3,2,1,0:T(8,128)S(1)} collective-permute-done((f32[2,3,16,256]{3,2,1,0:T(8,128)S(1)}, f32[2,3,16,256]{3,2,1,0:T(8,128)S(1)}, u32[]{:S(2)}, u32[]{:S(2)}) %collective-permute-start.7) | collective-permute-done | bytes 98336 | tf_op jit(solution)/shard_map/ppermute | solution.py:339
  10.7 1.5 %collective-permute-start.5 = (f32[108,128]{1,0:T(8,128)S(1)}, f32[108,128]{1,0:T(8,128)S(1)}, u32[]{:S(2)}, u32[]{:S(2)}) collective-permute-start(f32[108,128]{1,0:T(8,128)S(1)} %reshape.10.link_ref.link_a), channel_id=1, source_target_pairs={{0,2},{1,3},{2,0},{3,1},{4,6},{5,7},{6,4},{7,5},{8,10},{9,11},{10,... | collective-permute-start | bytes 165896 | tf_op jit(solution)/shard_map/ppermute | solution.py:339
  12.3 3.0 %collective-permute-done.2.vb_ref.before_ref = f32[2,3,64,256]{3,2,1,0:T(8,128)S(1)} collective-permute-done((f32[2,3,64,256]{3,2,1,0:T(8,128)S(1)}, f32[2,3,64,256]{3,2,1,0:T(8,128)S(1)}, u32[]{:S(2)}, u32[]{:S(2)}) %collective-permute-start.2) | collective-permute-done | bytes 393248 | tf_op jit(solution)/shard_map/ppermute | solution.py:339
  15.2 4.1 %collective-permute-start.6 = (f32[36,128]{1,0:T(8,128)S(1)}, f32[36,128]{1,0:T(8,128)S(1)}, u32[]{:S(2)}, u32[]{:S(2)}) collective-permute-start(f32[36,128]{1,0:T(8,128)S(1)} %reshape.11), channel_id=1, source_target_pairs={{0,12},{1,13},{2,6},{3,7},{4,0},{5,1},{6,10},{7,11},{8,4},{9,5},{1... | collective-permute-start | bytes 55304 | tf_op jit(solution)/shard_map/ppermute | solution.py:339
  19.3 2.9 %shard_map.78.own_ref = f32[2,256,256]{2,1,0:T(8,128)S(1)} custom-call(s32[1]{0:T(128)} %bitcast.place_ref, f32[2,3,64,256]{3,2,1,0:T(8,128)S(1)} %get-tuple-element.26.v0_ref.va_ref, f32[2,3,64,256]{3,2,1,0:T(8,128)S(1)} %get-tuple-element.28.v1_ref.va_ref, f32[2,3,16,256]{3,2,1,0:T(8,128)S(1)} %collective-permute-done.7.halo_ref, ...), custom_call_target="tpu_custom_call" | custom-call | flops 1207959552 | bytes 1464324 | tf_op jit(solution)/shard_map/pallas_call | solution.py:315
  22.3 3.6 %collective-permute-done.6.link_c = f32[36,128]{1,0:T(8,128)S(1)} collective-permute-done((f32[36,128]{1,0:T(8,128)S(1)}, f32[36,128]{1,0:T(8,128)S(1)}, u32[]{:S(2)}, u32[]{:S(2)}) %collective-permute-start.6) | collective-permute-done | bytes 18464 | tf_op jit(solution)/shard_map/ppermute | solution.py:339
  25.8 2.5 %shard_map.79 = (f32[768,256]{1,0:T(8,128)S(1)}, f32[128,128]{1,0:T(8,128)S(1)}) custom-call(s32[1]{0:T(128)} %bitcast.place_ref, f32[2,3,64,256]{3,2,1,0:T(8,128)S(1)} %get-tuple-element.26.v0_ref.va_ref, f32[2,3,64,256]{3,2,1,0:T(8,128)S(1)} %collective-permute-done.2.vb_ref.before_ref, f32[2,3,64,256]{3,2,1,0:T(8,128)S(1)} %collective-permute-done.4.vc_ref, ...), custom_call_target="tpu_custom_call" | custom-call | flops 1207959552 | bytes 2684932 | tf_op jit(solution)/shard_map/pallas_call | solution.py:315
  28.4 2.6 %shard_map.80 = (f32[384,256]{1,0:T(8,128)S(1)}, f32[384,256]{1,0:T(8,128)S(1)}) custom-call(s32[1]{0:T(128)} %bitcast.place_ref, f32[2,3,64,256]{3,2,1,0:T(8,128)S(1)} %get-tuple-element.28.v1_ref.va_ref, f32[2,3,64,256]{3,2,1,0:T(8,128)S(1)} %collective-permute-done.vb_ref, f32[2,3,64,256]{3,2,1,0:T(8,128)S(1)} %collective-permute-done.1.vc_ref, ...), custom_call_target="tpu_custom_call" | custom-call | flops 1207959552 | bytes 3309572 | tf_op jit(solution)/shard_map/pallas_call | solution.py:315
  31.6 1.3 %collective-permute-done.8.got_ref = f32[384,256]{1,0:T(8,128)S(1)} collective-permute-done((f32[384,256]{1,0:T(8,128)S(1)}, f32[384,256]{1,0:T(8,128)S(1)}, u32[]{:S(2)}, u32[]{:S(2)}) %collective-permute-start.8) | collective-permute-done | bytes 393248 | tf_op jit(solution)/shard_map/ppermute | solution.py:339
  33.0 1.5 %collective-permute-start.10 = (f32[96,256]{1,0:T(8,128)S(1)}, f32[96,256]{1,0:T(8,128)S(1)}, u32[]{:S(2)}, u32[]{:S(2)}) collective-permute-start(f32[96,256]{1,0:T(8,128)S(1)} %get-tuple-element.24), channel_id=1, source_target_pairs={{0,8},{1,9},{2,10},{3,11},{4,12},{5,13},{6,14},{7,15},{8,0},{9,1},... | collective-permute-start | bytes 294920 | tf_op jit(solution)/shard_map/ppermute | solution.py:339
  34.6 2.9 %collective-permute-start.11 = (f32[96,256]{1,0:T(8,128)S(1)}, f32[96,256]{1,0:T(8,128)S(1)}, u32[]{:S(2)}, u32[]{:S(2)}) collective-permute-start(f32[96,256]{1,0:T(8,128)S(1)} %get-tuple-element.25), channel_id=1, source_target_pairs={{0,12},{1,13},{2,14},{3,15},{4,0},{5,1},{6,2},{7,3},{8,4},{9,5},{1... | collective-permute-start | bytes 294920 | tf_op jit(solution)/shard_map/ppermute | solution.py:339
  37.9 3.6 %collective-permute-done.10.refs_2_ = f32[96,256]{1,0:T(8,128)S(1)} collective-permute-done((f32[96,256]{1,0:T(8,128)S(1)}, f32[96,256]{1,0:T(8,128)S(1)}, u32[]{:S(2)}, u32[]{:S(2)}) %collective-permute-start.10) | collective-permute-done | bytes 98336 | tf_op jit(solution)/shard_map/ppermute | solution.py:339
  41.6 3.5 %collective-permute-done.9.refs_1_ = f32[96,256]{1,0:T(8,128)S(1)} collective-permute-done((f32[96,256]{1,0:T(8,128)S(1)}, f32[96,256]{1,0:T(8,128)S(1)}, u32[]{:S(2)}, u32[]{:S(2)}) %collective-permute-start.9) | collective-permute-done | bytes 98336 | tf_op jit(solution)/shard_map/ppermute | solution.py:339
  46.0 2.4 %collective-permute-start.13 = (f32[96,256]{1,0:T(8,128)S(1)}, f32[96,256]{1,0:T(8,128)S(1)}, u32[]{:S(2)}, u32[]{:S(2)}) collective-permute-start(f32[96,256]{1,0:T(8,128)S(1)} %shard_map.82.refs_0_), channel_id=1, source_target_pairs={{0,8},{1,9},{2,10},{3,11},{4,12},{5,13},{6,14},{7,15},{8,0},{9,1},... | collective-permute-start | bytes 294920 | tf_op jit(solution)/shard_map/ppermute | solution.py:339
  48.4 1.5 %collective-permute-start.14 = (f32[96,256]{1,0:T(8,128)S(1)}, f32[96,256]{1,0:T(8,128)S(1)}, u32[]{:S(2)}, u32[]{:S(2)}) collective-permute-start(f32[96,256]{1,0:T(8,128)S(1)} %shard_map.82.refs_0_), channel_id=1, source_target_pairs={{0,12},{1,13},{2,14},{3,15},{4,0},{5,1},{6,2},{7,3},{8,4},{9,5},{1... | collective-permute-start | bytes 294920 | tf_op jit(solution)/shard_map/ppermute | solution.py:339
  50.6 2.1 %collective-permute-done.12.refs_1_ = f32[96,256]{1,0:T(8,128)S(1)} collective-permute-done((f32[96,256]{1,0:T(8,128)S(1)}, f32[96,256]{1,0:T(8,128)S(1)}, u32[]{:S(2)}, u32[]{:S(2)}) %collective-permute-start.12) | collective-permute-done | bytes 98336 | tf_op jit(solution)/shard_map/ppermute | solution.py:339
  52.7 3.0 %collective-permute-done.13.refs_2_ = f32[96,256]{1,0:T(8,128)S(1)} collective-permute-done((f32[96,256]{1,0:T(8,128)S(1)}, f32[96,256]{1,0:T(8,128)S(1)}, u32[]{:S(2)}, u32[]{:S(2)}) %collective-permute-start.13) | collective-permute-done | bytes 98336 | tf_op jit(solution)/shard_map/ppermute | solution.py:339
  55.7 2.0 %collective-permute-start.18 = (f32[96,256]{1,0:T(8,128)S(1)}, f32[96,256]{1,0:T(8,128)S(1)}, u32[]{:S(2)}, u32[]{:S(2)}) collective-permute-start(f32[96,256]{1,0:T(8,128)S(1)} %collective-permute-done.14.refs_3_), channel_id=1, source_target_pairs={{0,2},{1,3},{2,0},{3,1},{4,6},{5,7},{6,4},{7,5},{8,10},{9,11},{10,... | collective-permute-start | bytes 294920 | tf_op jit(solution)/shard_map/ppermute | solution.py:339
  58.3 2.5 %collective-permute-done.17.refs_6_ = f32[96,256]{1,0:T(8,128)S(1)} collective-permute-done((f32[96,256]{1,0:T(8,128)S(1)}, f32[96,256]{1,0:T(8,128)S(1)}, u32[]{:S(2)}, u32[]{:S(2)}) %collective-permute-start.17) | collective-permute-done | bytes 98336 | tf_op jit(solution)/shard_map/ppermute | solution.py:339
  60.8 1.1 %collective-permute-done.18.refs_7_ = f32[96,256]{1,0:T(8,128)S(1)} collective-permute-done((f32[96,256]{1,0:T(8,128)S(1)}, f32[96,256]{1,0:T(8,128)S(1)}, u32[]{:S(2)}, u32[]{:S(2)}) %collective-permute-start.18) | collective-permute-done | bytes 98336 | tf_op jit(solution)/shard_map/ppermute | solution.py:339
  63.7 3.4 %shard_map.83 = (f32[2,3,2,16,256]{4,3,2,1,0:T(8,128)}, f32[2,64,64]{2,1,0:T(8,128)}) custom-call(s32[1]{0:T(128)} %bitcast.place_ref, s32[3]{0:T(128)S(1)} %copy-done.1, s32[2]{0:T(128)S(1)} %copy-done.2, s32[1]{0:T(128)S(6)} %copy.10.block_ref, bf16[256,1536]{1,0:T(8,128)(2,1)S(1)} %get-tuple-element.14.b_high, ...), custom_call_target="tpu_custom_call" | custom-call | flops 150994944 | bytes 3637276 | tf_op jit(solution)/shard_map/pallas_call | solution.py:315
  (53 shorter events, 5.2 us)
Async XLA Ops:
  2.2 13.0 %collective-permute-start.2 = (f32[2,3,64,256]{3,2,1,0:T(8,128)S(1)}, f32[2,3,64,256]{3,2,1,0:T(8,128)S(1)}, u32[]{:S(2)}, u32[]{:S(2)}) collective-permute-start(f32[2,3,64,256]{3,2,1,0:T(8,128)S(1)} %get-tuple-element.29), channel_id=1, source_target_pairs={{0,2},{1,3},{2,0},{3,1},{4,6},{5,7},{6,4},{7,5},{8,10},{9,11},{10,... | collective-permute-start | bytes 1179656 | tf_op jit(solution)/shard_map/ppermute | solution.py:339
  5.3 20.6 %collective-permute-start.4 = (f32[2,3,64,256]{3,2,1,0:T(8,128)S(1)}, f32[2,3,64,256]{3,2,1,0:T(8,128)S(1)}, u32[]{:S(2)}, u32[]{:S(2)}) collective-permute-start(f32[2,3,64,256]{3,2,1,0:T(8,128)S(1)} %get-tuple-element.26.v0_ref.va_ref), channel_id=1, source_target_pairs={{0,12},{1,13},{2,6},{3,7},{4,0},{5,1},{6,10},{7,11},{8,4},{9,5},{1... | collective-permute-start | bytes 1179656 | tf_op jit(solution)/shard_map/ppermute | solution.py:339
  8.9 19.5 %collective-permute-start = (f32[2,3,64,256]{3,2,1,0:T(8,128)S(1)}, f32[2,3,64,256]{3,2,1,0:T(8,128)S(1)}, u32[]{:S(2)}, u32[]{:S(2)}) collective-permute-start(f32[2,3,64,256]{3,2,1,0:T(8,128)S(1)} %get-tuple-element.27), channel_id=1, source_target_pairs={{0,2},{1,3},{2,0},{3,1},{4,6},{5,7},{6,4},{7,5},{8,10},{9,11},{10,... | collective-permute-start | bytes 1179656 | tf_op jit(solution)/shard_map/ppermute | solution.py:339
  8.9 19.5 %collective-permute-start.1 = (f32[2,3,64,256]{3,2,1,0:T(8,128)S(1)}, f32[2,3,64,256]{3,2,1,0:T(8,128)S(1)}, u32[]{:S(2)}, u32[]{:S(2)}) collective-permute-start(f32[2,3,64,256]{3,2,1,0:T(8,128)S(1)} %get-tuple-element.28.v1_ref.va_ref), channel_id=1, source_target_pairs={{0,12},{1,13},{2,6},{3,7},{4,0},{5,1},{6,10},{7,11},{8,4},{9,5},{1... | collective-permute-start | bytes 1179656 | tf_op jit(solution)/shard_map/ppermute | solution.py:339
  10.7 15.1 %collective-permute-start.5 = (f32[108,128]{1,0:T(8,128)S(1)}, f32[108,128]{1,0:T(8,128)S(1)}, u32[]{:S(2)}, u32[]{:S(2)}) collective-permute-start(f32[108,128]{1,0:T(8,128)S(1)} %reshape.10.link_ref.link_a), channel_id=1, source_target_pairs={{0,2},{1,3},{2,0},{3,1},{4,6},{5,7},{6,4},{7,5},{8,10},{9,11},{10,... | collective-permute-start | bytes 165896 | tf_op jit(solution)/shard_map/ppermute | solution.py:339
  15.2 10.6 %collective-permute-start.6 = (f32[36,128]{1,0:T(8,128)S(1)}, f32[36,128]{1,0:T(8,128)S(1)}, u32[]{:S(2)}, u32[]{:S(2)}) collective-permute-start(f32[36,128]{1,0:T(8,128)S(1)} %reshape.11), channel_id=1, source_target_pairs={{0,12},{1,13},{2,6},{3,7},{4,0},{5,1},{6,10},{7,11},{8,4},{9,5},{1... | collective-permute-start | bytes 55304 | tf_op jit(solution)/shard_map/ppermute | solution.py:339
  25.8 2.6 %collective-permute-start.3 = (f32[2,3,16,256]{3,2,1,0:T(8,128)S(1)}, f32[2,3,16,256]{3,2,1,0:T(8,128)S(1)}, u32[]{:S(2)}, u32[]{:S(2)}) collective-permute-start(f32[2,3,16,256]{3,2,1,0:T(8,128)S(1)} %slice.12), channel_id=1, source_target_pairs={{0,1},{1,0},{2,3},{3,2},{4,5},{5,4},{6,7},{7,6},{8,9},{9,8},{10,11... | collective-permute-start | bytes 294920 | tf_op jit(solution)/shard_map/ppermute | solution.py:339
  31.1 1.9 %collective-permute-start.8 = (f32[384,256]{1,0:T(8,128)S(1)}, f32[384,256]{1,0:T(8,128)S(1)}, u32[]{:S(2)}, u32[]{:S(2)}) collective-permute-start(f32[384,256]{1,0:T(8,128)S(1)} %get-tuple-element.21), channel_id=1, source_target_pairs={{0,1},{1,0},{2,3},{3,2},{4,5},{5,4},{6,7},{7,6},{8,9},{9,8},{10,11... | collective-permute-start | bytes 1179656 | tf_op jit(solution)/shard_map/ppermute | solution.py:339
  33.0 8.5 %collective-permute-start.10 = (f32[96,256]{1,0:T(8,128)S(1)}, f32[96,256]{1,0:T(8,128)S(1)}, u32[]{:S(2)}, u32[]{:S(2)}) collective-permute-start(f32[96,256]{1,0:T(8,128)S(1)} %get-tuple-element.24), channel_id=1, source_target_pairs={{0,8},{1,9},{2,10},{3,11},{4,12},{5,13},{6,14},{7,15},{8,0},{9,1},... | collective-permute-start | bytes 294920 | tf_op jit(solution)/shard_map/ppermute | solution.py:339
  34.6 7.0 %collective-permute-start.11 = (f32[96,256]{1,0:T(8,128)S(1)}, f32[96,256]{1,0:T(8,128)S(1)}, u32[]{:S(2)}, u32[]{:S(2)}) collective-permute-start(f32[96,256]{1,0:T(8,128)S(1)} %get-tuple-element.25), channel_id=1, source_target_pairs={{0,12},{1,13},{2,14},{3,15},{4,0},{5,1},{6,2},{7,3},{8,4},{9,5},{1... | collective-permute-start | bytes 294920 | tf_op jit(solution)/shard_map/ppermute | solution.py:339
  37.4 7.6 %collective-permute-start.9 = (f32[96,256]{1,0:T(8,128)S(1)}, f32[96,256]{1,0:T(8,128)S(1)}, u32[]{:S(2)}, u32[]{:S(2)}) collective-permute-start(f32[96,256]{1,0:T(8,128)S(1)} %get-tuple-element.23), channel_id=1, source_target_pairs={{0,4},{1,5},{2,6},{3,7},{4,8},{5,9},{6,10},{7,11},{8,12},{9,13},{1... | collective-permute-start | bytes 294920 | tf_op jit(solution)/shard_map/ppermute | solution.py:339
  45.1 7.6 %collective-permute-start.12 = (f32[96,256]{1,0:T(8,128)S(1)}, f32[96,256]{1,0:T(8,128)S(1)}, u32[]{:S(2)}, u32[]{:S(2)}) collective-permute-start(f32[96,256]{1,0:T(8,128)S(1)} %shard_map.82.refs_0_), channel_id=1, source_target_pairs={{0,4},{1,5},{2,6},{3,7},{4,8},{5,9},{6,10},{7,11},{8,12},{9,13},{1... | collective-permute-start | bytes 294920 | tf_op jit(solution)/shard_map/ppermute | solution.py:339
  46.0 9.7 %collective-permute-start.13 = (f32[96,256]{1,0:T(8,128)S(1)}, f32[96,256]{1,0:T(8,128)S(1)}, u32[]{:S(2)}, u32[]{:S(2)}) collective-permute-start(f32[96,256]{1,0:T(8,128)S(1)} %shard_map.82.refs_0_), channel_id=1, source_target_pairs={{0,8},{1,9},{2,10},{3,11},{4,12},{5,13},{6,14},{7,15},{8,0},{9,1},... | collective-permute-start | bytes 294920 | tf_op jit(solution)/shard_map/ppermute | solution.py:339
  48.4 7.3 %collective-permute-start.14 = (f32[96,256]{1,0:T(8,128)S(1)}, f32[96,256]{1,0:T(8,128)S(1)}, u32[]{:S(2)}, u32[]{:S(2)}) collective-permute-start(f32[96,256]{1,0:T(8,128)S(1)} %shard_map.82.refs_0_), channel_id=1, source_target_pairs={{0,12},{1,13},{2,14},{3,15},{4,0},{5,1},{6,2},{7,3},{8,4},{9,5},{1... | collective-permute-start | bytes 294920 | tf_op jit(solution)/shard_map/ppermute | solution.py:339
  49.9 7.8 %collective-permute-start.15 = (f32[96,256]{1,0:T(8,128)S(1)}, f32[96,256]{1,0:T(8,128)S(1)}, u32[]{:S(2)}, u32[]{:S(2)}) collective-permute-start(f32[96,256]{1,0:T(8,128)S(1)} %shard_map.82.refs_0_), channel_id=1, source_target_pairs={{0,2},{1,3},{2,0},{3,1},{4,6},{5,7},{6,4},{7,5},{8,10},{9,11},{10,... | collective-permute-start | bytes 294920 | tf_op jit(solution)/shard_map/ppermute | solution.py:339
  50.6 7.1 %collective-permute-start.19 = (f32[96,256]{1,0:T(8,128)S(1)}, f32[96,256]{1,0:T(8,128)S(1)}, u32[]{:S(2)}, u32[]{:S(2)}) collective-permute-start(f32[96,256]{1,0:T(8,128)S(1)} %shard_map.82.refs_0_), channel_id=1, source_target_pairs={{0,1},{1,0},{2,3},{3,2},{4,5},{5,4},{6,7},{7,6},{8,9},{9,8},{10,11... | collective-permute-start | bytes 294920 | tf_op jit(solution)/shard_map/ppermute | solution.py:339
  52.7 5.5 %collective-permute-start.16 = (f32[96,256]{1,0:T(8,128)S(1)}, f32[96,256]{1,0:T(8,128)S(1)}, u32[]{:S(2)}, u32[]{:S(2)}) collective-permute-start(f32[96,256]{1,0:T(8,128)S(1)} %collective-permute-done.12.refs_1_), channel_id=1, source_target_pairs={{0,2},{1,3},{2,0},{3,1},{4,6},{5,7},{6,4},{7,5},{8,10},{9,11},{10,... | collective-permute-start | bytes 294920 | tf_op jit(solution)/shard_map/ppermute | solution.py:339
  55.7 5.1 %collective-permute-start.17 = (f32[96,256]{1,0:T(8,128)S(1)}, f32[96,256]{1,0:T(8,128)S(1)}, u32[]{:S(2)}, u32[]{:S(2)}) collective-permute-start(f32[96,256]{1,0:T(8,128)S(1)} %collective-permute-done.13.refs_2_), channel_id=1, source_target_pairs={{0,2},{1,3},{2,0},{3,1},{4,6},{5,7},{6,4},{7,5},{8,10},{9,11},{10,... | collective-permute-start | bytes 294920 | tf_op jit(solution)/shard_map/ppermute | solution.py:339
  55.7 6.2 %collective-permute-start.18 = (f32[96,256]{1,0:T(8,128)S(1)}, f32[96,256]{1,0:T(8,128)S(1)}, u32[]{:S(2)}, u32[]{:S(2)}) collective-permute-start(f32[96,256]{1,0:T(8,128)S(1)} %collective-permute-done.14.refs_3_), channel_id=1, source_target_pairs={{0,2},{1,3},{2,0},{3,1},{4,6},{5,7},{6,4},{7,5},{8,10},{9,11},{10,... | collective-permute-start | bytes 294920 | tf_op jit(solution)/shard_map/ppermute | solution.py:339
  57.7 4.2 %collective-permute-start.20 = (f32[96,256]{1,0:T(8,128)S(1)}, f32[96,256]{1,0:T(8,128)S(1)}, u32[]{:S(2)}, u32[]{:S(2)}) collective-permute-start(f32[96,256]{1,0:T(8,128)S(1)} %collective-permute-done.12.refs_1_), channel_id=1, source_target_pairs={{0,1},{1,0},{2,3},{3,2},{4,5},{5,4},{6,7},{7,6},{8,9},{9,8},{10,11... | collective-permute-start | bytes 294920 | tf_op jit(solution)/shard_map/ppermute | solution.py:339
  57.7 4.7 %collective-permute-start.21 = (f32[96,256]{1,0:T(8,128)S(1)}, f32[96,256]{1,0:T(8,128)S(1)}, u32[]{:S(2)}, u32[]{:S(2)}) collective-permute-start(f32[96,256]{1,0:T(8,128)S(1)} %collective-permute-done.13.refs_2_), channel_id=1, source_target_pairs={{0,1},{1,0},{2,3},{3,2},{4,5},{5,4},{6,7},{7,6},{8,9},{9,8},{10,11... | collective-permute-start | bytes 294920 | tf_op jit(solution)/shard_map/ppermute | solution.py:339
  58.3 5.0 %collective-permute-start.22 = (f32[96,256]{1,0:T(8,128)S(1)}, f32[96,256]{1,0:T(8,128)S(1)}, u32[]{:S(2)}, u32[]{:S(2)}) collective-permute-start(f32[96,256]{1,0:T(8,128)S(1)} %collective-permute-done.14.refs_3_), channel_id=1, source_target_pairs={{0,1},{1,0},{2,3},{3,2},{4,5},{5,4},{6,7},{7,6},{8,9},{9,8},{10,11... | collective-permute-start | bytes 294920 | tf_op jit(solution)/shard_map/ppermute | solution.py:339
  60.8 2.5 %collective-permute-start.23 = (f32[96,256]{1,0:T(8,128)S(1)}, f32[96,256]{1,0:T(8,128)S(1)}, u32[]{:S(2)}, u32[]{:S(2)}) collective-permute-start(f32[96,256]{1,0:T(8,128)S(1)} %collective-permute-done.15.refs_4_), channel_id=1, source_target_pairs={{0,1},{1,0},{2,3},{3,2},{4,5},{5,4},{6,7},{7,6},{8,9},{9,8},{10,11... | collective-permute-start | bytes 294920 | tf_op jit(solution)/shard_map/ppermute | solution.py:339
  61.9 1.5 %collective-permute-start.25 = (f32[96,256]{1,0:T(8,128)S(1)}, f32[96,256]{1,0:T(8,128)S(1)}, u32[]{:S(2)}, u32[]{:S(2)}) collective-permute-start(f32[96,256]{1,0:T(8,128)S(1)} %collective-permute-done.17.refs_6_), channel_id=1, source_target_pairs={{0,1},{1,0},{2,3},{3,2},{4,5},{5,4},{6,7},{7,6},{8,9},{9,8},{10,11... | collective-permute-start | bytes 294920 | tf_op jit(solution)/shard_map/ppermute | solution.py:339
  (7 other events, 109.7 us)

commit v5 on v4

--- a/solution.py
+++ b/solution.py
@@ -400,7 +400,12 @@
     parts = [spread[0]] + [send(spread[d], shift(d)) for d in range(1, pairs)]
     shard = call(sum_kernel, shape(size, width), parts)
     here = [shard] + [send(shard, shift(d)) for d in range(1, pairs)]
-    there = [send(x, partner) for x in here]
+    there = [send(here[0], partner)]
+    for d in range(1, pairs):
+        if d == 1:
+            there.append(send(there[0], shift(d)))
+        else:
+            there.append(send(here[d], partner))
     pieces = here + there
     pieces = pieces + [send(x, twin) for x in pieces]
 

time: 67.3 us -> 69 us (1.025)
  waiting for transfers between devices: 25.2 us -> 27 us
    ppermute x27, waiting for transfers between devices: 25.2 us -> 27 us  [send(): return lax.ppermute(value, 'space', route)]
where the time goes in v5:
time: 69 us; the launch traced here: 68.9 us
  starting transfers between devices  27 us (39%)
  waiting for transfers between devices  27 us (39%)
  Pallas kernels  11.7 us (17%)
  local copies, waits for them, and re-layouts  1.63 us (2%)
  between operations  1.54 us (2%)
    ppermute x27, starting transfers between devices, send(): return lax.ppermute(value, 'space', route)  27 us
    ppermute x27, waiting for transfers between devices, send(): return lax.ppermute(value, 'space', route)  27 us
    pallas_call x7, Pallas kernels, call(): pl.pallas_call(kernel, out_shape=out, in_specs=[SMEM] * scalars + [VMEM]...  11.7 us
    squeeze x1, local copies, waits for them, and re-layouts, cut(): return lax.dynamic_slice(vectors, (time, 0, 0, i * part, 0), block)[0]  1.51 us
  transfers between devices with their start and end apart: 27, of which 11 were waited for; matrix products, arithmetic and copies ran while one was open for 0% of the time, Pallas kernels for 8%

profile of v5, /device:TPU:0, one launch (start us, length us, event | category | flops | bytes accessed | tf_op | source)
XLA Modules:
  0.0 68.9 jit_solution(2466200712160515481)
XLA Ops:
  0.7 1.5 %dynamic-slice_bitcast_fusion = (f32[2,3,64,256]{3,2,1,0:T(8,128)S(1)}, f32[2,3,64,256]{3,2,1,0:T(8,128)S(1)}, f32[2,3,64,256]{3,2,1,0:T(8,128)S(1)}, f32[2,3,64,256]{3,2,1,0:T(8,128)S(1)}) fusion(f32[2,2,3,128,256]{4,3,2,1,0:T(8,128)} %param.6, s32[]{:T(128)S(6)} %select_n.21, s32[]{:T(128)S(6)} %select_n.22), kind=kLoop, calls=%fused_computation | loop fusion | bytes 3145736 | tf_op jit(solution)/shard_map/squeeze | solution.py:353
  2.2 3.1 %collective-permute-start.2 = (f32[2,3,64,256]{3,2,1,0:T(8,128)S(1)}, f32[2,3,64,256]{3,2,1,0:T(8,128)S(1)}, u32[]{:S(2)}, u32[]{:S(2)}) collective-permute-start(f32[2,3,64,256]{3,2,1,0:T(8,128)S(1)} %get-tuple-element.29), channel_id=1, source_target_pairs={{0,2},{1,3},{2,0},{3,1},{4,6},{5,7},{6,4},{7,5},{8,10},{9,11},{10,... | collective-permute-start | bytes 1179656 | tf_op jit(solution)/shard_map/ppermute | solution.py:339
  5.3 3.6 %collective-permute-start.4 = (f32[2,3,64,256]{3,2,1,0:T(8,128)S(1)}, f32[2,3,64,256]{3,2,1,0:T(8,128)S(1)}, u32[]{:S(2)}, u32[]{:S(2)}) collective-permute-start(f32[2,3,64,256]{3,2,1,0:T(8,128)S(1)} %get-tuple-element.26.v0_ref.va_ref), channel_id=1, source_target_pairs={{0,12},{1,13},{2,6},{3,7},{4,0},{5,1},{6,10},{7,11},{8,4},{9,5},{1... | collective-permute-start | bytes 1179656 | tf_op jit(solution)/shard_map/ppermute | solution.py:339
  9.6 1.2 %collective-permute-done.7.halo_ref = f32[2,3,16,256]{3,2,1,0:T(8,128)S(1)} collective-permute-done((f32[2,3,16,256]{3,2,1,0:T(8,128)S(1)}, f32[2,3,16,256]{3,2,1,0:T(8,128)S(1)}, u32[]{:S(2)}, u32[]{:S(2)}) %collective-permute-start.7) | collective-permute-done | bytes 98336 | tf_op jit(solution)/shard_map/ppermute | solution.py:339
  10.7 1.5 %collective-permute-start.5 = (f32[108,128]{1,0:T(8,128)S(1)}, f32[108,128]{1,0:T(8,128)S(1)}, u32[]{:S(2)}, u32[]{:S(2)}) collective-permute-start(f32[108,128]{1,0:T(8,128)S(1)} %reshape.10.link_ref.link_a), channel_id=1, source_target_pairs={{0,2},{1,3},{2,0},{3,1},{4,6},{5,7},{6,4},{7,5},{8,10},{9,11},{10,... | collective-permute-start | bytes 165896 | tf_op jit(solution)/shard_map/ppermute | solution.py:339
  12.3 3.0 %collective-permute-done.2.vb_ref.before_ref = f32[2,3,64,256]{3,2,1,0:T(8,128)S(1)} collective-permute-done((f32[2,3,64,256]{3,2,1,0:T(8,128)S(1)}, f32[2,3,64,256]{3,2,1,0:T(8,128)S(1)}, u32[]{:S(2)}, u32[]{:S(2)}) %collective-permute-start.2) | collective-permute-done | bytes 393248 | tf_op jit(solution)/shard_map/ppermute | solution.py:339
  15.2 4.1 %collective-permute-start.6 = (f32[36,128]{1,0:T(8,128)S(1)}, f32[36,128]{1,0:T(8,128)S(1)}, u32[]{:S(2)}, u32[]{:S(2)}) collective-permute-start(f32[36,128]{1,0:T(8,128)S(1)} %reshape.11), channel_id=1, source_target_pairs={{0,12},{1,13},{2,6},{3,7},{4,0},{5,1},{6,10},{7,11},{8,4},{9,5},{1... | collective-permute-start | bytes 55304 | tf_op jit(solution)/shard_map/ppermute | solution.py:339
  19.3 2.9 %shard_map.78.own_ref = f32[2,256,256]{2,1,0:T(8,128)S(1)} custom-call(s32[1]{0:T(128)} %bitcast.place_ref, f32[2,3,64,256]{3,2,1,0:T(8,128)S(1)} %get-tuple-element.26.v0_ref.va_ref, f32[2,3,64,256]{3,2,1,0:T(8,128)S(1)} %get-tuple-element.28.v1_ref.va_ref, f32[2,3,16,256]{3,2,1,0:T(8,128)S(1)} %collective-permute-done.7.halo_ref, ...), custom_call_target="tpu_custom_call" | custom-call | flops 1207959552 | bytes 1464324 | tf_op jit(solution)/shard_map/pallas_call | solution.py:315
  22.3 3.6 %collective-permute-done.6.link_c = f32[36,128]{1,0:T(8,128)S(1)} collective-permute-done((f32[36,128]{1,0:T(8,128)S(1)}, f32[36,128]{1,0:T(8,128)S(1)}, u32[]{:S(2)}, u32[]{:S(2)}) %collective-permute-start.6) | collective-permute-done | bytes 18464 | tf_op jit(solution)/shard_map/ppermute | solution.py:339
  25.8 2.5 %shard_map.79 = (f32[768,256]{1,0:T(8,128)S(1)}, f32[128,128]{1,0:T(8,128)S(1)}) custom-call(s32[1]{0:T(128)} %bitcast.place_ref, f32[2,3,64,256]{3,2,1,0:T(8,128)S(1)} %get-tuple-element.26.v0_ref.va_ref, f32[2,3,64,256]{3,2,1,0:T(8,128)S(1)} %collective-permute-done.2.vb_ref.before_ref, f32[2,3,64,256]{3,2,1,0:T(8,128)S(1)} %collective-permute-done.4.vc_ref, ...), custom_call_target="tpu_custom_call" | custom-call | flops 1207959552 | bytes 2684932 | tf_op jit(solution)/shard_map/pallas_call | solution.py:315
  28.4 2.6 %shard_map.80 = (f32[384,256]{1,0:T(8,128)S(1)}, f32[384,256]{1,0:T(8,128)S(1)}) custom-call(s32[1]{0:T(128)} %bitcast.place_ref, f32[2,3,64,256]{3,2,1,0:T(8,128)S(1)} %get-tuple-element.28.v1_ref.va_ref, f32[2,3,64,256]{3,2,1,0:T(8,128)S(1)} %collective-permute-done.vb_ref, f32[2,3,64,256]{3,2,1,0:T(8,128)S(1)} %collective-permute-done.1.vc_ref, ...), custom_call_target="tpu_custom_call" | custom-call | flops 1207959552 | bytes 3309572 | tf_op jit(solution)/shard_map/pallas_call | solution.py:315
  31.6 1.3 %collective-permute-done.8.got_ref = f32[384,256]{1,0:T(8,128)S(1)} collective-permute-done((f32[384,256]{1,0:T(8,128)S(1)}, f32[384,256]{1,0:T(8,128)S(1)}, u32[]{:S(2)}, u32[]{:S(2)}) %collective-permute-start.8) | collective-permute-done | bytes 393248 | tf_op jit(solution)/shard_map/ppermute | solution.py:339
  33.0 1.5 %collective-permute-start.10 = (f32[96,256]{1,0:T(8,128)S(1)}, f32[96,256]{1,0:T(8,128)S(1)}, u32[]{:S(2)}, u32[]{:S(2)}) collective-permute-start(f32[96,256]{1,0:T(8,128)S(1)} %get-tuple-element.24), channel_id=1, source_target_pairs={{0,8},{1,9},{2,10},{3,11},{4,12},{5,13},{6,14},{7,15},{8,0},{9,1},... | collective-permute-start | bytes 294920 | tf_op jit(solution)/shard_map/ppermute | solution.py:339
  34.6 2.9 %collective-permute-start.11 = (f32[96,256]{1,0:T(8,128)S(1)}, f32[96,256]{1,0:T(8,128)S(1)}, u32[]{:S(2)}, u32[]{:S(2)}) collective-permute-start(f32[96,256]{1,0:T(8,128)S(1)} %get-tuple-element.25), channel_id=1, source_target_pairs={{0,12},{1,13},{2,14},{3,15},{4,0},{5,1},{6,2},{7,3},{8,4},{9,5},{1... | collective-permute-start | bytes 294920 | tf_op jit(solution)/shard_map/ppermute | solution.py:339
  37.9 3.6 %collective-permute-done.10.refs_2_ = f32[96,256]{1,0:T(8,128)S(1)} collective-permute-done((f32[96,256]{1,0:T(8,128)S(1)}, f32[96,256]{1,0:T(8,128)S(1)}, u32[]{:S(2)}, u32[]{:S(2)}) %collective-permute-start.10) | collective-permute-done | bytes 98336 | tf_op jit(solution)/shard_map/ppermute | solution.py:339
  41.6 3.5 %collective-permute-done.9.refs_1_ = f32[96,256]{1,0:T(8,128)S(1)} collective-permute-done((f32[96,256]{1,0:T(8,128)S(1)}, f32[96,256]{1,0:T(8,128)S(1)}, u32[]{:S(2)}, u32[]{:S(2)}) %collective-permute-start.9) | collective-permute-done | bytes 98336 | tf_op jit(solution)/shard_map/ppermute | solution.py:339
  45.2 2.5 %collective-permute-start.13 = (f32[96,256]{1,0:T(8,128)S(1)}, f32[96,256]{1,0:T(8,128)S(1)}, u32[]{:S(2)}, u32[]{:S(2)}) collective-permute-start(f32[96,256]{1,0:T(8,128)S(1)} %shard_map.82.refs_0_), channel_id=1, source_target_pairs={{0,8},{1,9},{2,10},{3,11},{4,12},{5,13},{6,14},{7,15},{8,0},{9,1},... | collective-permute-start | bytes 294920 | tf_op jit(solution)/shard_map/ppermute | solution.py:339
  47.7 1.4 %collective-permute-start.14 = (f32[96,256]{1,0:T(8,128)S(1)}, f32[96,256]{1,0:T(8,128)S(1)}, u32[]{:S(2)}, u32[]{:S(2)}) collective-permute-start(f32[96,256]{1,0:T(8,128)S(1)} %shard_map.82.refs_0_), channel_id=1, source_target_pairs={{0,12},{1,13},{2,14},{3,15},{4,0},{5,1},{6,2},{7,3},{8,4},{9,5},{1... | collective-permute-start | bytes 294920 | tf_op jit(solution)/shard_map/ppermute | solution.py:339
  50.7 7.2 %collective-permute-done.13.refs_2_ = f32[96,256]{1,0:T(8,128)S(1)} collective-permute-done((f32[96,256]{1,0:T(8,128)S(1)}, f32[96,256]{1,0:T(8,128)S(1)}, u32[]{:S(2)}, u32[]{:S(2)}) %collective-permute-start.13) | collective-permute-done | bytes 98336 | tf_op jit(solution)/shard_map/ppermute | solution.py:339
  57.9 1.1 %collective-permute-start.17 = (f32[96,256]{1,0:T(8,128)S(1)}, f32[96,256]{1,0:T(8,128)S(1)}, u32[]{:S(2)}, u32[]{:S(2)}) collective-permute-start(f32[96,256]{1,0:T(8,128)S(1)} %collective-permute-done.13.refs_2_), channel_id=1, source_target_pairs={{0,2},{1,3},{2,0},{3,1},{4,6},{5,7},{6,4},{7,5},{8,10},{9,11},{10,... | collective-permute-start | bytes 294920 | tf_op jit(solution)/shard_map/ppermute | solution.py:339
  59.0 0.9 %collective-permute-start.18 = (f32[96,256]{1,0:T(8,128)S(1)}, f32[96,256]{1,0:T(8,128)S(1)}, u32[]{:S(2)}, u32[]{:S(2)}) collective-permute-start(f32[96,256]{1,0:T(8,128)S(1)} %collective-permute-done.14.refs_3_), channel_id=1, source_target_pairs={{0,2},{1,3},{2,0},{3,1},{4,6},{5,7},{6,4},{7,5},{8,10},{9,11},{10,... | collective-permute-start | bytes 294920 | tf_op jit(solution)/shard_map/ppermute | solution.py:339
  60.5 2.0 %collective-permute-done.17.refs_6_ = f32[96,256]{1,0:T(8,128)S(1)} collective-permute-done((f32[96,256]{1,0:T(8,128)S(1)}, f32[96,256]{1,0:T(8,128)S(1)}, u32[]{:S(2)}, u32[]{:S(2)}) %collective-permute-start.17) | collective-permute-done | bytes 98336 | tf_op jit(solution)/shard_map/ppermute | solution.py:339
  62.5 1.1 %collective-permute-done.18.refs_7_ = f32[96,256]{1,0:T(8,128)S(1)} collective-permute-done((f32[96,256]{1,0:T(8,128)S(1)}, f32[96,256]{1,0:T(8,128)S(1)}, u32[]{:S(2)}, u32[]{:S(2)}) %collective-permute-start.18) | collective-permute-done | bytes 98336 | tf_op jit(solution)/shard_map/ppermute | solution.py:339
  65.5 3.4 %shard_map.83 = (f32[2,3,2,16,256]{4,3,2,1,0:T(8,128)}, f32[2,64,64]{2,1,0:T(8,128)}) custom-call(s32[1]{0:T(128)} %bitcast.place_ref, s32[3]{0:T(128)S(1)} %copy-done.1, s32[2]{0:T(128)S(1)} %copy-done.2, s32[1]{0:T(128)S(6)} %copy.10.block_ref, bf16[256,1536]{1,0:T(8,128)(2,1)S(1)} %get-tuple-element.14.b_high, ...), custom_call_target="tpu_custom_call" | custom-call | flops 150994944 | bytes 3637276 | tf_op jit(solution)/shard_map/pallas_call | solution.py:315
  (53 shorter events, 5.3 us)
Async XLA Ops:
  2.2 13.0 %collective-permute-start.2 = (f32[2,3,64,256]{3,2,1,0:T(8,128)S(1)}, f32[2,3,64,256]{3,2,1,0:T(8,128)S(1)}, u32[]{:S(2)}, u32[]{:S(2)}) collective-permute-start(f32[2,3,64,256]{3,2,1,0:T(8,128)S(1)} %get-tuple-element.29), channel_id=1, source_target_pairs={{0,2},{1,3},{2,0},{3,1},{4,6},{5,7},{6,4},{7,5},{8,10},{9,11},{10,... | collective-permute-start | bytes 1179656 | tf_op jit(solution)/shard_map/ppermute | solution.py:339
  5.3 20.6 %collective-permute-start.4 = (f32[2,3,64,256]{3,2,1,0:T(8,128)S(1)}, f32[2,3,64,256]{3,2,1,0:T(8,128)S(1)}, u32[]{:S(2)}, u32[]{:S(2)}) collective-permute-start(f32[2,3,64,256]{3,2,1,0:T(8,128)S(1)} %get-tuple-element.26.v0_ref.va_ref), channel_id=1, source_target_pairs={{0,12},{1,13},{2,6},{3,7},{4,0},{5,1},{6,10},{7,11},{8,4},{9,5},{1... | collective-permute-start | bytes 1179656 | tf_op jit(solution)/shard_map/ppermute | solution.py:339
  8.9 19.5 %collective-permute-start = (f32[2,3,64,256]{3,2,1,0:T(8,128)S(1)}, f32[2,3,64,256]{3,2,1,0:T(8,128)S(1)}, u32[]{:S(2)}, u32[]{:S(2)}) collective-permute-start(f32[2,3,64,256]{3,2,1,0:T(8,128)S(1)} %get-tuple-element.27), channel_id=1, source_target_pairs={{0,2},{1,3},{2,0},{3,1},{4,6},{5,7},{6,4},{7,5},{8,10},{9,11},{10,... | collective-permute-start | bytes 1179656 | tf_op jit(solution)/shard_map/ppermute | solution.py:339
  8.9 19.5 %collective-permute-start.1 = (f32[2,3,64,256]{3,2,1,0:T(8,128)S(1)}, f32[2,3,64,256]{3,2,1,0:T(8,128)S(1)}, u32[]{:S(2)}, u32[]{:S(2)}) collective-permute-start(f32[2,3,64,256]{3,2,1,0:T(8,128)S(1)} %get-tuple-element.28.v1_ref.va_ref), channel_id=1, source_target_pairs={{0,12},{1,13},{2,6},{3,7},{4,0},{5,1},{6,10},{7,11},{8,4},{9,5},{1... | collective-permute-start | bytes 1179656 | tf_op jit(solution)/shard_map/ppermute | solution.py:339
  10.7 15.1 %collective-permute-start.5 = (f32[108,128]{1,0:T(8,128)S(1)}, f32[108,128]{1,0:T(8,128)S(1)}, u32[]{:S(2)}, u32[]{:S(2)}) collective-permute-start(f32[108,128]{1,0:T(8,128)S(1)} %reshape.10.link_ref.link_a), channel_id=1, source_target_pairs={{0,2},{1,3},{2,0},{3,1},{4,6},{5,7},{6,4},{7,5},{8,10},{9,11},{10,... | collective-permute-start | bytes 165896 | tf_op jit(solution)/shard_map/ppermute | solution.py:339
  15.2 10.6 %collective-permute-start.6 = (f32[36,128]{1,0:T(8,128)S(1)}, f32[36,128]{1,0:T(8,128)S(1)}, u32[]{:S(2)}, u32[]{:S(2)}) collective-permute-start(f32[36,128]{1,0:T(8,128)S(1)} %reshape.11), channel_id=1, source_target_pairs={{0,12},{1,13},{2,6},{3,7},{4,0},{5,1},{6,10},{7,11},{8,4},{9,5},{1... | collective-permute-start | bytes 55304 | tf_op jit(solution)/shard_map/ppermute | solution.py:339
  25.8 2.6 %collective-permute-start.3 = (f32[2,3,16,256]{3,2,1,0:T(8,128)S(1)}, f32[2,3,16,256]{3,2,1,0:T(8,128)S(1)}, u32[]{:S(2)}, u32[]{:S(2)}) collective-permute-start(f32[2,3,16,256]{3,2,1,0:T(8,128)S(1)} %slice.12), channel_id=1, source_target_pairs={{0,1},{1,0},{2,3},{3,2},{4,5},{5,4},{6,7},{7,6},{8,9},{9,8},{10,11... | collective-permute-start | bytes 294920 | tf_op jit(solution)/shard_map/ppermute | solution.py:339
  31.1 1.9 %collective-permute-start.8 = (f32[384,256]{1,0:T(8,128)S(1)}, f32[384,256]{1,0:T(8,128)S(1)}, u32[]{:S(2)}, u32[]{:S(2)}) collective-permute-start(f32[384,256]{1,0:T(8,128)S(1)} %get-tuple-element.21), channel_id=1, source_target_pairs={{0,1},{1,0},{2,3},{3,2},{4,5},{5,4},{6,7},{7,6},{8,9},{9,8},{10,11... | collective-permute-start | bytes 1179656 | tf_op jit(solution)/shard_map/ppermute | solution.py:339
  33.0 8.5 %collective-permute-start.10 = (f32[96,256]{1,0:T(8,128)S(1)}, f32[96,256]{1,0:T(8,128)S(1)}, u32[]{:S(2)}, u32[]{:S(2)}) collective-permute-start(f32[96,256]{1,0:T(8,128)S(1)} %get-tuple-element.24), channel_id=1, source_target_pairs={{0,8},{1,9},{2,10},{3,11},{4,12},{5,13},{6,14},{7,15},{8,0},{9,1},... | collective-permute-start | bytes 294920 | tf_op jit(solution)/shard_map/ppermute | solution.py:339
  34.6 7.0 %collective-permute-start.11 = (f32[96,256]{1,0:T(8,128)S(1)}, f32[96,256]{1,0:T(8,128)S(1)}, u32[]{:S(2)}, u32[]{:S(2)}) collective-permute-start(f32[96,256]{1,0:T(8,128)S(1)} %get-tuple-element.25), channel_id=1, source_target_pairs={{0,12},{1,13},{2,14},{3,15},{4,0},{5,1},{6,2},{7,3},{8,4},{9,5},{1... | collective-permute-start | bytes 294920 | tf_op jit(solution)/shard_map/ppermute | solution.py:339
  37.4 7.6 %collective-permute-start.9 = (f32[96,256]{1,0:T(8,128)S(1)}, f32[96,256]{1,0:T(8,128)S(1)}, u32[]{:S(2)}, u32[]{:S(2)}) collective-permute-start(f32[96,256]{1,0:T(8,128)S(1)} %get-tuple-element.23), channel_id=1, source_target_pairs={{0,4},{1,5},{2,6},{3,7},{4,8},{5,9},{6,10},{7,11},{8,12},{9,13},{1... | collective-permute-start | bytes 294920 | tf_op jit(solution)/shard_map/ppermute | solution.py:339
  45.1 4.7 %collective-permute-start.15 = (f32[96,256]{1,0:T(8,128)S(1)}, f32[96,256]{1,0:T(8,128)S(1)}, u32[]{:S(2)}, u32[]{:S(2)}) collective-permute-start(f32[96,256]{1,0:T(8,128)S(1)} %shard_map.82.refs_0_), channel_id=1, source_target_pairs={{0,2},{1,3},{2,0},{3,1},{4,6},{5,7},{6,4},{7,5},{8,10},{9,11},{10,... | collective-permute-start | bytes 294920 | tf_op jit(solution)/shard_map/ppermute | solution.py:339
  45.2 12.7 %collective-permute-start.13 = (f32[96,256]{1,0:T(8,128)S(1)}, f32[96,256]{1,0:T(8,128)S(1)}, u32[]{:S(2)}, u32[]{:S(2)}) collective-permute-start(f32[96,256]{1,0:T(8,128)S(1)} %shard_map.82.refs_0_), channel_id=1, source_target_pairs={{0,8},{1,9},{2,10},{3,11},{4,12},{5,13},{6,14},{7,15},{8,0},{9,1},... | collective-permute-start | bytes 294920 | tf_op jit(solution)/shard_map/ppermute | solution.py:339
  47.7 11.3 %collective-permute-start.14 = (f32[96,256]{1,0:T(8,128)S(1)}, f32[96,256]{1,0:T(8,128)S(1)}, u32[]{:S(2)}, u32[]{:S(2)}) collective-permute-start(f32[96,256]{1,0:T(8,128)S(1)} %shard_map.82.refs_0_), channel_id=1, source_target_pairs={{0,12},{1,13},{2,14},{3,15},{4,0},{5,1},{6,2},{7,3},{8,4},{9,5},{1... | collective-permute-start | bytes 294920 | tf_op jit(solution)/shard_map/ppermute | solution.py:339
  49.1 10.9 %collective-permute-start.12 = (f32[96,256]{1,0:T(8,128)S(1)}, f32[96,256]{1,0:T(8,128)S(1)}, u32[]{:S(2)}, u32[]{:S(2)}) collective-permute-start(f32[96,256]{1,0:T(8,128)S(1)} %shard_map.82.refs_0_), channel_id=1, source_target_pairs={{0,4},{1,5},{2,6},{3,7},{4,8},{5,9},{6,10},{7,11},{8,12},{9,13},{1... | collective-permute-start | bytes 294920 | tf_op jit(solution)/shard_map/ppermute | solution.py:339
  49.7 10.2 %collective-permute-start.19 = (f32[96,256]{1,0:T(8,128)S(1)}, f32[96,256]{1,0:T(8,128)S(1)}, u32[]{:S(2)}, u32[]{:S(2)}) collective-permute-start(f32[96,256]{1,0:T(8,128)S(1)} %shard_map.82.refs_0_), channel_id=1, source_target_pairs={{0,1},{1,0},{2,3},{3,2},{4,5},{5,4},{6,7},{7,6},{8,9},{9,8},{10,11... | collective-permute-start | bytes 294920 | tf_op jit(solution)/shard_map/ppermute | solution.py:339
  49.8 10.7 %collective-permute-start.16 = (f32[96,256]{1,0:T(8,128)S(1)}, f32[96,256]{1,0:T(8,128)S(1)}, u32[]{:S(2)}, u32[]{:S(2)}) collective-permute-start(f32[96,256]{1,0:T(8,128)S(1)} %collective-permute-done.15.refs_4_), channel_id=1, source_target_pairs={{0,4},{1,5},{2,6},{3,7},{4,8},{5,9},{6,10},{7,11},{8,12},{9,13},{1... | collective-permute-start | bytes 294920 | tf_op jit(solution)/shard_map/ppermute | solution.py:339
  57.9 4.6 %collective-permute-start.17 = (f32[96,256]{1,0:T(8,128)S(1)}, f32[96,256]{1,0:T(8,128)S(1)}, u32[]{:S(2)}, u32[]{:S(2)}) collective-permute-start(f32[96,256]{1,0:T(8,128)S(1)} %collective-permute-done.13.refs_2_), channel_id=1, source_target_pairs={{0,2},{1,3},{2,0},{3,1},{4,6},{5,7},{6,4},{7,5},{8,10},{9,11},{10,... | collective-permute-start | bytes 294920 | tf_op jit(solution)/shard_map/ppermute | solution.py:339
  59.0 4.6 %collective-permute-start.18 = (f32[96,256]{1,0:T(8,128)S(1)}, f32[96,256]{1,0:T(8,128)S(1)}, u32[]{:S(2)}, u32[]{:S(2)}) collective-permute-start(f32[96,256]{1,0:T(8,128)S(1)} %collective-permute-done.14.refs_3_), channel_id=1, source_target_pairs={{0,2},{1,3},{2,0},{3,1},{4,6},{5,7},{6,4},{7,5},{8,10},{9,11},{10,... | collective-permute-start | bytes 294920 | tf_op jit(solution)/shard_map/ppermute | solution.py:339
  60.0 3.7 %collective-permute-start.20 = (f32[96,256]{1,0:T(8,128)S(1)}, f32[96,256]{1,0:T(8,128)S(1)}, u32[]{:S(2)}, u32[]{:S(2)}) collective-permute-start(f32[96,256]{1,0:T(8,128)S(1)} %collective-permute-done.12.refs_1_), channel_id=1, source_target_pairs={{0,1},{1,0},{2,3},{3,2},{4,5},{5,4},{6,7},{7,6},{8,9},{9,8},{10,11... | collective-permute-start | bytes 294920 | tf_op jit(solution)/shard_map/ppermute | solution.py:339
  60.0 4.2 %collective-permute-start.21 = (f32[96,256]{1,0:T(8,128)S(1)}, f32[96,256]{1,0:T(8,128)S(1)}, u32[]{:S(2)}, u32[]{:S(2)}) collective-permute-start(f32[96,256]{1,0:T(8,128)S(1)} %collective-permute-done.13.refs_2_), channel_id=1, source_target_pairs={{0,1},{1,0},{2,3},{3,2},{4,5},{5,4},{6,7},{7,6},{8,9},{9,8},{10,11... | collective-permute-start | bytes 294920 | tf_op jit(solution)/shard_map/ppermute | solution.py:339
  60.5 4.6 %collective-permute-start.22 = (f32[96,256]{1,0:T(8,128)S(1)}, f32[96,256]{1,0:T(8,128)S(1)}, u32[]{:S(2)}, u32[]{:S(2)}) collective-permute-start(f32[96,256]{1,0:T(8,128)S(1)} %collective-permute-done.14.refs_3_), channel_id=1, source_target_pairs={{0,1},{1,0},{2,3},{3,2},{4,5},{5,4},{6,7},{7,6},{8,9},{9,8},{10,11... | collective-permute-start | bytes 294920 | tf_op jit(solution)/shard_map/ppermute | solution.py:339
  62.5 2.5 %collective-permute-start.23 = (f32[96,256]{1,0:T(8,128)S(1)}, f32[96,256]{1,0:T(8,128)S(1)}, u32[]{:S(2)}, u32[]{:S(2)}) collective-permute-start(f32[96,256]{1,0:T(8,128)S(1)} %collective-permute-done.15.refs_4_), channel_id=1, source_target_pairs={{0,1},{1,0},{2,3},{3,2},{4,5},{5,4},{6,7},{7,6},{8,9},{9,8},{10,11... | collective-permute-start | bytes 294920 | tf_op jit(solution)/shard_map/ppermute | solution.py:339
  63.7 1.5 %collective-permute-start.25 = (f32[96,256]{1,0:T(8,128)S(1)}, f32[96,256]{1,0:T(8,128)S(1)}, u32[]{:S(2)}, u32[]{:S(2)}) collective-permute-start(f32[96,256]{1,0:T(8,128)S(1)} %collective-permute-done.17.refs_6_), channel_id=1, source_target_pairs={{0,1},{1,0},{2,3},{3,2},{4,5},{5,4},{6,7},{7,6},{8,9},{9,8},{10,11... | collective-permute-start | bytes 294920 | tf_op jit(solution)/shard_map/ppermute | solution.py:339
  (7 other events, 115.0 us)

commit v6 on v5

--- a/solution.py
+++ b/solution.py
@@ -128,16 +128,25 @@
         out_ref[i] = contract(left_ref, right_ref.at[i])
 
 
-def chunk(va_ref, vb_ref, vc_ref, coef, start, ahead, left_ref, right_ref):
-    sites = vb_ref.shape[2]
-    store_left(lambda p, c: vb_ref[p, c], left_ref)
+def fill(right_ref, sites, sources):
     for row in range(sites // LZ):
+        store_right(right_ref, row, sites, sources(row))
+
+
+def crossing(va_ref, vc_ref, coef, start):
+    def sources(row):
         here = coef[start + row * LZ : start + (row + 1) * LZ]
-        along = [(here, 56, row_of(va_ref, row), False), (here, 80, row_of(vc_ref, row), False)]
-        store_right(right_ref.at[0], row, sites, along)
-        store_right(right_ref.at[1], row, sites, ahead(row, here))
-        store_right(right_ref.at[2], row, sites, [(here, 36, row_of(vb_ref, row, True), False)])
-    return [contract(left_ref, right_ref.at[i]) for i in range(3)]
+        return [(here, 56, row_of(va_ref, row), False), (here, 80, row_of(vc_ref, row), False)]
+
+    return sources
+
+
+def turning(vb_ref, coef, start):
+    def sources(row):
+        here = coef[start + row * LZ : start + (row + 1) * LZ]
+        return [(here, 36, row_of(vb_ref, row, True), False)]
+
+    return sources
 
 
 def first_kernel(place_ref, va_ref, vb_ref, vc_ref, link_a, link_b, link_c, own_ref,
@@ -154,40 +163,63 @@
     turned_ref[...] = coef_ref[...].T
     coef = turned_ref[...]
 
-    def ahead(row, here):
+    sites = rows * LZ
+
+    def ahead(row):
+        here = coef[row * LZ : (row + 1) * LZ]
         return [(here, 18, row_of(vb_ref, row + 1), False)] if row + 1 < rows else []
 
-    sums = chunk(va_ref, vb_ref, vc_ref, coef, 0, ahead, left_ref, right_ref)
-    for i, value in enumerate(sums):
+    store_left(lambda p, c: vb_ref[p, c], left_ref)
+    fill(right_ref.at[0], sites, crossing(va_ref, vc_ref, coef, 0))
+    fill(right_ref.at[1], sites, ahead)
+    fill(right_ref.at[2], sites, turning(vb_ref, coef, 0))
+    for i in range(3):
+        value = contract(left_ref, right_ref.at[i])
         out_ref[i * width : (i + 1) * width, :] = value + own_ref[i - 1] if i else value
 
 
-def last_kernel(place_ref, va_ref, vb_ref, vc_ref, before_ref, halo_ref, turned_ref, first_ref,
-                keep_ref, send_ref, left_ref, right_ref, total_ref):
+def inner_kernel(place_ref, vb_ref, before_ref, halo_ref, turned_ref, first_ref,
+                 keep_ref, send_ref, left_ref, right_ref, both_ref):
     sites, width = vb_ref.shape[2], vb_ref.shape[3]
     rows = sites // LZ
     coef = turned_ref[...]
 
-    def ahead(row, here):
+    def ahead(row):
+        here = coef[sites + row * LZ : sites + (row + 1) * LZ]
         field = row_of(vb_ref, row + 1) if row + 1 < rows else row_of(halo_ref, 0)
         out = [(here, 18, field, False)]
         if row == 0:
             out.append((coef[sites - LZ : sites], 18, row_of(before_ref, rows - 1), True))
         return out
 
-    sums = chunk(va_ref, vb_ref, vc_ref, coef, sites, ahead, left_ref, right_ref)
-    for i, value in enumerate(sums):
-        at = slice(i * width, (i + 1) * width)
-        total_ref[at, :] = value + first_ref[at, :]
+    store_left(lambda p, c: vb_ref[p, c], left_ref)
+    fill(right_ref.at[0], sites, ahead)
+    fill(right_ref.at[1], sites, turning(vb_ref, coef, sites))
+    for i in range(2):
+        value = contract(left_ref, right_ref.at[i])
+        at = slice((i + 1) * width, (i + 2) * width)
+        both_ref[i * width : (i + 1) * width, :] = value + first_ref[at, :]
     core = place_ref[0] % 2
-    half = 3 * width // 2
+    keep_ref[...] = both_ref[pl.ds(pl.multiple_of(core * width, 8), width), :]
+    send_ref[...] = both_ref[pl.ds(pl.multiple_of((1 - core) * width, 8), width), :]
+
+
+def last_kernel(place_ref, va_ref, vc_ref, left_ref, turned_ref, first_ref,
+                keep_ref, send_ref, right_ref, total_ref):
+    sites, width = va_ref.shape[2], va_ref.shape[3]
+    fill(right_ref, sites, crossing(va_ref, vc_ref, turned_ref[...], sites))
+    total_ref[...] = contract(left_ref, right_ref) + first_ref[:width, :]
+    core = place_ref[0] % 2
+    half = width // 2
     keep_ref[...] = total_ref[pl.ds(pl.multiple_of(core * half, 8), half), :]
     send_ref[...] = total_ref[pl.ds(pl.multiple_of((1 - core) * half, 8), half), :]
 
 
-def spread_kernel(place_ref, keep_ref, got_ref, *refs):
+def spread_kernel(place_ref, keep_ref, got_ref, keep_x_ref, got_x_ref, *refs):
     outs, total_ref = refs[:-1], refs[-1]
-    total_ref[...] = keep_ref[...] + got_ref[...]
+    width = keep_ref.shape[0]
+    total_ref[:width, :] = keep_ref[...] + got_ref[...]
+    total_ref[width:, :] = keep_x_ref[...] + got_x_ref[...]
     count = len(outs)
     size = outs[0].shape[0]
     pair = place_ref[0] // 4
@@ -267,23 +299,33 @@
     rows = elem_ref.shape[3]
     first = place * rows
     lane = pl.multiple_of((first // 128) * 128, 128)
+    block = width // 2
+
+    def start(time, way, h):
+        inside = jnp.where(way == 0, h * half + width, (way - 1) * half + h * block)
+        return time * 2 * half + inside
+
     for i in range(6):
-        block = all_ref[i * width : (i + 1) * width, pl.ds(lane, 128)]
-        turn_ref[i * 128 : (i + 1) * 128, :] = block.T
+        for h in range(2):
+            core, at = (h, width) if i % 3 == 0 else (i % 3 - 1, h * block)
+            at += (i // 3 * 2 + core) * half
+            piece = all_ref[at : at + block, pl.ds(lane, 128)]
+            turn_ref[i * 128 : (i + 1) * 128, h * block : (h + 1) * block] = piece.T
     inner = lax.rem(first, 128)
     for g in range(2):
         time = jnp.where(slice_ref[0] == g, 0, 1)
         for k in range(3):
-            which = time * 3 + direct_ref[k]
-            row = take(all_ref, which * width + first, rows)
+            way = direct_ref[k]
+            which = time * 3 + way
+            row = take(all_ref, start(time, way, first // block) + lax.rem(first, block), rows)
             col = take(turn_ref, which * 128 + inner, rows)
             elem_ref[g, k, 0] = 0.5 * (row - col)
             elem_ref[g, k, 1] = 0.5 * (row + col)
     time = jnp.where(slice_ref[0] == block_ref[0], 0, 1)
     turned = None
     for k in range(3):
-        at = pl.multiple_of((time * 3 + direct_ref[k]) * width, 8)
-        parts = split(all_ref[pl.ds(at, width), :])
+        places = [pl.multiple_of(start(time, direct_ref[k], h), 8) for h in range(2)]
+        parts = split(jnp.concatenate([all_ref[pl.ds(at, block), :] for at in places], axis=0))
         one = slice(k * width, (k + 1) * width)
         two = slice((3 + k) * width, (4 + k) * width)
         term = dot3((b_high[:, one], b_low[:, one]), parts, NT_DIMS) + dot3(
@@ -387,14 +429,20 @@
         first_kernel, (shape(3 * width, width), shape(sites, 128)),
         (places, mine[0], vec_b[0], vec_c[0], flat, link_b, link_c, own), scalars=1,
         scratch=(left(part), right(3, part), coef), flops=2 * work)
-    keep, give = call(
-        last_kernel, (shape(half, width),) * 2,
-        (places, mine[1], vec_b[1], vec_c[1], vec_b[0], halo_b, turned, first), scalars=1,
-        scratch=(left(part), right(3, part), pltpu.VMEM((3 * width, width), jnp.float32)),
-        flops=2 * work)
+    keep, give, turned_left = call(
+        inner_kernel,
+        (shape(width, width),) * 2 + (shape(2, 2 * width, 6 * part, dtype=bf16),),
+        (places, vec_b[1], vec_b[0], halo_b, turned, first), scalars=1,
+        scratch=(right(2, part), pltpu.VMEM((2 * width, width), jnp.float32)), flops=2 * work)
     got = send(give, twin)
+    keep_x, give_x = call(
+        last_kernel, (shape(width // 2, width),) * 2,
+        (places, mine[1], vec_c[1], turned_left, turned, first), scalars=1,
+        scratch=(pltpu.VMEM((2, 6 * part, width), bf16),
+                 pltpu.VMEM((width, width), jnp.float32)), flops=2 * work)
+    got_x = send(give_x, twin)
     size = half // pairs
-    spread = call(spread_kernel, (shape(size, width),) * pairs, (places, keep, got), scalars=1,
+    spread = call(spread_kernel, (shape(size, width),) * pairs, (places, keep, got, keep_x, got_x), scalars=1,
                   scratch=(pltpu.VMEM((half, width), jnp.float32),))
 
     parts = [spread[0]] + [send(spread[d], shift(d)) for d in range(1, pairs)]

time: 69 us -> 67.9 us (0.984)
  the two profiles are of different devices: /device:TPU:0 before, /device:TPU:13 now
where the time goes in v6:
time: 67.9 us; the launch traced here: 67.7 us
  starting transfers between devices  31.5 us (46%)
  waiting for transfers between devices  20.7 us (30%)
  Pallas kernels  12.5 us (18%)
  local copies, waits for them, and re-layouts  1.63 us (2%)
  between operations  1.52 us (2%)
    ppermute x28, starting transfers between devices, send(): return lax.ppermute(value, 'space', route)  31.5 us
    ppermute x28, waiting for transfers between devices, send(): return lax.ppermute(value, 'space', route)  20.7 us
    pallas_call x8, Pallas kernels, call(): pl.pallas_call(kernel, out_shape=out, in_specs=[SMEM] * scalars + [VMEM]...  12.5 us
    squeeze x1, local copies, waits for them, and re-layouts, cut(): return lax.dynamic_slice(vectors, (time, 0, 0, i * part, 0), block)[0]  1.51 us
  transfers between devices with their start and end apart: 28, of which 10 were waited for; matrix products, arithmetic and copies ran while one was open for 0% of the time, Pallas kernels for 13%

profile of v6, /device:TPU:13, one launch (start us, length us, event | category | flops | bytes accessed | tf_op | source)
XLA Modules:
  0.0 67.7 jit_solution(2740795047021339941)
XLA Ops:
  0.7 1.5 %dynamic-slice_bitcast_fusion = (f32[2,3,64,256]{3,2,1,0:T(8,128)S(1)}, f32[2,3,64,256]{3,2,1,0:T(8,128)S(1)}, f32[2,3,64,256]{3,2,1,0:T(8,128)S(1)}, f32[2,3,64,256]{3,2,1,0:T(8,128)S(1)}) fusion(f32[2,2,3,128,256]{4,3,2,1,0:T(8,128)} %param.6, s32[]{:T(128)S(6)} %select_n.22, s32[]{:T(128)S(6)} %select_n.21), kind=kLoop, calls=%fused_computation | loop fusion | bytes 3145736 | tf_op jit(solution)/shard_map/squeeze | solution.py:395
  3.9 1.6 %collective-permute-start.6 = (f32[2,3,16,256]{3,2,1,0:T(8,128)S(1)}, f32[2,3,16,256]{3,2,1,0:T(8,128)S(1)}, u32[]{:S(2)}, u32[]{:S(2)}) collective-permute-start(f32[2,3,16,256]{3,2,1,0:T(8,128)S(1)} %slice.14), channel_id=1, source_target_pairs={{0,1},{1,0},{2,3},{3,2},{4,5},{5,4},{6,7},{7,6},{8,9},{9,8},{10,11... | collective-permute-start | bytes 294920 | tf_op jit(solution)/shard_map/ppermute | solution.py:381
  5.5 1.3 %collective-permute-start.8 = (f32[2,3,64,256]{3,2,1,0:T(8,128)S(1)}, f32[2,3,64,256]{3,2,1,0:T(8,128)S(1)}, u32[]{:S(2)}, u32[]{:S(2)}) collective-permute-start(f32[2,3,64,256]{3,2,1,0:T(8,128)S(1)} %get-tuple-element.32.v1_ref.va_ref), channel_id=1, source_target_pairs={{0,12},{1,13},{2,6},{3,7},{4,0},{5,1},{6,10},{7,11},{8,4},{9,5},{1... | collective-permute-start | bytes 1179656 | tf_op jit(solution)/shard_map/ppermute | solution.py:381
  6.9 1.8 %collective-permute-start.4 = (f32[108,128]{1,0:T(8,128)S(1)}, f32[108,128]{1,0:T(8,128)S(1)}, u32[]{:S(2)}, u32[]{:S(2)}) collective-permute-start(f32[108,128]{1,0:T(8,128)S(1)} %reshape.10.link_ref.link_a), channel_id=1, source_target_pairs={{0,2},{1,3},{2,0},{3,1},{4,6},{5,7},{6,4},{7,5},{8,10},{9,11},{10,... | collective-permute-start | bytes 165896 | tf_op jit(solution)/shard_map/ppermute | solution.py:381
  8.7 3.5 %collective-permute-done.1.vb_ref.before_ref = f32[2,3,64,256]{3,2,1,0:T(8,128)S(1)} collective-permute-done((f32[2,3,64,256]{3,2,1,0:T(8,128)S(1)}, f32[2,3,64,256]{3,2,1,0:T(8,128)S(1)}, u32[]{:S(2)}, u32[]{:S(2)}) %collective-permute-start.1) | collective-permute-done | bytes 393248 | tf_op jit(solution)/shard_map/ppermute | solution.py:381
  12.3 1.3 %collective-permute-start.5 = (f32[36,128]{1,0:T(8,128)S(1)}, f32[36,128]{1,0:T(8,128)S(1)}, u32[]{:S(2)}, u32[]{:S(2)}) collective-permute-start(f32[36,128]{1,0:T(8,128)S(1)} %reshape.11), channel_id=1, source_target_pairs={{0,12},{1,13},{2,6},{3,7},{4,0},{5,1},{6,10},{7,11},{8,4},{9,5},{1... | collective-permute-start | bytes 55304 | tf_op jit(solution)/shard_map/ppermute | solution.py:381
  13.6 2.9 %shard_map.78.own_ref = f32[2,256,256]{2,1,0:T(8,128)S(1)} custom-call(s32[1]{0:T(128)} %bitcast.place_ref, f32[2,3,64,256]{3,2,1,0:T(8,128)S(1)} %get-tuple-element.35.v0_ref.va_ref, f32[2,3,64,256]{3,2,1,0:T(8,128)S(1)} %get-tuple-element.32.v1_ref.va_ref, f32[2,3,16,256]{3,2,1,0:T(8,128)S(1)} %collective-permute-done.6.halo_ref, ...), custom_call_target="tpu_custom_call" | custom-call | flops 1207959552 | bytes 1464324 | tf_op jit(solution)/shard_map/pallas_call | solution.py:357
  16.5 4.6 %collective-permute-done.5.link_c = f32[36,128]{1,0:T(8,128)S(1)} collective-permute-done((f32[36,128]{1,0:T(8,128)S(1)}, f32[36,128]{1,0:T(8,128)S(1)}, u32[]{:S(2)}, u32[]{:S(2)}) %collective-permute-start.5) | collective-permute-done | bytes 18464 | tf_op jit(solution)/shard_map/ppermute | solution.py:381
  21.1 1.8 %collective-permute-start.2 = (f32[2,3,16,256]{3,2,1,0:T(8,128)S(1)}, f32[2,3,16,256]{3,2,1,0:T(8,128)S(1)}, u32[]{:S(2)}, u32[]{:S(2)}) collective-permute-start(f32[2,3,16,256]{3,2,1,0:T(8,128)S(1)} %slice.12), channel_id=1, source_target_pairs={{0,1},{1,0},{2,3},{3,2},{4,5},{5,4},{6,7},{7,6},{8,9},{9,8},{10,11... | collective-permute-start | bytes 294920 | tf_op jit(solution)/shard_map/ppermute | solution.py:381
  22.9 2.5 %shard_map.79 = (f32[768,256]{1,0:T(8,128)S(1)}, f32[128,128]{1,0:T(8,128)S(1)}) custom-call(s32[1]{0:T(128)} %bitcast.place_ref, f32[2,3,64,256]{3,2,1,0:T(8,128)S(1)} %get-tuple-element.35.v0_ref.va_ref, f32[2,3,64,256]{3,2,1,0:T(8,128)S(1)} %collective-permute-done.1.vb_ref.before_ref, f32[2,3,64,256]{3,2,1,0:T(8,128)S(1)} %collective-permute-done.3.vc_ref, ...), custom_call_target="tpu_custom_call" | custom-call | flops 1207959552 | bytes 2684932 | tf_op jit(solution)/shard_map/pallas_call | solution.py:357
  25.5 2.0 %shard_map.80 = (f32[256,256]{1,0:T(8,128)S(1)}, f32[256,256]{1,0:T(8,128)S(1)}, bf16[2,512,384]{2,1,0:T(8,128)(2,1)S(1)}) custom-call(s32[1]{0:T(128)} %bitcast.place_ref, f32[2,3,64,256]{3,2,1,0:T(8,128)S(1)} %collective-permute-done.vb_ref, f32[2,3,64,256]{3,2,1,0:T(8,128)S(1)} %collective-permute-done.1.vb_ref.before_ref, ...), custom_call_target="tpu_custom_call" | custom-call | flops 1207959552 | bytes 3047428 | tf_op jit(solution)/shard_map/pallas_call | solution.py:357
  28.1 1.3 %shard_map.81 = (f32[128,256]{1,0:T(8,128)S(1)}, f32[128,256]{1,0:T(8,128)S(1)}) custom-call(s32[1]{0:T(128)} %bitcast.place_ref, f32[2,3,64,256]{3,2,1,0:T(8,128)S(1)} %get-tuple-element.32.v1_ref.va_ref, f32[2,3,64,256]{3,2,1,0:T(8,128)S(1)} %collective-permute-done.8.vc_ref, bf16[2,512,384]{2,1,0:T(8,128)(2,1)S(1)} %get-tuple-element.25.left_ref, ...), custom_call_target="tpu_custom_call" | custom-call | flops 1207959552 | bytes 2686980 | tf_op jit(solution)/shard_map/pallas_call | solution.py:357
  29.6 1.3 %collective-permute-done.9.got_x_ref = f32[128,256]{1,0:T(8,128)S(1)} collective-permute-done((f32[128,256]{1,0:T(8,128)S(1)}, f32[128,256]{1,0:T(8,128)S(1)}, u32[]{:S(2)}, u32[]{:S(2)}) %collective-permute-start.9) | collective-permute-done | bytes 131104 | tf_op jit(solution)/shard_map/ppermute | solution.py:381
  31.0 1.4 %collective-permute-start.10 = (f32[96,256]{1,0:T(8,128)S(1)}, f32[96,256]{1,0:T(8,128)S(1)}, u32[]{:S(2)}, u32[]{:S(2)}) collective-permute-start(f32[96,256]{1,0:T(8,128)S(1)} %get-tuple-element.29), channel_id=1, source_target_pairs={{0,4},{1,5},{2,6},{3,7},{4,8},{5,9},{6,10},{7,11},{8,12},{9,13},{1... | collective-permute-start | bytes 294920 | tf_op jit(solution)/shard_map/ppermute | solution.py:381
  32.3 2.4 %collective-permute-start.11 = (f32[96,256]{1,0:T(8,128)S(1)}, f32[96,256]{1,0:T(8,128)S(1)}, u32[]{:S(2)}, u32[]{:S(2)}) collective-permute-start(f32[96,256]{1,0:T(8,128)S(1)} %get-tuple-element.30), channel_id=1, source_target_pairs={{0,8},{1,9},{2,10},{3,11},{4,12},{5,13},{6,14},{7,15},{8,0},{9,1},... | collective-permute-start | bytes 294920 | tf_op jit(solution)/shard_map/ppermute | solution.py:381
  35.5 5.8 %collective-permute-done.11.refs_2_ = f32[96,256]{1,0:T(8,128)S(1)} collective-permute-done((f32[96,256]{1,0:T(8,128)S(1)}, f32[96,256]{1,0:T(8,128)S(1)}, u32[]{:S(2)}, u32[]{:S(2)}) %collective-permute-start.11) | collective-permute-done | bytes 98336 | tf_op jit(solution)/shard_map/ppermute | solution.py:381
  41.3 1.5 %collective-permute-done.12.refs_3_ = f32[96,256]{1,0:T(8,128)S(1)} collective-permute-done((f32[96,256]{1,0:T(8,128)S(1)}, f32[96,256]{1,0:T(8,128)S(1)}, u32[]{:S(2)}, u32[]{:S(2)}) %collective-permute-start.12) | collective-permute-done | bytes 98336 | tf_op jit(solution)/shard_map/ppermute | solution.py:381
  42.8 2.9 %collective-permute-start.16 = (f32[96,256]{1,0:T(8,128)S(1)}, f32[96,256]{1,0:T(8,128)S(1)}, u32[]{:S(2)}, u32[]{:S(2)}) collective-permute-start(f32[96,256]{1,0:T(8,128)S(1)} %shard_map.83.refs_0_), channel_id=1, source_target_pairs={{0,2},{1,3},{2,0},{3,1},{4,6},{5,7},{6,4},{7,5},{8,10},{9,11},{10,... | collective-permute-start | bytes 294920 | tf_op jit(solution)/shard_map/ppermute | solution.py:381
  47.1 2.0 %collective-permute-start.20 = (f32[96,256]{1,0:T(8,128)S(1)}, f32[96,256]{1,0:T(8,128)S(1)}, u32[]{:S(2)}, u32[]{:S(2)}) collective-permute-start(f32[96,256]{1,0:T(8,128)S(1)} %shard_map.83.refs_0_), channel_id=1, source_target_pairs={{0,1},{1,0},{2,3},{3,2},{4,5},{5,4},{6,7},{7,6},{8,9},{9,8},{10,11... | collective-permute-start | bytes 294920 | tf_op jit(solution)/shard_map/ppermute | solution.py:381
  49.6 1.4 %collective-permute-done.14.refs_2_ = f32[96,256]{1,0:T(8,128)S(1)} collective-permute-done((f32[96,256]{1,0:T(8,128)S(1)}, f32[96,256]{1,0:T(8,128)S(1)}, u32[]{:S(2)}, u32[]{:S(2)}) %collective-permute-start.14) | collective-permute-done | bytes 98336 | tf_op jit(solution)/shard_map/ppermute | solution.py:381
  53.0 1.3 %collective-permute-done.13.refs_1_ = f32[96,256]{1,0:T(8,128)S(1)} collective-permute-done((f32[96,256]{1,0:T(8,128)S(1)}, f32[96,256]{1,0:T(8,128)S(1)}, u32[]{:S(2)}, u32[]{:S(2)}) %collective-permute-start.13) | collective-permute-done | bytes 98336 | tf_op jit(solution)/shard_map/ppermute | solution.py:381
  54.3 4.4 %collective-permute-start.21 = (f32[96,256]{1,0:T(8,128)S(1)}, f32[96,256]{1,0:T(8,128)S(1)}, u32[]{:S(2)}, u32[]{:S(2)}) collective-permute-start(f32[96,256]{1,0:T(8,128)S(1)} %collective-permute-done.13.refs_1_), channel_id=1, source_target_pairs={{0,1},{1,0},{2,3},{3,2},{4,5},{5,4},{6,7},{7,6},{8,9},{9,8},{10,11... | collective-permute-start | bytes 294920 | tf_op jit(solution)/shard_map/ppermute | solution.py:381
  59.4 3.5 %collective-permute-start.25 = (f32[96,256]{1,0:T(8,128)S(1)}, f32[96,256]{1,0:T(8,128)S(1)}, u32[]{:S(2)}, u32[]{:S(2)}) collective-permute-start(f32[96,256]{1,0:T(8,128)S(1)} %collective-permute-done.17.refs_5_), channel_id=1, source_target_pairs={{0,1},{1,0},{2,3},{3,2},{4,5},{5,4},{6,7},{7,6},{8,9},{9,8},{10,11... | collective-permute-start | bytes 294920 | tf_op jit(solution)/shard_map/ppermute | solution.py:381
  64.3 3.4 %shard_map.84 = (f32[2,3,2,16,256]{4,3,2,1,0:T(8,128)}, f32[2,64,64]{2,1,0:T(8,128)}) custom-call(s32[1]{0:T(128)} %bitcast.place_ref, s32[3]{0:T(128)S(1)} %copy-done.1, s32[2]{0:T(128)S(1)} %copy-done.2, s32[1]{0:T(128)S(6)} %copy.10.block_ref, bf16[256,1536]{1,0:T(8,128)(2,1)S(1)} %get-tuple-element.17.b_high, ...), custom_call_target="tpu_custom_call" | custom-call | flops 150994944 | bytes 3637276 | tf_op jit(solution)/shard_map/pallas_call | solution.py:357
  (56 shorter events, 8.7 us)
Async XLA Ops:
  2.2 10.1 %collective-permute-start.1 = (f32[2,3,64,256]{3,2,1,0:T(8,128)S(1)}, f32[2,3,64,256]{3,2,1,0:T(8,128)S(1)}, u32[]{:S(2)}, u32[]{:S(2)}) collective-permute-start(f32[2,3,64,256]{3,2,1,0:T(8,128)S(1)} %get-tuple-element.33), channel_id=1, source_target_pairs={{0,2},{1,3},{2,0},{3,1},{4,6},{5,7},{6,4},{7,5},{8,10},{9,11},{10,... | collective-permute-start | bytes 1179656 | tf_op jit(solution)/shard_map/ppermute | solution.py:381
  2.5 20.4 %collective-permute-start.3 = (f32[2,3,64,256]{3,2,1,0:T(8,128)S(1)}, f32[2,3,64,256]{3,2,1,0:T(8,128)S(1)}, u32[]{:S(2)}, u32[]{:S(2)}) collective-permute-start(f32[2,3,64,256]{3,2,1,0:T(8,128)S(1)} %get-tuple-element.35.v0_ref.va_ref), channel_id=1, source_target_pairs={{0,12},{1,13},{2,6},{3,7},{4,0},{5,1},{6,10},{7,11},{8,4},{9,5},{1... | collective-permute-start | bytes 1179656 | tf_op jit(solution)/shard_map/ppermute | solution.py:381
  3.8 21.7 %collective-permute-start = (f32[2,3,64,256]{3,2,1,0:T(8,128)S(1)}, f32[2,3,64,256]{3,2,1,0:T(8,128)S(1)}, u32[]{:S(2)}, u32[]{:S(2)}) collective-permute-start(f32[2,3,64,256]{3,2,1,0:T(8,128)S(1)} %get-tuple-element.34), channel_id=1, source_target_pairs={{0,2},{1,3},{2,0},{3,1},{4,6},{5,7},{6,4},{7,5},{8,10},{9,11},{10,... | collective-permute-start | bytes 1179656 | tf_op jit(solution)/shard_map/ppermute | solution.py:381
  5.5 22.6 %collective-permute-start.8 = (f32[2,3,64,256]{3,2,1,0:T(8,128)S(1)}, f32[2,3,64,256]{3,2,1,0:T(8,128)S(1)}, u32[]{:S(2)}, u32[]{:S(2)}) collective-permute-start(f32[2,3,64,256]{3,2,1,0:T(8,128)S(1)} %get-tuple-element.32.v1_ref.va_ref), channel_id=1, source_target_pairs={{0,12},{1,13},{2,6},{3,7},{4,0},{5,1},{6,10},{7,11},{8,4},{9,5},{1... | collective-permute-start | bytes 1179656 | tf_op jit(solution)/shard_map/ppermute | solution.py:381
  6.9 16.0 %collective-permute-start.4 = (f32[108,128]{1,0:T(8,128)S(1)}, f32[108,128]{1,0:T(8,128)S(1)}, u32[]{:S(2)}, u32[]{:S(2)}) collective-permute-start(f32[108,128]{1,0:T(8,128)S(1)} %reshape.10.link_ref.link_a), channel_id=1, source_target_pairs={{0,2},{1,3},{2,0},{3,1},{4,6},{5,7},{6,4},{7,5},{8,10},{9,11},{10,... | collective-permute-start | bytes 165896 | tf_op jit(solution)/shard_map/ppermute | solution.py:381
  12.3 8.8 %collective-permute-start.5 = (f32[36,128]{1,0:T(8,128)S(1)}, f32[36,128]{1,0:T(8,128)S(1)}, u32[]{:S(2)}, u32[]{:S(2)}) collective-permute-start(f32[36,128]{1,0:T(8,128)S(1)} %reshape.11), channel_id=1, source_target_pairs={{0,12},{1,13},{2,6},{3,7},{4,0},{5,1},{6,10},{7,11},{8,4},{9,5},{1... | collective-permute-start | bytes 55304 | tf_op jit(solution)/shard_map/ppermute | solution.py:381
  21.1 4.4 %collective-permute-start.2 = (f32[2,3,16,256]{3,2,1,0:T(8,128)S(1)}, f32[2,3,16,256]{3,2,1,0:T(8,128)S(1)}, u32[]{:S(2)}, u32[]{:S(2)}) collective-permute-start(f32[2,3,16,256]{3,2,1,0:T(8,128)S(1)} %slice.12), channel_id=1, source_target_pairs={{0,1},{1,0},{2,3},{3,2},{4,5},{5,4},{6,7},{7,6},{8,9},{9,8},{10,11... | collective-permute-start | bytes 294920 | tf_op jit(solution)/shard_map/ppermute | solution.py:381
  27.5 3.4 %collective-permute-start.7 = (f32[256,256]{1,0:T(8,128)S(1)}, f32[256,256]{1,0:T(8,128)S(1)}, u32[]{:S(2)}, u32[]{:S(2)}) collective-permute-start(f32[256,256]{1,0:T(8,128)S(1)} %get-tuple-element.24), channel_id=1, source_target_pairs={{0,1},{1,0},{2,3},{3,2},{4,5},{5,4},{6,7},{7,6},{8,9},{9,8},{10,11... | collective-permute-start | bytes 786440 | tf_op jit(solution)/shard_map/ppermute | solution.py:381
  31.0 4.5 %collective-permute-start.10 = (f32[96,256]{1,0:T(8,128)S(1)}, f32[96,256]{1,0:T(8,128)S(1)}, u32[]{:S(2)}, u32[]{:S(2)}) collective-permute-start(f32[96,256]{1,0:T(8,128)S(1)} %get-tuple-element.29), channel_id=1, source_target_pairs={{0,4},{1,5},{2,6},{3,7},{4,8},{5,9},{6,10},{7,11},{8,12},{9,13},{1... | collective-permute-start | bytes 294920 | tf_op jit(solution)/shard_map/ppermute | solution.py:381
  32.3 8.9 %collective-permute-start.11 = (f32[96,256]{1,0:T(8,128)S(1)}, f32[96,256]{1,0:T(8,128)S(1)}, u32[]{:S(2)}, u32[]{:S(2)}) collective-permute-start(f32[96,256]{1,0:T(8,128)S(1)} %get-tuple-element.30), channel_id=1, source_target_pairs={{0,8},{1,9},{2,10},{3,11},{4,12},{5,13},{6,14},{7,15},{8,0},{9,1},... | collective-permute-start | bytes 294920 | tf_op jit(solution)/shard_map/ppermute | solution.py:381
  34.7 8.0 %collective-permute-start.12 = (f32[96,256]{1,0:T(8,128)S(1)}, f32[96,256]{1,0:T(8,128)S(1)}, u32[]{:S(2)}, u32[]{:S(2)}) collective-permute-start(f32[96,256]{1,0:T(8,128)S(1)} %get-tuple-element.31), channel_id=1, source_target_pairs={{0,12},{1,13},{2,14},{3,15},{4,0},{5,1},{6,2},{7,3},{8,4},{9,5},{1... | collective-permute-start | bytes 294920 | tf_op jit(solution)/shard_map/ppermute | solution.py:381
  42.8 6.3 %collective-permute-start.16 = (f32[96,256]{1,0:T(8,128)S(1)}, f32[96,256]{1,0:T(8,128)S(1)}, u32[]{:S(2)}, u32[]{:S(2)}) collective-permute-start(f32[96,256]{1,0:T(8,128)S(1)} %shard_map.83.refs_0_), channel_id=1, source_target_pairs={{0,2},{1,3},{2,0},{3,1},{4,6},{5,7},{6,4},{7,5},{8,10},{9,11},{10,... | collective-permute-start | bytes 294920 | tf_op jit(solution)/shard_map/ppermute | solution.py:381
  45.7 5.3 %collective-permute-start.14 = (f32[96,256]{1,0:T(8,128)S(1)}, f32[96,256]{1,0:T(8,128)S(1)}, u32[]{:S(2)}, u32[]{:S(2)}) collective-permute-start(f32[96,256]{1,0:T(8,128)S(1)} %shard_map.83.refs_0_), channel_id=1, source_target_pairs={{0,8},{1,9},{2,10},{3,11},{4,12},{5,13},{6,14},{7,15},{8,0},{9,1},... | collective-permute-start | bytes 294920 | tf_op jit(solution)/shard_map/ppermute | solution.py:381
  45.7 6.8 %collective-permute-start.15 = (f32[96,256]{1,0:T(8,128)S(1)}, f32[96,256]{1,0:T(8,128)S(1)}, u32[]{:S(2)}, u32[]{:S(2)}) collective-permute-start(f32[96,256]{1,0:T(8,128)S(1)} %shard_map.83.refs_0_), channel_id=1, source_target_pairs={{0,12},{1,13},{2,14},{3,15},{4,0},{5,1},{6,2},{7,3},{8,4},{9,5},{1... | collective-permute-start | bytes 294920 | tf_op jit(solution)/shard_map/ppermute | solution.py:381
  46.1 8.2 %collective-permute-start.13 = (f32[96,256]{1,0:T(8,128)S(1)}, f32[96,256]{1,0:T(8,128)S(1)}, u32[]{:S(2)}, u32[]{:S(2)}) collective-permute-start(f32[96,256]{1,0:T(8,128)S(1)} %shard_map.83.refs_0_), channel_id=1, source_target_pairs={{0,4},{1,5},{2,6},{3,7},{4,8},{5,9},{6,10},{7,11},{8,12},{9,13},{1... | collective-permute-start | bytes 294920 | tf_op jit(solution)/shard_map/ppermute | solution.py:381
  47.1 11.6 %collective-permute-start.20 = (f32[96,256]{1,0:T(8,128)S(1)}, f32[96,256]{1,0:T(8,128)S(1)}, u32[]{:S(2)}, u32[]{:S(2)}) collective-permute-start(f32[96,256]{1,0:T(8,128)S(1)} %shard_map.83.refs_0_), channel_id=1, source_target_pairs={{0,1},{1,0},{2,3},{3,2},{4,5},{5,4},{6,7},{7,6},{8,9},{9,8},{10,11... | collective-permute-start | bytes 294920 | tf_op jit(solution)/shard_map/ppermute | solution.py:381
  49.1 9.7 %collective-permute-start.17 = (f32[96,256]{1,0:T(8,128)S(1)}, f32[96,256]{1,0:T(8,128)S(1)}, u32[]{:S(2)}, u32[]{:S(2)}) collective-permute-start(f32[96,256]{1,0:T(8,128)S(1)} %collective-permute-done.16.refs_4_), channel_id=1, source_target_pairs={{0,4},{1,5},{2,6},{3,7},{4,8},{5,9},{6,10},{7,11},{8,12},{9,13},{1... | collective-permute-start | bytes 294920 | tf_op jit(solution)/shard_map/ppermute | solution.py:381
  51.0 8.3 %collective-permute-start.18 = (f32[96,256]{1,0:T(8,128)S(1)}, f32[96,256]{1,0:T(8,128)S(1)}, u32[]{:S(2)}, u32[]{:S(2)}) collective-permute-start(f32[96,256]{1,0:T(8,128)S(1)} %collective-permute-done.14.refs_2_), channel_id=1, source_target_pairs={{0,2},{1,3},{2,0},{3,1},{4,6},{5,7},{6,4},{7,5},{8,10},{9,11},{10,... | collective-permute-start | bytes 294920 | tf_op jit(solution)/shard_map/ppermute | solution.py:381
  52.5 6.9 %collective-permute-start.19 = (f32[96,256]{1,0:T(8,128)S(1)}, f32[96,256]{1,0:T(8,128)S(1)}, u32[]{:S(2)}, u32[]{:S(2)}) collective-permute-start(f32[96,256]{1,0:T(8,128)S(1)} %collective-permute-done.15.refs_3_), channel_id=1, source_target_pairs={{0,2},{1,3},{2,0},{3,1},{4,6},{5,7},{6,4},{7,5},{8,10},{9,11},{10,... | collective-permute-start | bytes 294920 | tf_op jit(solution)/shard_map/ppermute | solution.py:381
  54.3 8.6 %collective-permute-start.21 = (f32[96,256]{1,0:T(8,128)S(1)}, f32[96,256]{1,0:T(8,128)S(1)}, u32[]{:S(2)}, u32[]{:S(2)}) collective-permute-start(f32[96,256]{1,0:T(8,128)S(1)} %collective-permute-done.13.refs_1_), channel_id=1, source_target_pairs={{0,1},{1,0},{2,3},{3,2},{4,5},{5,4},{6,7},{7,6},{8,9},{9,8},{10,11... | collective-permute-start | bytes 294920 | tf_op jit(solution)/shard_map/ppermute | solution.py:381
  58.8 4.1 %collective-permute-start.22 = (f32[96,256]{1,0:T(8,128)S(1)}, f32[96,256]{1,0:T(8,128)S(1)}, u32[]{:S(2)}, u32[]{:S(2)}) collective-permute-start(f32[96,256]{1,0:T(8,128)S(1)} %collective-permute-done.14.refs_2_), channel_id=1, source_target_pairs={{0,1},{1,0},{2,3},{3,2},{4,5},{5,4},{6,7},{7,6},{8,9},{9,8},{10,11... | collective-permute-start | bytes 294920 | tf_op jit(solution)/shard_map/ppermute | solution.py:381
  58.8 5.4 %collective-permute-start.23 = (f32[96,256]{1,0:T(8,128)S(1)}, f32[96,256]{1,0:T(8,128)S(1)}, u32[]{:S(2)}, u32[]{:S(2)}) collective-permute-start(f32[96,256]{1,0:T(8,128)S(1)} %collective-permute-done.15.refs_3_), channel_id=1, source_target_pairs={{0,1},{1,0},{2,3},{3,2},{4,5},{5,4},{6,7},{7,6},{8,9},{9,8},{10,11... | collective-permute-start | bytes 294920 | tf_op jit(solution)/shard_map/ppermute | solution.py:381
  59.3 4.9 %collective-permute-start.24 = (f32[96,256]{1,0:T(8,128)S(1)}, f32[96,256]{1,0:T(8,128)S(1)}, u32[]{:S(2)}, u32[]{:S(2)}) collective-permute-start(f32[96,256]{1,0:T(8,128)S(1)} %collective-permute-done.16.refs_4_), channel_id=1, source_target_pairs={{0,1},{1,0},{2,3},{3,2},{4,5},{5,4},{6,7},{7,6},{8,9},{9,8},{10,11... | collective-permute-start | bytes 294920 | tf_op jit(solution)/shard_map/ppermute | solution.py:381
  59.4 4.9 %collective-permute-start.25 = (f32[96,256]{1,0:T(8,128)S(1)}, f32[96,256]{1,0:T(8,128)S(1)}, u32[]{:S(2)}, u32[]{:S(2)}) collective-permute-start(f32[96,256]{1,0:T(8,128)S(1)} %collective-permute-done.17.refs_5_), channel_id=1, source_target_pairs={{0,1},{1,0},{2,3},{3,2},{4,5},{5,4},{6,7},{7,6},{8,9},{9,8},{10,11... | collective-permute-start | bytes 294920 | tf_op jit(solution)/shard_map/ppermute | solution.py:381
  (8 other events, 117.0 us)
